TPU v7x, 256 devices: a whole 4x4x8 slice. The times are simulated.
256 devices in a mesh: sec: 32 (over x, z), op: 8 (over y, core).
Axes of the slice: x: 4, y: 4, z: 8, core: 2. Of those that a mesh axis runs over, the one named last changes fastest.
Arguments:
- state_start: bfloat16 [64, 256, 256], P('sec'), may hold values from -60 to 60
- left_ops: bfloat16 [64, 64, 256, 256], P('op', 'sec'), may hold values from -0.375 to 0.375
- right_ops: bfloat16 [64, 64, 256, 256], P('op', 'sec'), may hold values from -0.046875 to 0.046875
- shift: float32 [64], P('sec'), may hold values from 0.2 to 2.2
- partner: int32 [64, 64], P('op', 'sec'), may hold values from 0 to 5
- kept: int32 [64], P('sec'), may hold values from 128 to 256
Outputs:
- state_final: bfloat16 [64, 256, 256], P('sec')
- new_ops: bfloat16 [64, 64, 256, 256], P('op', 'sec')
Inputs may be any that keep to these rules, and one draw needn't show every extreme that they name: `partner`: position in the window of 6 sector blocks.
All inputs are finite; a program needn't handle non-finite values.
Results may differ from a plain program's by a relative error of at most 0.015.
Values may be sent and summed in bfloat16 or wider, within the bound.
A program may use at most 64 MiB of HBM per device.

v0:
```python
import jax
import jax.numpy as jnp
from jax import lax
from jax.sharding import PartitionSpec as P

ITERS = 4


step_size = 0.5


def padded(cells, sides, width):
    for axis, dim in sides:
        count = lax.axis_size(axis)
        head = lax.slice_in_dim(cells, 0, width, axis=dim)
        tail = lax.slice_in_dim(cells, cells.shape[dim] - width, cells.shape[dim], axis=dim)
        cells = jnp.concatenate(
            [
                lax.ppermute(tail, axis, [(i, (i + 1) % count) for i in range(count)]),
                cells,
                lax.ppermute(head, axis, [((i + 1) % count, i) for i in range(count)]),
            ],
            axis=dim,
        )
    return cells


def shifted(block, axis, distance):
    devices = range(lax.axis_size(axis))
    route = [((i - distance) % len(devices), i) for i in devices]
    return lax.ppermute(block, axis, route)


def per_device(state_start, left_ops, right_ops, shift, partner, kept):
    sector_local = state_start.shape[0]
    width = state_start.shape[1]
    share_rows = width // lax.axis_size("op")
    share_start = lax.axis_index("op") * share_rows
    count = float(sector_local * lax.axis_size("sec") * width * width)
    shift_col = shift[:, None, None]
    state = state_start
    for iteration in range(ITERS):
        window = padded(state, (("sec", 0),), sector_local)
        sources = window[partner]
        halfway = jnp.einsum(
            "tbij,tbjk->tbik", left_ops, sources, preferred_element_type=jnp.float32
        ).astype(jnp.bfloat16)
        partial_sigma = jnp.einsum(
            "tbij,tbjk->bik", halfway, right_ops, preferred_element_type=jnp.float32
        )
        state_wide = state.astype(jnp.float32)
        state_part = lax.dynamic_slice_in_dim(state_wide, share_start, share_rows, 1)
        sigma = lax.psum(partial_sigma, "op") + shift_col * state_wide
        sigma_part = lax.dynamic_slice_in_dim(sigma, share_start, share_rows, 1)
        energy_sum, norm_sum, square_sum = lax.psum(
            (
                jnp.sum(state_part * sigma_part),
                jnp.sum(state_part * state_part),
                jnp.sum(sigma_part * sigma_part),
            ),
            ("sec", "op"),
        )
        ratio = energy_sum / norm_sum
        updated_part = state_part - step_size * (sigma_part - ratio * state_part)
        new_norm = lax.psum(jnp.sum(updated_part * updated_part), ("sec", "op"))
        factor = jnp.sqrt(count / new_norm)
        updated = state_wide - step_size * (sigma - ratio * state_wide)
        state = (updated * factor).astype(jnp.bfloat16)
    columns = jnp.arange(width, dtype=jnp.int32)
    keep_mask = (columns[None, :] < kept[:, None]).astype(jnp.bfloat16)
    kept_block = state * keep_mask[:, None, :]
    out_scale = 1.0 / float(width) ** 0.5
    projected = jnp.einsum(
        "tbij,bjk->tbik", left_ops, kept_block, preferred_element_type=jnp.float32
    ).astype(jnp.bfloat16)
    renormed = (
        jnp.einsum("bji,tbjk->tbik", kept_block, projected, preferred_element_type=jnp.float32)
        * out_scale
    ).astype(jnp.bfloat16)
    new_ops = shifted(renormed, "sec", 1)
    return (state, new_ops)


def solution(mesh):
    in_specs = (
        P("sec", None, None),
        P("op", "sec", None, None),
        P("op", "sec", None, None),
        P("sec"),
        P("op", "sec"),
        P("sec"),
    )
    out_specs = (P("sec", None, None), P("op", "sec", None, None))
    return jax.shard_map(
        per_device, mesh=mesh, in_specs=in_specs, out_specs=out_specs, check_vma=False
    )
```

profile of v0, /device:TPU:1, one launch (start us, length us, event | category | flops | bytes accessed | tf_op | source)
XLA Modules:
  0.0 1021.9 jit_solution(1389676207874550599)
XLA Ops:
  9.8 6.2 collective-permute-start.1
  16.9 5.3 collective-permute-done
  25.2 4.3 fusion.47
  30.5 62.1 %all-reduce.9.cloned.1.call-done = f32[2,256,256]{2,1,0:T(8,128)} async-done(((f32[2,256,256]{2,1,0:T(8,128)}), f32[2,256,256]{2,1,0:T(8,128)}) %all-reduce.9.cloned.1.call-update) | async-done | bytes 524304 | tf_op jit(solution)/shard_map/psum | solution.py:53
  95.3 78.5 %all-reduce.3 = (f32[]{:T(128)}, f32[]{:T(128)}) all-reduce(f32[]{:T(128)} %get-tuple-element.13, f32[]{:T(128)} %get-tuple-element.12), channel_id=1, replica_groups=mesh['sec'=32,'op'=8] {'sec','op'}, use_global_device_ids=true, to_apply=%region_2.0 | all-reduce | flops 2 | bytes 16 | tf_op jit(solution)/shard_map/psum | solution.py:55
  176.5 73.4 %psum.115 = f32[]{:T(128)} all-reduce(f32[]{:T(128)} %multiply_reduce_fusion.9), channel_id=1, replica_groups=mesh['sec'=32,'op'=8] {'sec','op'}, use_global_device_ids=true, to_apply=%region_6.0 | all-reduce | flops 1 | bytes 8 | tf_op jit(solution)/shard_map/psum | solution.py:65
  253.7 5.0 collective-permute-done.3
  258.8 5.2 collective-permute-done.2
  266.0 4.3 fusion.54
  270.4 57.5 %all-reduce.11.cloned.1.call-done = f32[2,256,256]{2,1,0:T(8,128)} async-done(((f32[2,256,256]{2,1,0:T(8,128)}), f32[2,256,256]{2,1,0:T(8,128)}) %all-reduce.11.cloned.1.call-update) | async-done | bytes 524304 | tf_op jit(solution)/shard_map/psum | solution.py:53
  330.6 78.5 %all-reduce.2 = (f32[]{:T(128)}, f32[]{:T(128)}) all-reduce(f32[]{:T(128)} %get-tuple-element.11, f32[]{:T(128)} %get-tuple-element.10), channel_id=1, replica_groups=mesh['sec'=32,'op'=8] {'sec','op'}, use_global_device_ids=true, to_apply=%region_9.0 | all-reduce | flops 2 | bytes 16 | tf_op jit(solution)/shard_map/psum | solution.py:55
  411.9 73.4 %psum.119 = f32[]{:T(128)} all-reduce(f32[]{:T(128)} %multiply_reduce_fusion.6), channel_id=1, replica_groups=mesh['sec'=32,'op'=8] {'sec','op'}, use_global_device_ids=true, to_apply=%region_13.0 | all-reduce | flops 1 | bytes 8 | tf_op jit(solution)/shard_map/psum | solution.py:65
  489.1 5.0 collective-permute-done.5
  494.1 5.2 collective-permute-done.4
  505.8 57.6 %all-reduce.13.cloned.1.call-done = f32[2,256,256]{2,1,0:T(8,128)} async-done(((f32[2,256,256]{2,1,0:T(8,128)}), f32[2,256,256]{2,1,0:T(8,128)}) %all-reduce.13.cloned.1.call-update) | async-done | bytes 524304 | tf_op jit(solution)/shard_map/psum | solution.py:53
  566.0 78.5 %all-reduce.1 = (f32[]{:T(128)}, f32[]{:T(128)}) all-reduce(f32[]{:T(128)} %get-tuple-element.9, f32[]{:T(128)} %get-tuple-element.8), channel_id=1, replica_groups=mesh['sec'=32,'op'=8] {'sec','op'}, use_global_device_ids=true, to_apply=%region_16.0 | all-reduce | flops 2 | bytes 16 | tf_op jit(solution)/shard_map/psum | solution.py:55
  647.3 73.4 %psum.123 = f32[]{:T(128)} all-reduce(f32[]{:T(128)} %multiply_reduce_fusion.3), channel_id=1, replica_groups=mesh['sec'=32,'op'=8] {'sec','op'}, use_global_device_ids=true, to_apply=%region_20.0 | all-reduce | flops 1 | bytes 8 | tf_op jit(solution)/shard_map/psum | solution.py:65
  724.5 5.0 collective-permute-done.7
  729.5 5.2 collective-permute-done.6
  741.1 57.6 %all-reduce.15.cloned.1.call-done = f32[2,256,256]{2,1,0:T(8,128)} async-done(((f32[2,256,256]{2,1,0:T(8,128)}), f32[2,256,256]{2,1,0:T(8,128)}) %all-reduce.15.cloned.1.call-update) | async-done | bytes 524304 | tf_op jit(solution)/shard_map/psum | solution.py:53
  801.4 78.5 %all-reduce = (f32[]{:T(128)}, f32[]{:T(128)}) all-reduce(f32[]{:T(128)} %get-tuple-element.7, f32[]{:T(128)} %get-tuple-element.6), channel_id=1, replica_groups=mesh['sec'=32,'op'=8] {'sec','op'}, use_global_device_ids=true, to_apply=%region_23.0 | all-reduce | flops 2 | bytes 16 | tf_op jit(solution)/shard_map/psum | solution.py:55
  882.7 73.4 %psum.127 = f32[]{:T(128)} all-reduce(f32[]{:T(128)} %multiply_reduce_fusion), channel_id=1, replica_groups=mesh['sec'=32,'op'=8] {'sec','op'}, use_global_device_ids=true, to_apply=%region_27.0 | all-reduce | flops 1 | bytes 8 | tf_op jit(solution)/shard_map/psum | solution.py:65
  957.0 4.3 fusion.40
  962.3 49.2 %collective-permute-done.8 = bf16[8,2,256,256]{2,3,0,1:T(8,128)(2,1)} collective-permute-done((bf16[8,2,256,256]{2,3,0,1:T(8,128)(2,1)}, bf16[8,2,256,256]{2,3,0,1:T(8,128)(2,1)}, u32[]{:S(2)}, u32[]{:S(2)}) %collective-permute-start.8) | collective-permute-done | bytes 2097184 | tf_op jit(solution)/shard_map/ppermute | solution.py:31
  (60 shorter events, 53.2 us)
Async XLA Ops:
  7.2 18.0 %copy-start = (bf16[8,2,256,256]{3,2,1,0:T(8,128)(2,1)S(1)}, bf16[8,2,256,256]{3,2,1,0:T(8,128)(2,1)}, u32[]{:S(2)}) copy-start(bf16[8,2,256,256]{3,2,1,0:T(8,128)(2,1)} %param.8) | copy-start | bytes 6291460
  7.2 85.4 %all-reduce.9.cloned.1.call-start = ((), (), s32[]{:S(2)}) async-start(), calls=%async_computation | async-start | bytes 1048576 | tf_op jit(solution)/shard_map/psum | solution.py:53
  7.2 14.9 %collective-permute-start = (bf16[2,256,256]{2,1,0:T(8,128)(2,1)}, bf16[2,256,256]{2,1,0:T(8,128)(2,1)S(1)}, u32[]{:S(2)}, u32[]{:S(2)}) collective-permute-start(bf16[2,256,256]{2,1,0:T(8,128)(2,1)} %param.6), channel_id=1, source_target_pairs={{0,8},{8,16},{16,24},{24,32},{32,40},{40,48},{48,56},{56,64},{64,7... | collective-permute-start | bytes 786440 | tf_op jit(solution)/shard_map/ppermute | solution.py:19
  9.8 12.4 %collective-permute-start.1 = (bf16[2,256,256]{2,1,0:T(8,128)(2,1)}, bf16[2,256,256]{2,1,0:T(8,128)(2,1)S(1)}, u32[]{:S(2)}, u32[]{:S(2)}) collective-permute-start(bf16[2,256,256]{2,1,0:T(8,128)(2,1)} %param.6), channel_id=1, source_target_pairs={{8,0},{16,8},{24,16},{32,24},{40,32},{48,40},{56,48},{64,56},{72,6... | collective-permute-start | bytes 786440 | tf_op jit(solution)/shard_map/ppermute | solution.py:21
  25.2 4.4 copy-start.1
  25.2 67.4 %copy-start.3 = (f32[2]{0:T(128)S(1)}, f32[2]{0:T(128)}, u32[]{:S(2)}) copy-start(f32[2]{0:T(128)} %param.9) | copy-start | bytes 28
  29.6 298.4 %all-reduce.11.cloned.1.call-start = ((), (), s32[]{:S(2)}) async-start(), calls=%async_computation.1 | async-start | bytes 1048576 | tf_op jit(solution)/shard_map/psum | solution.py:53
  251.6 7.2 collective-permute-start.3
  253.7 10.2 collective-permute-start.2
  270.3 293.0 %all-reduce.13.cloned.1.call-start = ((), (), s32[]{:S(2)}) async-start(), calls=%async_computation.2 | async-start | bytes 1048576 | tf_op jit(solution)/shard_map/psum | solution.py:53
  486.9 7.2 collective-permute-start.5
  489.1 10.2 collective-permute-start.4
  505.7 293.0 %all-reduce.15.cloned.1.call-start = ((), (), s32[]{:S(2)}) async-start(), calls=%async_computation.3 | async-start | bytes 1048576 | tf_op jit(solution)/shard_map/psum | solution.py:53
  722.3 7.2 collective-permute-start.7
  724.5 10.2 collective-permute-start.6
  741.1 141.5 %copy-start.4 = (s32[2]{0:T(128)S(1)}, s32[2]{0:T(128)}, u32[]{:S(2)}) copy-start(s32[2]{0:T(128)} %param.11) | copy-start | bytes 28
  957.0 4.3 copy-start.2
  961.3 50.2 %collective-permute-start.8 = (bf16[8,2,256,256]{2,3,0,1:T(8,128)(2,1)}, bf16[8,2,256,256]{2,3,0,1:T(8,128)(2,1)}, u32[]{:S(2)}, u32[]{:S(2)}) collective-permute-start(bf16[8,2,256,256]{2,3,0,1:T(8,128)(2,1)} %fusion.40), channel_id=1, source_target_pairs={{248,0},{0,8},{8,16},{16,24},{24,32},{32,40},{40,48},{48,56},{56,6... | collective-permute-start | bytes 6291464 | tf_op jit(solution)/shard_map/ppermute | solution.py:31
Sparse Core Ops, SparseCore 0:
  29.7 62.8 all-reduce.8
  270.5 57.4 all-reduce.10
  505.8 57.4 all-reduce.12
  741.2 57.4 all-reduce.14
where the time goes:
time: 1020 us
  blocking collectives  608 us (60%)
  waiting for transfers between devices  320 us (31%)
  other arithmetic  22.3 us (2%)
  between operations  22.1 us (2%)
  matrix products  21.6 us (2%)
  starting transfers between devices  16.4 us (2%)
  local copies, waits for them, and re-layouts  12.1 us (1%)
    psum x4, blocking collectives, per_device(): lax.psum((jnp.sum(state_part * sigma_part), jnp.sum(state_part * state_pa...  314 us
    psum x4, blocking collectives, per_device(): new_norm = lax.psum(jnp.sum(updated_part * updated_part), ('sec', 'op'))  294 us
    psum x4, waiting for transfers between devices, per_device(): sigma = lax.psum(partial_sigma, 'op') + shift_col * state_wide  235 us
    ppermute x1, waiting for transfers between devices, shifted(): return lax.ppermute(block, axis, route)  49.2 us
    ppermute x4, waiting for transfers between devices, padded(): lax.ppermute(tail, axis, [(i, (i + 1) % count) for i in range(count)])  20.8 us
  transfers between devices with their start and end apart: 13, of which 12 were waited for; matrix products, arithmetic and copies ran while one was open for 0% of the time, Pallas kernels for 0%

commit v1 on v0

--- a/solution.py
+++ b/solution.py
@@ -34,10 +34,9 @@
 def per_device(state_start, left_ops, right_ops, shift, partner, kept):
     sector_local = state_start.shape[0]
     width = state_start.shape[1]
-    share_rows = width // lax.axis_size("op")
-    share_start = lax.axis_index("op") * share_rows
     count = float(sector_local * lax.axis_size("sec") * width * width)
     shift_col = shift[:, None, None]
+    first_op = lax.axis_index("op") == 0
     state = state_start
     for iteration in range(ITERS):
         window = padded(state, (("sec", 0),), sector_local)
@@ -49,22 +48,22 @@
             "tbij,tbjk->bik", halfway, right_ops, preferred_element_type=jnp.float32
         )
         state_wide = state.astype(jnp.float32)
-        state_part = lax.dynamic_slice_in_dim(state_wide, share_start, share_rows, 1)
+        own_square = jnp.sum(state_wide * state_wide, axis=(1, 2))
+        energy_part = jnp.sum(state_wide * partial_sigma) + jnp.where(
+            first_op, jnp.sum(shift * own_square), 0.0
+        )
+        norm_part = jnp.where(first_op, jnp.sum(own_square), 0.0)
+        energy_sum, norm_sum = lax.psum((energy_part, norm_part), ("sec", "op"))
         sigma = lax.psum(partial_sigma, "op") + shift_col * state_wide
-        sigma_part = lax.dynamic_slice_in_dim(sigma, share_start, share_rows, 1)
-        energy_sum, norm_sum, square_sum = lax.psum(
-            (
-                jnp.sum(state_part * sigma_part),
-                jnp.sum(state_part * state_part),
-                jnp.sum(sigma_part * sigma_part),
-            ),
-            ("sec", "op"),
-        )
         ratio = energy_sum / norm_sum
-        updated_part = state_part - step_size * (sigma_part - ratio * state_part)
-        new_norm = lax.psum(jnp.sum(updated_part * updated_part), ("sec", "op"))
-        factor = jnp.sqrt(count / new_norm)
         updated = state_wide - step_size * (sigma - ratio * state_wide)
+        if iteration < ITERS - 1:
+            factor = jnp.sqrt(count / norm_sum)
+        else:
+            new_norm = lax.psum(
+                jnp.where(first_op, jnp.sum(updated * updated), 0.0), ("sec", "op")
+            )
+            factor = jnp.sqrt(count / new_norm)
         state = (updated * factor).astype(jnp.bfloat16)
     columns = jnp.arange(width, dtype=jnp.int32)
     keep_mask = (columns[None, :] < kept[:, None]).astype(jnp.bfloat16)

time: 1020 us -> 553 us (0.54)
  waiting for transfers between devices: 320 us -> 83.8 us
  blocking collectives: 608 us -> 372 us
  other arithmetic: 22.3 us -> 11.3 us
    psum x8 -> x5, blocking collectives: 608 us -> 372 us  [the longest x4 298 us: per_device(): energy_sum, norm_sum = lax.psum((energy_part, norm_part), ('sec', 'op'))]
    psum x4, waiting for transfers between devices: 235 us -> 0.08 us  [per_device(): sigma = lax.psum(partial_sigma, 'op') + shift_col * state_wide]
  transfers between devices with their start and end apart: 13 -> 13, of which waited for: 12 -> 8; matrix products, arithmetic and copies ran while one was open for 0% -> 1% of each run, Pallas kernels for 0% -> 0%
where the time goes in v1:
time: 553 us; the launch traced here: 552 us
  blocking collectives  372 us (67%)
  waiting for transfers between devices  83.8 us (15%)
  between operations  30.8 us (6%)
  matrix products  24.3 us (4%)
  starting transfers between devices  17.6 us (3%)
  local copies, waits for them, and re-layouts  12.1 us (2%)
  other arithmetic  11.3 us (2%)
    psum x4, blocking collectives, per_device(): energy_sum, norm_sum = lax.psum((energy_part, norm_part), ('sec', 'op'))  298 us
    psum x1, blocking collectives, per_device(): lax.psum(jnp.where(first_op, jnp.sum(updated * updated), 0.0), ('sec', 'o...  74.2 us
    ppermute x1, waiting for transfers between devices, shifted(): return lax.ppermute(block, axis, route)  49.2 us
    dot_general x4, matrix products, per_device(): jnp.einsum('tbij,tbjk->bik', halfway, right_ops, preferred_element_type=j...  19.9 us
    ppermute x4, waiting for transfers between devices, padded(): lax.ppermute(tail, axis, [(i, (i + 1) % count) for i in range(count)])  18.9 us
    ppermute x4, waiting for transfers between devices, padded(): lax.ppermute(head, axis, [((i + 1) % count, i) for i in range(count)])  15.5 us
    ppermute x4, starting transfers between devices, padded(): lax.ppermute(head, axis, [((i + 1) % count, i) for i in range(count)])  12.5 us
  transfers between devices with their start and end apart: 13, of which 8 were waited for; matrix products, arithmetic and copies ran while one was open for 1% of the time, Pallas kernels for 0%

profile of v1, /device:TPU:1, one launch (start us, length us, event | category | flops | bytes accessed | tf_op | source)
XLA Modules:
  0.0 551.6 jit_solution(2810122551099413732)
XLA Ops:
  7.2 2.5 collective-permute-start
  9.8 6.2 %collective-permute-start.1 = (bf16[2,256,256]{2,1,0:T(8,128)(2,1)}, bf16[2,256,256]{2,1,0:T(8,128)(2,1)S(1)}, u32[]{:S(2)}, u32[]{:S(2)}) collective-permute-start(bf16[2,256,256]{2,1,0:T(8,128)(2,1)} %param.6), channel_id=1, source_target_pairs={{8,0},{16,8},{24,16},{32,24},{40,32},{48,40},{56,48},{64,56},{72,6... | collective-permute-start | bytes 786440 | tf_op jit(solution)/shard_map/ppermute | solution.py:21
  16.9 5.3 collective-permute-done
  23.2 2.0 gather_fusion
  25.2 5.0 fusion.86
  32.9 78.0 %all-reduce.3 = (f32[]{:T(128)}, f32[]{:T(128)}) all-reduce(f32[]{:T(128)S(6)} %select_n.36, f32[]{:T(128)S(6)} %add.58), channel_id=1, replica_groups=mesh['sec'=32,'op'=8] {'sec','op'}, use_global_device_ids=true, to_apply=%region_6.7 | all-reduce | flops 2 | bytes 16 | tf_op jit(solution)/shard_map/psum | solution.py:56
  115.7 5.4 collective-permute-done.3
  121.1 3.4 collective-permute-done.2
  126.6 5.0 fusion.88
  134.2 73.8 %all-reduce.2 = (f32[]{:T(128)}, f32[]{:T(128)}) all-reduce(f32[]{:T(128)S(6)} %select_n.38, f32[]{:T(128)S(6)} %add.60), channel_id=1, replica_groups=mesh['sec'=32,'op'=8] {'sec','op'}, use_global_device_ids=true, to_apply=%region_13.14 | all-reduce | flops 2 | bytes 16 | tf_op jit(solution)/shard_map/psum | solution.py:56
  211.3 2.7 collective-permute-start.5
  214.0 5.2 collective-permute-done.5
  219.2 5.0 collective-permute-done.4
  226.3 5.0 fusion.90
  233.9 73.1 %all-reduce.1 = (f32[]{:T(128)}, f32[]{:T(128)}) all-reduce(f32[]{:T(128)S(6)} %select_n.40, f32[]{:T(128)S(6)} %add.62), channel_id=1, replica_groups=mesh['sec'=32,'op'=8] {'sec','op'}, use_global_device_ids=true, to_apply=%region_20.21 | all-reduce | flops 2 | bytes 16 | tf_op jit(solution)/shard_map/psum | solution.py:56
  310.4 3.5 collective-permute-start.7
  313.9 5.0 collective-permute-done.7
  318.8 5.2 collective-permute-done.6
  326.1 5.0 fusion.91
  333.7 72.9 %all-reduce = (f32[]{:T(128)}, f32[]{:T(128)}) all-reduce(f32[]{:T(128)S(6)} %add.64, f32[]{:T(128)S(6)} %select_n.42), channel_id=1, replica_groups=mesh['sec'=32,'op'=8] {'sec','op'}, use_global_device_ids=true, to_apply=%region_25.26 | all-reduce | flops 2 | bytes 16 | tf_op jit(solution)/shard_map/psum | solution.py:56
  410.6 74.2 %psum.103 = f32[]{:T(128)} all-reduce(f32[]{:T(128)S(6)} %select_n.43), channel_id=1, replica_groups=mesh['sec'=32,'op'=8] {'sec','op'}, use_global_device_ids=true, to_apply=%region_29.30 | all-reduce | flops 1 | bytes 8 | tf_op jit(solution)/shard_map/psum | solution.py:63
  486.7 4.3 fusion.40
  492.0 49.2 %collective-permute-done.8 = bf16[8,2,256,256]{2,3,0,1:T(8,128)(2,1)} collective-permute-done((bf16[8,2,256,256]{2,3,0,1:T(8,128)(2,1)}, bf16[8,2,256,256]{2,3,0,1:T(8,128)(2,1)}, u32[]{:S(2)}, u32[]{:S(2)}) %collective-permute-start.8) | collective-permute-done | bytes 2097184 | tf_op jit(solution)/shard_map/ppermute | solution.py:31
  541.2 3.9 copy.19
  (49 shorter events, 20.3 us)
Async XLA Ops:
  7.2 18.0 %copy-start = (bf16[8,2,256,256]{3,2,1,0:T(8,128)(2,1)S(1)}, bf16[8,2,256,256]{3,2,1,0:T(8,128)(2,1)}, u32[]{:S(2)}) copy-start(bf16[8,2,256,256]{3,2,1,0:T(8,128)(2,1)} %param.8) | copy-start | bytes 6291460
  7.2 105.7 %all-reduce.9.cloned.1.call-start = ((), (), s32[]{:S(2)}) async-start(), calls=%async_computation | async-start | bytes 1048576 | tf_op jit(solution)/shard_map/psum | solution.py:57
  7.2 14.9 %collective-permute-start = (bf16[2,256,256]{2,1,0:T(8,128)(2,1)}, bf16[2,256,256]{2,1,0:T(8,128)(2,1)S(1)}, u32[]{:S(2)}, u32[]{:S(2)}) collective-permute-start(bf16[2,256,256]{2,1,0:T(8,128)(2,1)} %param.6), channel_id=1, source_target_pairs={{0,8},{8,16},{16,24},{24,32},{32,40},{40,48},{48,56},{56,64},{64,7... | collective-permute-start | bytes 786440 | tf_op jit(solution)/shard_map/ppermute | solution.py:19
  9.8 12.4 %collective-permute-start.1 = (bf16[2,256,256]{2,1,0:T(8,128)(2,1)}, bf16[2,256,256]{2,1,0:T(8,128)(2,1)S(1)}, u32[]{:S(2)}, u32[]{:S(2)}) collective-permute-start(bf16[2,256,256]{2,1,0:T(8,128)(2,1)} %param.6), channel_id=1, source_target_pairs={{8,0},{16,8},{24,16},{32,24},{40,32},{48,40},{56,48},{64,56},{72,6... | collective-permute-start | bytes 786440 | tf_op jit(solution)/shard_map/ppermute | solution.py:21
  23.2 2.0 copy-start.1
  25.2 5.8 %copy-start.3 = (f32[2]{0:T(128)S(1)}, f32[2]{0:T(128)}, u32[]{:S(2)}) copy-start(f32[2]{0:T(128)} %param.9) | copy-start | bytes 28
  30.2 179.9 %all-reduce.11.cloned.1.call-start = ((), (), s32[]{:S(2)}) async-start(), calls=%async_computation.1 | async-start | bytes 1048576 | tf_op jit(solution)/shard_map/psum | solution.py:57
  114.2 6.9 %collective-permute-start.3 = (bf16[2,256,256]{2,1,0:T(8,128)(2,1)S(1)}, bf16[2,256,256]{2,1,0:T(8,128)(2,1)S(1)}, u32[]{:S(2)}, u32[]{:S(2)}) collective-permute-start(bf16[2,256,256]{2,1,0:T(8,128)(2,1)S(1)} %fusion.98), channel_id=1, source_target_pairs={{8,0},{16,8},{24,16},{32,24},{40,32},{48,40},{56,48},{64,56},{72,6... | collective-permute-start | bytes 786440 | tf_op jit(solution)/shard_map/ppermute | solution.py:21
  114.3 10.2 %collective-permute-start.2 = (bf16[2,256,256]{2,1,0:T(8,128)(2,1)S(1)}, bf16[2,256,256]{2,1,0:T(8,128)(2,1)S(1)}, u32[]{:S(2)}, u32[]{:S(2)}) collective-permute-start(bf16[2,256,256]{2,1,0:T(8,128)(2,1)S(1)} %fusion.98), channel_id=1, source_target_pairs={{0,8},{8,16},{16,24},{24,32},{32,40},{40,48},{48,56},{56,64},{64,7... | collective-permute-start | bytes 786440 | tf_op jit(solution)/shard_map/ppermute | solution.py:19
  131.6 177.5 %all-reduce.13.cloned.1.call-start = ((), (), s32[]{:S(2)}) async-start(), calls=%async_computation.2 | async-start | bytes 1048576 | tf_op jit(solution)/shard_map/psum | solution.py:57
  211.3 7.9 %collective-permute-start.5 = (bf16[2,256,256]{2,1,0:T(8,128)(2,1)S(1)}, bf16[2,256,256]{2,1,0:T(8,128)(2,1)S(1)}, u32[]{:S(2)}, u32[]{:S(2)}) collective-permute-start(bf16[2,256,256]{2,1,0:T(8,128)(2,1)S(1)} %fusion.104), channel_id=1, source_target_pairs={{8,0},{16,8},{24,16},{32,24},{40,32},{48,40},{56,48},{64,56},{72,6... | collective-permute-start | bytes 786440 | tf_op jit(solution)/shard_map/ppermute | solution.py:21
  214.0 10.2 %collective-permute-start.4 = (bf16[2,256,256]{2,1,0:T(8,128)(2,1)S(1)}, bf16[2,256,256]{2,1,0:T(8,128)(2,1)S(1)}, u32[]{:S(2)}, u32[]{:S(2)}) collective-permute-start(bf16[2,256,256]{2,1,0:T(8,128)(2,1)S(1)} %fusion.104), channel_id=1, source_target_pairs={{0,8},{8,16},{16,24},{24,32},{32,40},{40,48},{48,56},{56,64},{64,7... | collective-permute-start | bytes 786440 | tf_op jit(solution)/shard_map/ppermute | solution.py:19
  231.3 176.7 %all-reduce.15.cloned.1.call-start = ((), (), s32[]{:S(2)}) async-start(), calls=%async_computation.3 | async-start | bytes 1048576 | tf_op jit(solution)/shard_map/psum | solution.py:57
  310.4 8.5 %collective-permute-start.7 = (bf16[2,256,256]{2,1,0:T(8,128)(2,1)S(1)}, bf16[2,256,256]{2,1,0:T(8,128)(2,1)S(1)}, u32[]{:S(2)}, u32[]{:S(2)}) collective-permute-start(bf16[2,256,256]{2,1,0:T(8,128)(2,1)S(1)} %fusion.110), channel_id=1, source_target_pairs={{8,0},{16,8},{24,16},{32,24},{40,32},{48,40},{56,48},{64,56},{72,6... | collective-permute-start | bytes 786440 | tf_op jit(solution)/shard_map/ppermute | solution.py:21
  313.9 10.2 %collective-permute-start.6 = (bf16[2,256,256]{2,1,0:T(8,128)(2,1)S(1)}, bf16[2,256,256]{2,1,0:T(8,128)(2,1)S(1)}, u32[]{:S(2)}, u32[]{:S(2)}) collective-permute-start(bf16[2,256,256]{2,1,0:T(8,128)(2,1)S(1)} %fusion.110), channel_id=1, source_target_pairs={{0,8},{8,16},{16,24},{24,32},{32,40},{40,48},{48,56},{56,64},{64,7... | collective-permute-start | bytes 786440 | tf_op jit(solution)/shard_map/ppermute | solution.py:19
  326.1 84.4 %copy-start.4 = (s32[2]{0:T(128)S(1)}, s32[2]{0:T(128)}, u32[]{:S(2)}) copy-start(s32[2]{0:T(128)} %param.11) | copy-start | bytes 28
  486.7 4.3 copy-start.2
  491.1 50.2 %collective-permute-start.8 = (bf16[8,2,256,256]{2,3,0,1:T(8,128)(2,1)}, bf16[8,2,256,256]{2,3,0,1:T(8,128)(2,1)}, u32[]{:S(2)}, u32[]{:S(2)}) collective-permute-start(bf16[8,2,256,256]{2,3,0,1:T(8,128)(2,1)} %fusion.40), channel_id=1, source_target_pairs={{248,0},{0,8},{8,16},{16,24},{24,32},{32,40},{40,48},{48,56},{56,6... | collective-permute-start | bytes 6291464 | tf_op jit(solution)/shard_map/ppermute | solution.py:31
Sparse Core Ops, SparseCore 0:
  30.3 62.8 all-reduce.8
  131.7 57.4 all-reduce.10
  231.4 56.8 all-reduce.12
  331.3 56.7 all-reduce.14

commit v2 on v1

--- a/solution.py
+++ b/solution.py
@@ -1,7 +1,13 @@
+import functools
+
 import jax
 import jax.numpy as jnp
 from jax import lax
+from jax.experimental import pallas as pl
+from jax.experimental.pallas import tpu as pltpu
 from jax.sharding import PartitionSpec as P
+
+MESH = pl.DeviceIdType.MESH
 
 ITERS = 4
 
@@ -25,6 +31,78 @@
     return cells
 
 
+def all_sum_kernel(n_sec, n_op, x_ref, o_ref, op_buf, sec_buf, mid, out_buf,
+                   send_a, recv_a, send_b, recv_b, local_sem):
+    me_sec = lax.axis_index("sec")
+    me_op = lax.axis_index("op")
+    barrier = pltpu.get_barrier_semaphore()
+    for d in range(1, n_op):
+        pl.semaphore_signal(barrier, 1, device_id=(me_sec, (me_op + d) % n_op),
+                            device_id_type=MESH)
+    for d in range(1, n_sec):
+        pl.semaphore_signal(barrier, 1, device_id=((me_sec + d) % n_sec, me_op),
+                            device_id_type=MESH)
+    pl.semaphore_wait(barrier, n_op - 1 + n_sec - 1)
+
+    def stage(n, me, src, buf, send, recv, peer_of):
+        for d in range(1, n):
+            pltpu.make_async_remote_copy(
+                src_ref=src, dst_ref=buf.at[me], send_sem=send.at[d],
+                recv_sem=recv.at[me], device_id=peer_of((me + d) % n),
+                device_id_type=MESH).start()
+        buf[me] = src[...]
+        for d in range(1, n):
+            slot = (me + n - d) % n
+            pltpu.make_async_remote_copy(
+                src_ref=src, dst_ref=buf.at[slot], send_sem=send.at[d],
+                recv_sem=recv.at[slot], device_id=peer_of(slot),
+                device_id_type=MESH).wait_recv()
+        for d in range(1, n):
+            pltpu.make_async_remote_copy(
+                src_ref=src, dst_ref=buf.at[me], send_sem=send.at[d],
+                recv_sem=recv.at[me], device_id=peer_of((me + d) % n),
+                device_id_type=MESH).wait_send()
+        total = buf[0]
+        for j in range(1, n):
+            total = total + buf[j]
+        return total
+
+    mid[...] = stage(n_op, me_op, x_ref, op_buf, send_a, recv_a,
+                     lambda j: (me_sec, j))
+    local = pltpu.make_async_copy(mid, out_buf, local_sem)
+    local.start()
+    local.wait()
+    o_ref[...] = stage(n_sec, me_sec, out_buf, sec_buf, send_b, recv_b,
+                       lambda j: (j, me_op))
+
+
+def all_sum(values, n_sec, n_op):
+    lane = lax.broadcasted_iota(jnp.int32, (8, 128), 1)
+    tile = jnp.zeros((8, 128), jnp.float32)
+    for k, v in enumerate(values):
+        tile = jnp.where(lane == k, v, tile)
+    tile_spec = pl.BlockSpec(memory_space=pltpu.VMEM)
+    out = pl.pallas_call(
+        functools.partial(all_sum_kernel, n_sec, n_op),
+        out_shape=jax.ShapeDtypeStruct((8, 128), jnp.float32),
+        in_specs=[tile_spec],
+        out_specs=tile_spec,
+        scratch_shapes=[
+            pltpu.VMEM((n_op, 8, 128), jnp.float32),
+            pltpu.VMEM((n_sec, 8, 128), jnp.float32),
+            pltpu.VMEM((8, 128), jnp.float32),
+            pltpu.VMEM((8, 128), jnp.float32),
+            pltpu.SemaphoreType.DMA((n_op,)),
+            pltpu.SemaphoreType.DMA((n_op,)),
+            pltpu.SemaphoreType.DMA((n_sec,)),
+            pltpu.SemaphoreType.DMA((n_sec,)),
+            pltpu.SemaphoreType.DMA(()),
+        ],
+        compiler_params=pltpu.CompilerParams(collective_id=0, has_side_effects=True),
+    )(tile)
+    return tuple(out[0, k] for k in range(len(values)))
+
+
 def shifted(block, axis, distance):
     devices = range(lax.axis_size(axis))
     route = [((i - distance) % len(devices), i) for i in devices]
@@ -37,6 +115,8 @@
     count = float(sector_local * lax.axis_size("sec") * width * width)
     shift_col = shift[:, None, None]
     first_op = lax.axis_index("op") == 0
+    n_sec = lax.axis_size("sec")
+    n_op = lax.axis_size("op")
     state = state_start
     for iteration in range(ITERS):
         window = padded(state, (("sec", 0),), sector_local)
@@ -53,15 +133,15 @@
             first_op, jnp.sum(shift * own_square), 0.0
         )
         norm_part = jnp.where(first_op, jnp.sum(own_square), 0.0)
-        energy_sum, norm_sum = lax.psum((energy_part, norm_part), ("sec", "op"))
+        energy_sum, norm_sum = all_sum((energy_part, norm_part), n_sec, n_op)
         sigma = lax.psum(partial_sigma, "op") + shift_col * state_wide
         ratio = energy_sum / norm_sum
         updated = state_wide - step_size * (sigma - ratio * state_wide)
         if iteration < ITERS - 1:
             factor = jnp.sqrt(count / norm_sum)
         else:
-            new_norm = lax.psum(
-                jnp.where(first_op, jnp.sum(updated * updated), 0.0), ("sec", "op")
+            (new_norm,) = all_sum(
+                (jnp.where(first_op, jnp.sum(updated * updated), 0.0),), n_sec, n_op
             )
             factor = jnp.sqrt(count / new_norm)
         state = (updated * factor).astype(jnp.bfloat16)

time: 553 us -> 446 us (0.81)
  blocking collectives: 372 us -> 0 us
  waiting for transfers between devices: 83.8 us -> 231 us
  Pallas kernels: 0 us -> 98.7 us
  starting transfers between devices: 17.6 us -> 25.6 us
  local copies, waits for them, and re-layouts: 12.1 us -> 19.2 us
    psum x5 -> x0, blocking collectives: 372 us -> none  [the longest x4 298 us: per_device(): energy_sum, norm_sum = lax.psum((energy_part, norm_part), ('sec', 'op'))]
    psum x4, waiting for transfers between devices: 0.08 us -> 153 us  [per_device(): sigma = lax.psum(partial_sigma, 'op') + shift_col * state_wide]
    pallas_call x0 -> x5, Pallas kernels: none -> 98.7 us  [all_sum(): pl.pallas_call(functools.partial(all_sum_kernel, n_sec, n_op), out_shape=...]
    ppermute x4, starting transfers between devices: 12.5 us -> 21.9 us  [padded(): lax.ppermute(head, axis, [((i + 1) % count, i) for i in range(count)])]
    slice x0 -> x5, local copies, waits for them, and re-layouts: none -> 6.53 us  [all_sum(): return tuple((out[0, k] for k in range(len(values))))]
    ppermute x4, waiting for transfers between devices: 15.5 us -> 9.87 us  [padded(): lax.ppermute(head, axis, [((i + 1) % count, i) for i in range(count)])]
  transfers between devices with their start and end apart: 13 -> 13, of which waited for: 8 -> 12; matrix products, arithmetic and copies ran while one was open for 1% -> 2% of each run, Pallas kernels for 0% -> 18%
where the time goes in v2:
time: 446 us; the launch traced here: 443 us
  waiting for transfers between devices  231 us (52%)
  Pallas kernels  98.7 us (22%)
  between operations  30.8 us (7%)
  starting transfers between devices  25.6 us (6%)
  matrix products  24.2 us (5%)
  local copies, waits for them, and re-layouts  19.2 us (4%)
  other arithmetic  13.7 us (3%)
    psum x4, waiting for transfers between devices, per_device(): sigma = lax.psum(partial_sigma, 'op') + shift_col * state_wide  153 us
    pallas_call x5, Pallas kernels, all_sum(): pl.pallas_call(functools.partial(all_sum_kernel, n_sec, n_op), out_shape=...  98.7 us
    ppermute x1, waiting for transfers between devices, shifted(): return lax.ppermute(block, axis, route)  47.6 us
    ppermute x4, starting transfers between devices, padded(): lax.ppermute(head, axis, [((i + 1) % count, i) for i in range(count)])  21.9 us
    ppermute x4, waiting for transfers between devices, padded(): lax.ppermute(tail, axis, [(i, (i + 1) % count) for i in range(count)])  21 us
    dot_general x4, matrix products, per_device(): jnp.einsum('tbij,tbjk->bik', halfway, right_ops, preferred_element_type=j...  19.9 us
    ppermute x4, waiting for transfers between devices, padded(): lax.ppermute(head, axis, [((i + 1) % count, i) for i in range(count)])  9.87 us
  transfers between devices with their start and end apart: 13, of which 12 were waited for; matrix products, arithmetic and copies ran while one was open for 2% of the time, Pallas kernels for 18%

profile of v2, /device:TPU:1, one launch (start us, length us, event | category | flops | bytes accessed | tf_op | source)
XLA Modules:
  0.0 443.3 jit_solution(7728303376387900427)
XLA Ops:
  9.8 6.2 %collective-permute-start.1 = (bf16[2,256,256]{2,1,0:T(8,128)(2,1)}, bf16[2,256,256]{2,1,0:T(8,128)(2,1)S(1)}, u32[]{:S(2)}, u32[]{:S(2)}) collective-permute-start(bf16[2,256,256]{2,1,0:T(8,128)(2,1)} %param.6), channel_id=1, source_target_pairs={{8,0},{16,8},{24,16},{32,24},{40,32},{48,40},{56,48},{64,56},{72,6... | collective-permute-start | bytes 786440 | tf_op jit(solution)/shard_map/ppermute | solution.py:27
  16.9 5.3 %collective-permute-done = bf16[2,256,256]{2,1,0:T(8,128)(2,1)S(1)} collective-permute-done((bf16[2,256,256]{2,1,0:T(8,128)(2,1)}, bf16[2,256,256]{2,1,0:T(8,128)(2,1)S(1)}, u32[]{:S(2)}, u32[]{:S(2)}) %collective-permute-start) | collective-permute-done | bytes 262176 | tf_op jit(solution)/shard_map/ppermute | solution.py:25
  25.2 5.0 %fusion.86 = (f32[]{:T(128)}, f32[]{:T(128)}, f32[2]{0:T(128)S(1)}, f32[2,256,256]{2,1,0:T(8,128)}) fusion(bf16[2,256,256]{2,1,0:T(8,128)(2,1)S(1)} %copy-done.1, bf16[8,2,256,256]{3,2,1,0:T(8,128)(2,1)S(1)} %copy-done, bf16[8,2,256,256]{3,2,1,0:T(8,128)(2,1)} %bitcast.66, bf16[8,2,256,256]{3,2,1,0:T(8,128)(2,1)} %param.7), kind=kOutput, calls=%fused_computation.67 | convolution fusion | flops 1075576832 | bytes 7077904 | tf_op jit(solution)/shard_map/tbij,tbjk->bik/dot_general | solution.py:127
  33.5 19.5 %shard_map.77 = f32[8,128]{1,0:T(8,128)} custom-call(f32[8,128]{1,0:T(8,128)} %broadcast_select_fusion.3.x_ref), custom_call_target="tpu_custom_call" | custom-call | tf_op jit(solution)/shard_map/pallas_call | solution.py:85
  56.4 39.5 %all-reduce.5.cloned.1.call-done = f32[2,256,256]{2,1,0:T(8,128)} async-done(((f32[2,256,256]{2,1,0:T(8,128)}), f32[2,256,256]{2,1,0:T(8,128)}) %all-reduce.5.cloned.1.call-update) | async-done | bytes 524304 | tf_op jit(solution)/shard_map/psum | solution.py:137
  97.1 5.2 %collective-permute-start.3 = (bf16[2,256,256]{2,1,0:T(8,128)(2,1)S(1)}, bf16[2,256,256]{2,1,0:T(8,128)(2,1)S(1)}, u32[]{:S(2)}, u32[]{:S(2)}) collective-permute-start(bf16[2,256,256]{2,1,0:T(8,128)(2,1)S(1)} %fusion.98), channel_id=1, source_target_pairs={{8,0},{16,8},{24,16},{32,24},{40,32},{48,40},{56,48},{64,56},{72,6... | collective-permute-start | bytes 786440 | tf_op jit(solution)/shard_map/ppermute | solution.py:27
  105.7 5.2 %collective-permute-done.2 = bf16[2,256,256]{2,1,0:T(8,128)(2,1)S(1)} collective-permute-done((bf16[2,256,256]{2,1,0:T(8,128)(2,1)S(1)}, bf16[2,256,256]{2,1,0:T(8,128)(2,1)S(1)}, u32[]{:S(2)}, u32[]{:S(2)}) %collective-permute-start.2) | collective-permute-done | bytes 262176 | tf_op jit(solution)/shard_map/ppermute | solution.py:25
  113.0 5.0 %fusion.88 = (f32[]{:T(128)}, f32[]{:T(128)}, f32[2]{0:T(128)S(1)}, f32[2,256,256]{2,1,0:T(8,128)}) fusion(bf16[2,256,256]{2,1,0:T(8,128)(2,1)S(1)} %fusion.98, bf16[8,2,256,256]{3,2,1,0:T(8,128)(2,1)S(1)} %copy-done, bf16[8,2,256,256]{3,2,1,0:T(8,128)(2,1)} %bitcast.67, bf16[8,2,256,256]{3,2,1,0:T(8,128)(2,1)} %param.7), kind=kOutput, calls=%fused_computation.69 | convolution fusion | flops 1075576832 | bytes 7077904 | tf_op jit(solution)/shard_map/tbij,tbjk->bik/dot_general | solution.py:127
  121.3 20.1 %shard_map.78 = f32[8,128]{1,0:T(8,128)} custom-call(f32[8,128]{1,0:T(8,128)} %broadcast_select_fusion.2.x_ref), custom_call_target="tpu_custom_call" | custom-call | tf_op jit(solution)/shard_map/pallas_call | solution.py:85
  144.8 37.4 %all-reduce.7.cloned.1.call-done = f32[2,256,256]{2,1,0:T(8,128)} async-done(((f32[2,256,256]{2,1,0:T(8,128)}), f32[2,256,256]{2,1,0:T(8,128)}) %all-reduce.7.cloned.1.call-update) | async-done | bytes 524304 | tf_op jit(solution)/shard_map/psum | solution.py:137
  183.4 5.2 %collective-permute-start.5 = (bf16[2,256,256]{2,1,0:T(8,128)(2,1)S(1)}, bf16[2,256,256]{2,1,0:T(8,128)(2,1)S(1)}, u32[]{:S(2)}, u32[]{:S(2)}) collective-permute-start(bf16[2,256,256]{2,1,0:T(8,128)(2,1)S(1)} %fusion.104), channel_id=1, source_target_pairs={{8,0},{16,8},{24,16},{32,24},{40,32},{48,40},{56,48},{64,56},{72,6... | collective-permute-start | bytes 786440 | tf_op jit(solution)/shard_map/ppermute | solution.py:27
  192.0 5.2 %collective-permute-done.4 = bf16[2,256,256]{2,1,0:T(8,128)(2,1)S(1)} collective-permute-done((bf16[2,256,256]{2,1,0:T(8,128)(2,1)S(1)}, bf16[2,256,256]{2,1,0:T(8,128)(2,1)S(1)}, u32[]{:S(2)}, u32[]{:S(2)}) %collective-permute-start.4) | collective-permute-done | bytes 262176 | tf_op jit(solution)/shard_map/ppermute | solution.py:25
  199.3 5.0 %fusion.90 = (f32[]{:T(128)}, f32[]{:T(128)}, f32[2]{0:T(128)S(1)}, f32[2,256,256]{2,1,0:T(8,128)}) fusion(bf16[2,256,256]{2,1,0:T(8,128)(2,1)S(1)} %fusion.104, bf16[8,2,256,256]{3,2,1,0:T(8,128)(2,1)S(1)} %copy-done, bf16[8,2,256,256]{3,2,1,0:T(8,128)(2,1)} %bitcast.68, bf16[8,2,256,256]{3,2,1,0:T(8,128)(2,1)} %param.7), kind=kOutput, calls=%fused_computation.71 | convolution fusion | flops 1075576832 | bytes 7077904 | tf_op jit(solution)/shard_map/tbij,tbjk->bik/dot_general | solution.py:127
  207.5 20.1 %shard_map.79 = f32[8,128]{1,0:T(8,128)} custom-call(f32[8,128]{1,0:T(8,128)} %broadcast_select_fusion.1.x_ref), custom_call_target="tpu_custom_call" | custom-call | tf_op jit(solution)/shard_map/pallas_call | solution.py:85
  231.1 37.5 %all-reduce.9.cloned.1.call-done = f32[2,256,256]{2,1,0:T(8,128)} async-done(((f32[2,256,256]{2,1,0:T(8,128)}), f32[2,256,256]{2,1,0:T(8,128)}) %all-reduce.9.cloned.1.call-update) | async-done | bytes 524304 | tf_op jit(solution)/shard_map/psum | solution.py:137
  269.8 5.2 %collective-permute-start.7 = (bf16[2,256,256]{2,1,0:T(8,128)(2,1)S(1)}, bf16[2,256,256]{2,1,0:T(8,128)(2,1)S(1)}, u32[]{:S(2)}, u32[]{:S(2)}) collective-permute-start(bf16[2,256,256]{2,1,0:T(8,128)(2,1)S(1)} %fusion.110), channel_id=1, source_target_pairs={{8,0},{16,8},{24,16},{32,24},{40,32},{48,40},{56,48},{64,56},{72,6... | collective-permute-start | bytes 786440 | tf_op jit(solution)/shard_map/ppermute | solution.py:27
  278.3 5.2 %collective-permute-done.6 = bf16[2,256,256]{2,1,0:T(8,128)(2,1)S(1)} collective-permute-done((bf16[2,256,256]{2,1,0:T(8,128)(2,1)S(1)}, bf16[2,256,256]{2,1,0:T(8,128)(2,1)S(1)}, u32[]{:S(2)}, u32[]{:S(2)}) %collective-permute-start.6) | collective-permute-done | bytes 262176 | tf_op jit(solution)/shard_map/ppermute | solution.py:25
  285.6 5.0 %fusion.92 = (f32[]{:T(128)}, f32[]{:T(128)}, f32[2]{0:T(128)S(1)}, f32[2,256,256]{2,1,0:T(8,128)}) fusion(bf16[2,256,256]{2,1,0:T(8,128)(2,1)S(1)} %fusion.110, bf16[8,2,256,256]{3,2,1,0:T(8,128)(2,1)S(1)} %copy-done, bf16[8,2,256,256]{3,2,1,0:T(8,128)(2,1)} %bitcast.65, bf16[8,2,256,256]{3,2,1,0:T(8,128)(2,1)} %param.7), kind=kOutput, calls=%fused_computation.73 | convolution fusion | flops 1075576832 | bytes 7077904 | tf_op jit(solution)/shard_map/tbij,tbjk->bik/dot_general | solution.py:127
  293.9 20.1 %shard_map.80 = f32[8,128]{1,0:T(8,128)} custom-call(f32[8,128]{1,0:T(8,128)} %broadcast_select_fusion.x_ref), custom_call_target="tpu_custom_call" | custom-call | tf_op jit(solution)/shard_map/pallas_call | solution.py:85
  316.6 38.2 %all-reduce.11.cloned.1.call-done = f32[2,256,256]{2,1,0:T(8,128)} async-done(((f32[2,256,256]{2,1,0:T(8,128)}), f32[2,256,256]{2,1,0:T(8,128)}) %all-reduce.11.cloned.1.call-update) | async-done | bytes 524304 | tf_op jit(solution)/shard_map/psum | solution.py:137
  357.9 18.9 %shard_map.81 = f32[8,128]{1,0:T(8,128)} custom-call(f32[8,128]{1,0:T(8,128)} %iota.60.x_ref), custom_call_target="tpu_custom_call" | custom-call | tf_op jit(solution)/shard_map/pallas_call | solution.py:85
  380.0 4.3 fusion.40
  385.3 47.6 %collective-permute-done.8 = bf16[8,2,256,256]{2,3,0,1:T(8,128)(2,1)} collective-permute-done((bf16[8,2,256,256]{2,3,0,1:T(8,128)(2,1)}, bf16[8,2,256,256]{2,3,0,1:T(8,128)(2,1)}, u32[]{:S(2)}, u32[]{:S(2)}) %collective-permute-start.8) | collective-permute-done | bytes 2097184 | tf_op jit(solution)/shard_map/ppermute | solution.py:109
  432.9 3.9 copy.19
  (65 shorter events, 42.7 us)
Async XLA Ops:
  7.2 18.0 %copy-start = (bf16[8,2,256,256]{3,2,1,0:T(8,128)(2,1)S(1)}, bf16[8,2,256,256]{3,2,1,0:T(8,128)(2,1)}, u32[]{:S(2)}) copy-start(bf16[8,2,256,256]{3,2,1,0:T(8,128)(2,1)} %param.8) | copy-start | bytes 6291460
  7.2 88.7 %all-reduce.5.cloned.1.call-start = ((), (), s32[]{:S(2)}) async-start(), calls=%async_computation | async-start | bytes 1048576 | tf_op jit(solution)/shard_map/psum | solution.py:137
  7.2 14.9 %collective-permute-start = (bf16[2,256,256]{2,1,0:T(8,128)(2,1)}, bf16[2,256,256]{2,1,0:T(8,128)(2,1)S(1)}, u32[]{:S(2)}, u32[]{:S(2)}) collective-permute-start(bf16[2,256,256]{2,1,0:T(8,128)(2,1)} %param.6), channel_id=1, source_target_pairs={{0,8},{8,16},{16,24},{24,32},{32,40},{40,48},{48,56},{56,64},{64,7... | collective-permute-start | bytes 786440 | tf_op jit(solution)/shard_map/ppermute | solution.py:25
  9.8 12.4 %collective-permute-start.1 = (bf16[2,256,256]{2,1,0:T(8,128)(2,1)}, bf16[2,256,256]{2,1,0:T(8,128)(2,1)S(1)}, u32[]{:S(2)}, u32[]{:S(2)}) collective-permute-start(bf16[2,256,256]{2,1,0:T(8,128)(2,1)} %param.6), channel_id=1, source_target_pairs={{8,0},{16,8},{24,16},{32,24},{40,32},{48,40},{56,48},{64,56},{72,6... | collective-permute-start | bytes 786440 | tf_op jit(solution)/shard_map/ppermute | solution.py:27
  23.2 2.0 copy-start.1
  25.2 5.0 %copy-start.3 = (f32[2]{0:T(128)S(1)}, f32[2]{0:T(128)}, u32[]{:S(2)}) copy-start(f32[2]{0:T(128)} %param.9) | copy-start | bytes 28
  32.8 149.4 %all-reduce.7.cloned.1.call-start = ((), (), s32[]{:S(2)}) async-start(), calls=%async_computation.1 | async-start | bytes 1048576 | tf_op jit(solution)/shard_map/psum | solution.py:137
  97.1 8.6 %collective-permute-start.3 = (bf16[2,256,256]{2,1,0:T(8,128)(2,1)S(1)}, bf16[2,256,256]{2,1,0:T(8,128)(2,1)S(1)}, u32[]{:S(2)}, u32[]{:S(2)}) collective-permute-start(bf16[2,256,256]{2,1,0:T(8,128)(2,1)S(1)} %fusion.98), channel_id=1, source_target_pairs={{8,0},{16,8},{24,16},{32,24},{40,32},{48,40},{56,48},{64,56},{72,6... | collective-permute-start | bytes 786440 | tf_op jit(solution)/shard_map/ppermute | solution.py:27
  102.4 8.5 %collective-permute-start.2 = (bf16[2,256,256]{2,1,0:T(8,128)(2,1)S(1)}, bf16[2,256,256]{2,1,0:T(8,128)(2,1)S(1)}, u32[]{:S(2)}, u32[]{:S(2)}) collective-permute-start(bf16[2,256,256]{2,1,0:T(8,128)(2,1)S(1)} %fusion.98), channel_id=1, source_target_pairs={{0,8},{8,16},{16,24},{24,32},{32,40},{40,48},{48,56},{56,64},{64,7... | collective-permute-start | bytes 786440 | tf_op jit(solution)/shard_map/ppermute | solution.py:25
  120.6 147.9 %all-reduce.9.cloned.1.call-start = ((), (), s32[]{:S(2)}) async-start(), calls=%async_computation.2 | async-start | bytes 1048576 | tf_op jit(solution)/shard_map/psum | solution.py:137
  183.4 8.6 %collective-permute-start.5 = (bf16[2,256,256]{2,1,0:T(8,128)(2,1)S(1)}, bf16[2,256,256]{2,1,0:T(8,128)(2,1)S(1)}, u32[]{:S(2)}, u32[]{:S(2)}) collective-permute-start(bf16[2,256,256]{2,1,0:T(8,128)(2,1)S(1)} %fusion.104), channel_id=1, source_target_pairs={{8,0},{16,8},{24,16},{32,24},{40,32},{48,40},{56,48},{64,56},{72,6... | collective-permute-start | bytes 786440 | tf_op jit(solution)/shard_map/ppermute | solution.py:27
  188.7 8.5 %collective-permute-start.4 = (bf16[2,256,256]{2,1,0:T(8,128)(2,1)S(1)}, bf16[2,256,256]{2,1,0:T(8,128)(2,1)S(1)}, u32[]{:S(2)}, u32[]{:S(2)}) collective-permute-start(bf16[2,256,256]{2,1,0:T(8,128)(2,1)S(1)} %fusion.104), channel_id=1, source_target_pairs={{0,8},{8,16},{16,24},{24,32},{32,40},{40,48},{48,56},{56,64},{64,7... | collective-permute-start | bytes 786440 | tf_op jit(solution)/shard_map/ppermute | solution.py:25
  199.3 75.7 %copy-start.4 = (s32[2]{0:T(128)S(1)}, s32[2]{0:T(128)}, u32[]{:S(2)}) copy-start(s32[2]{0:T(128)} %param.11) | copy-start | bytes 28
  206.9 147.9 %all-reduce.11.cloned.1.call-start = ((), (), s32[]{:S(2)}) async-start(), calls=%async_computation.3 | async-start | bytes 1048576 | tf_op jit(solution)/shard_map/psum | solution.py:137
  269.8 8.6 %collective-permute-start.7 = (bf16[2,256,256]{2,1,0:T(8,128)(2,1)S(1)}, bf16[2,256,256]{2,1,0:T(8,128)(2,1)S(1)}, u32[]{:S(2)}, u32[]{:S(2)}) collective-permute-start(bf16[2,256,256]{2,1,0:T(8,128)(2,1)S(1)} %fusion.110), channel_id=1, source_target_pairs={{8,0},{16,8},{24,16},{32,24},{40,32},{48,40},{56,48},{64,56},{72,6... | collective-permute-start | bytes 786440 | tf_op jit(solution)/shard_map/ppermute | solution.py:27
  275.0 8.5 %collective-permute-start.6 = (bf16[2,256,256]{2,1,0:T(8,128)(2,1)S(1)}, bf16[2,256,256]{2,1,0:T(8,128)(2,1)S(1)}, u32[]{:S(2)}, u32[]{:S(2)}) collective-permute-start(bf16[2,256,256]{2,1,0:T(8,128)(2,1)S(1)} %fusion.110), channel_id=1, source_target_pairs={{0,8},{8,16},{16,24},{24,32},{32,40},{40,48},{48,56},{56,64},{64,7... | collective-permute-start | bytes 786440 | tf_op jit(solution)/shard_map/ppermute | solution.py:25
  380.0 4.3 copy-start.2
  384.3 48.6 %collective-permute-start.8 = (bf16[8,2,256,256]{2,3,0,1:T(8,128)(2,1)}, bf16[8,2,256,256]{2,3,0,1:T(8,128)(2,1)}, u32[]{:S(2)}, u32[]{:S(2)}) collective-permute-start(bf16[8,2,256,256]{2,3,0,1:T(8,128)(2,1)} %fusion.40), channel_id=1, source_target_pairs={{248,0},{0,8},{8,16},{16,24},{24,32},{32,40},{40,48},{48,56},{56,6... | collective-permute-start | bytes 6291464 | tf_op jit(solution)/shard_map/ppermute | solution.py:109
Sparse Core Ops, SparseCore 0:
  32.9 62.9 all-reduce.4
  120.7 61.4 all-reduce.6
  207.0 61.4 all-reduce.8
  293.4 61.3 all-reduce.10

commit v3 on v2

--- a/solution.py
+++ b/solution.py
@@ -101,6 +101,142 @@
         compiler_params=pltpu.CompilerParams(collective_id=0, has_side_effects=True),
     )(tile)
     return tuple(out[0, k] for k in range(len(values)))
+
+
+def sigma_sum_kernel(n_sec, n_op, x_ref, t_ref, o_ref, s_ref,
+                     rs_buf, red, red_out, ag_buf, op_buf, sec_buf, mid, mid_out,
+                     send_rs, recv_rs, send_ag, recv_ag, send_a, recv_a,
+                     send_b, recv_b, local_sem):
+    me_sec = lax.axis_index("sec")
+    me_op = lax.axis_index("op")
+    barrier = pltpu.get_barrier_semaphore()
+    for d in range(1, n_op):
+        pl.semaphore_signal(barrier, 1, device_id=(me_sec, (me_op + d) % n_op),
+                            device_id_type=MESH)
+    for d in range(1, n_sec):
+        pl.semaphore_signal(barrier, 1, device_id=((me_sec + d) % n_sec, me_op),
+                            device_id_type=MESH)
+    pl.semaphore_wait(barrier, n_op - 1 + n_sec - 1)
+
+    def op_peer(j):
+        return (me_sec, j)
+
+    def sec_peer(j):
+        return (j, me_op)
+
+    def rs_copy(d):
+        j = (me_op + d) % n_op
+        return pltpu.make_async_remote_copy(
+            src_ref=x_ref.at[j], dst_ref=rs_buf.at[me_op], send_sem=send_rs.at[d],
+            recv_sem=recv_rs.at[me_op], device_id=op_peer(j), device_id_type=MESH)
+
+    def rs_recv(d):
+        slot = (me_op + n_op - d) % n_op
+        return pltpu.make_async_remote_copy(
+            src_ref=x_ref.at[me_op], dst_ref=rs_buf.at[slot], send_sem=send_rs.at[d],
+            recv_sem=recv_rs.at[slot], device_id=op_peer(slot), device_id_type=MESH)
+
+    def gather_copy(n, me, src, buf, send, recv, peer_of, d):
+        return pltpu.make_async_remote_copy(
+            src_ref=src, dst_ref=buf.at[me], send_sem=send.at[d],
+            recv_sem=recv.at[me], device_id=peer_of((me + d) % n), device_id_type=MESH)
+
+    def gather_recv(n, me, src, buf, send, recv, peer_of, d):
+        slot = (me + n - d) % n
+        return pltpu.make_async_remote_copy(
+            src_ref=src, dst_ref=buf.at[slot], send_sem=send.at[d],
+            recv_sem=recv.at[slot], device_id=peer_of(slot), device_id_type=MESH)
+
+    def ordered_sum(buf, n):
+        total = buf[0]
+        for j in range(1, n):
+            total = total + buf[j]
+        return total
+
+    for d in range(1, n_op):
+        rs_copy(d).start()
+    a_args = (n_op, me_op, t_ref, op_buf, send_a, recv_a, op_peer)
+    for d in range(1, n_op):
+        gather_copy(*a_args, d).start()
+    rs_buf[me_op] = x_ref[me_op]
+    op_buf[me_op] = t_ref[...]
+
+    for d in range(1, n_op):
+        gather_recv(*a_args, d).wait_recv()
+    mid[...] = ordered_sum(op_buf, n_op)
+    local = pltpu.make_async_copy(mid, mid_out, local_sem.at[0])
+    local.start()
+    local.wait()
+    b_args = (n_sec, me_sec, mid_out, sec_buf, send_b, recv_b, sec_peer)
+    for d in range(1, n_sec):
+        gather_copy(*b_args, d).start()
+    sec_buf[me_sec] = mid_out[...]
+
+    for d in range(1, n_op):
+        rs_recv(d).wait_recv()
+    red[...] = ordered_sum(rs_buf, n_op)
+    local = pltpu.make_async_copy(red, red_out, local_sem.at[1])
+    local.start()
+    local.wait()
+    g_args = (n_op, me_op, red_out, ag_buf, send_ag, recv_ag, op_peer)
+    for d in range(1, n_op):
+        gather_copy(*g_args, d).start()
+    ag_buf[me_op] = red_out[...]
+
+    for d in range(1, n_sec):
+        gather_recv(*b_args, d).wait_recv()
+    s_ref[...] = ordered_sum(sec_buf, n_sec)
+    for d in range(1, n_op):
+        gather_recv(*g_args, d).wait_recv()
+    o_ref[...] = ag_buf[...]
+
+    for d in range(1, n_op):
+        rs_copy(d).wait_send()
+        gather_copy(*a_args, d).wait_send()
+        gather_copy(*g_args, d).wait_send()
+    for d in range(1, n_sec):
+        gather_copy(*b_args, d).wait_send()
+
+
+def sigma_sum(partial, values, n_sec, n_op):
+    shape = partial.shape
+    rows = shape[0] * shape[1] // n_op
+    chunks = partial.reshape(n_op, rows, shape[2])
+    lane = lax.broadcasted_iota(jnp.int32, (8, 128), 1)
+    tile = jnp.zeros((8, 128), jnp.float32)
+    for k, v in enumerate(values):
+        tile = jnp.where(lane == k, v, tile)
+    vmem = pl.BlockSpec(memory_space=pltpu.VMEM)
+    total, sums = pl.pallas_call(
+        functools.partial(sigma_sum_kernel, n_sec, n_op),
+        out_shape=(
+            jax.ShapeDtypeStruct(chunks.shape, jnp.float32),
+            jax.ShapeDtypeStruct((8, 128), jnp.float32),
+        ),
+        in_specs=[vmem, vmem],
+        out_specs=(vmem, vmem),
+        scratch_shapes=[
+            pltpu.VMEM(chunks.shape, jnp.float32),
+            pltpu.VMEM((rows, shape[2]), jnp.float32),
+            pltpu.VMEM((rows, shape[2]), jnp.float32),
+            pltpu.VMEM(chunks.shape, jnp.float32),
+            pltpu.VMEM((n_op, 8, 128), jnp.float32),
+            pltpu.VMEM((n_sec, 8, 128), jnp.float32),
+            pltpu.VMEM((8, 128), jnp.float32),
+            pltpu.VMEM((8, 128), jnp.float32),
+            pltpu.SemaphoreType.DMA((n_op,)),
+            pltpu.SemaphoreType.DMA((n_op,)),
+            pltpu.SemaphoreType.DMA((n_op,)),
+            pltpu.SemaphoreType.DMA((n_op,)),
+            pltpu.SemaphoreType.DMA((n_op,)),
+            pltpu.SemaphoreType.DMA((n_op,)),
+            pltpu.SemaphoreType.DMA((n_sec,)),
+            pltpu.SemaphoreType.DMA((n_sec,)),
+            pltpu.SemaphoreType.DMA((2,)),
+        ],
+        compiler_params=pltpu.CompilerParams(collective_id=1, has_side_effects=True),
+    )(chunks, tile)
+    return total.reshape(shape), tuple(sums[0, k] for k in range(len(values)))
 
 
 def shifted(block, axis, distance):
@@ -133,8 +269,10 @@
             first_op, jnp.sum(shift * own_square), 0.0
         )
         norm_part = jnp.where(first_op, jnp.sum(own_square), 0.0)
-        energy_sum, norm_sum = all_sum((energy_part, norm_part), n_sec, n_op)
-        sigma = lax.psum(partial_sigma, "op") + shift_col * state_wide
+        sigma_terms, (energy_sum, norm_sum) = sigma_sum(
+            partial_sigma, (energy_part, norm_part), n_sec, n_op
+        )
+        sigma = sigma_terms + shift_col * state_wide
         ratio = energy_sum / norm_sum
         updated = state_wide - step_size * (sigma - ratio * state_wide)
         if iteration < ITERS - 1:

time: 446 us -> 290 us (0.65)
  waiting for transfers between devices: 231 us -> 86.7 us
  between operations: 30.8 us -> 17.7 us
  Pallas kernels: 98.7 us -> 109 us
  starting transfers between devices: 25.6 us -> 18.4 us
    psum x4 -> x0, waiting for transfers between devices: 153 us -> none  [per_device(): sigma = lax.psum(partial_sigma, 'op') + shift_col * state_wide]
    pallas_call x0 -> x4, Pallas kernels: none -> 92.5 us  [sigma_sum(): pl.pallas_call(functools.partial(sigma_sum_kernel, n_sec, n_op), out_shap...]
    pallas_call x5 -> x1, Pallas kernels: 98.7 us -> 16.4 us  [all_sum(): pl.pallas_call(functools.partial(all_sum_kernel, n_sec, n_op), out_shape=...]
    ppermute x4, waiting for transfers between devices: 9.87 us -> 16.9 us  [padded(): lax.ppermute(head, axis, [((i + 1) % count, i) for i in range(count)])]
    ppermute x4, starting transfers between devices: 21.9 us -> 15.4 us  [padded(): lax.ppermute(head, axis, [((i + 1) % count, i) for i in range(count)])]
    slice x0 -> x4, local copies, waits for them, and re-layouts: none -> 5.33 us  [sigma_sum(): sums[0, k]]
    slice x5 -> x1, local copies, waits for them, and re-layouts: 6.53 us -> 1.19 us  [all_sum(): return tuple((out[0, k] for k in range(len(values))))]
  transfers between devices with their start and end apart: 13 -> 9, of which waited for: 12 -> 8; matrix products, arithmetic and copies ran while one was open for 2% -> 0% of each run, Pallas kernels for 18% -> 0%
where the time goes in v3:
time: 290 us; the launch traced here: 289 us
  Pallas kernels  109 us (38%)
  waiting for transfers between devices  86.7 us (30%)
  matrix products  24.2 us (8%)
  local copies, waits for them, and re-layouts  19.2 us (7%)
  starting transfers between devices  18.4 us (6%)
  between operations  17.7 us (6%)
  other arithmetic  13.7 us (5%)
    pallas_call x4, Pallas kernels, sigma_sum(): pl.pallas_call(functools.partial(sigma_sum_kernel, n_sec, n_op), out_shap...  92.5 us
    ppermute x1, waiting for transfers between devices, shifted(): return lax.ppermute(block, axis, route)  48.7 us
    ppermute x4, waiting for transfers between devices, padded(): lax.ppermute(tail, axis, [(i, (i + 1) % count) for i in range(count)])  21.2 us
    dot_general x4, matrix products, per_device(): jnp.einsum('tbij,tbjk->bik', halfway, right_ops, preferred_element_type=j...  19.9 us
    ppermute x4, waiting for transfers between devices, padded(): lax.ppermute(head, axis, [((i + 1) % count, i) for i in range(count)])  16.9 us
    pallas_call x1, Pallas kernels, all_sum(): pl.pallas_call(functools.partial(all_sum_kernel, n_sec, n_op), out_shape=...  16.4 us
    ppermute x4, starting transfers between devices, padded(): lax.ppermute(head, axis, [((i + 1) % count, i) for i in range(count)])  15.4 us
    gather x4, local copies, waits for them, and re-layouts, per_device(): sources = window[partner]  8 us
  transfers between devices with their start and end apart: 9, of which 8 were waited for; matrix products, arithmetic and copies ran while one was open for 0% of the time, Pallas kernels for 0%

profile of v3, /device:TPU:1, one launch (start us, length us, event | category | flops | bytes accessed | tf_op | source)
XLA Modules:
  0.0 288.8 jit_solution(455907681339658043)
XLA Ops:
  0.6 2.5 collective-permute-start
  3.2 6.2 %collective-permute-start.1 = (bf16[2,256,256]{2,1,0:T(8,128)(2,1)}, bf16[2,256,256]{2,1,0:T(8,128)(2,1)S(1)}, u32[]{:S(2)}, u32[]{:S(2)}) collective-permute-start(bf16[2,256,256]{2,1,0:T(8,128)(2,1)} %param.6), channel_id=1, source_target_pairs={{8,0},{16,8},{24,16},{32,24},{40,32},{48,40},{56,48},{64,56},{72,6... | collective-permute-start | bytes 786440 | tf_op jit(solution)/shard_map/ppermute | solution.py:27
  10.3 5.3 %collective-permute-done = bf16[2,256,256]{2,1,0:T(8,128)(2,1)S(1)} collective-permute-done((bf16[2,256,256]{2,1,0:T(8,128)(2,1)}, bf16[2,256,256]{2,1,0:T(8,128)(2,1)S(1)}, u32[]{:S(2)}, u32[]{:S(2)}) %collective-permute-start) | collective-permute-done | bytes 262176 | tf_op jit(solution)/shard_map/ppermute | solution.py:25
  18.6 5.0 %fusion.58 = (f32[]{:T(128)}, f32[2]{0:T(128)S(1)}, f32[]{:T(128)}, f32[2,256,256,1]{2,1,3,0:T(8,128)}) fusion(bf16[2,256,256]{2,1,0:T(8,128)(2,1)S(1)} %copy-done.1, bf16[8,2,256,256]{3,2,1,0:T(8,128)(2,1)S(1)} %copy-done, bf16[8,2,256,256]{3,2,1,0:T(8,128)(2,1)} %bitcast.83, bf16[8,2,256,256]{3,2,1,0:T(8,128)(2,1)} %param.7), kind=kOutput, calls=%fused_computation.63 | convolution fusion | flops 1075576832 | bytes 7077904 | tf_op jit(solution)/shard_map/tbij,tbjk->bik/dot_general | solution.py:263
  26.8 25.6 %shard_map.77 = (f32[8,64,256]{2,1,0:T(8,128)}, f32[8,128]{1,0:T(8,128)}) custom-call(f32[8,64,256]{2,1,0:T(8,128)} %bitcast.89, f32[8,128]{1,0:T(8,128)} %broadcast_select_fusion.3.t_ref), custom_call_target="tpu_custom_call" | custom-call | tf_op jit(solution)/shard_map/pallas_call | solution.py:210
  57.0 3.6 %collective-permute-start.3 = (bf16[2,256,256]{2,1,0:T(8,128)(2,1)S(1)}, bf16[2,256,256]{2,1,0:T(8,128)(2,1)S(1)}, u32[]{:S(2)}, u32[]{:S(2)}) collective-permute-start(bf16[2,256,256]{2,1,0:T(8,128)(2,1)S(1)} %fusion.70), channel_id=1, source_target_pairs={{8,0},{16,8},{24,16},{32,24},{40,32},{48,40},{56,48},{64,56},{72,6... | collective-permute-start | bytes 786440 | tf_op jit(solution)/shard_map/ppermute | solution.py:27
  60.6 5.2 %collective-permute-done.3 = bf16[2,256,256]{2,1,0:T(8,128)(2,1)S(1)} collective-permute-done((bf16[2,256,256]{2,1,0:T(8,128)(2,1)S(1)}, bf16[2,256,256]{2,1,0:T(8,128)(2,1)S(1)}, u32[]{:S(2)}, u32[]{:S(2)}) %collective-permute-start.3) | collective-permute-done | bytes 262176 | tf_op jit(solution)/shard_map/ppermute | solution.py:27
  65.8 5.2 %collective-permute-done.2 = bf16[2,256,256]{2,1,0:T(8,128)(2,1)S(1)} collective-permute-done((bf16[2,256,256]{2,1,0:T(8,128)(2,1)S(1)}, bf16[2,256,256]{2,1,0:T(8,128)(2,1)S(1)}, u32[]{:S(2)}, u32[]{:S(2)}) %collective-permute-start.2) | collective-permute-done | bytes 262176 | tf_op jit(solution)/shard_map/ppermute | solution.py:25
  73.1 5.0 %fusion.60 = (f32[]{:T(128)}, f32[2]{0:T(128)S(1)}, f32[]{:T(128)}, f32[2,256,256,1]{2,1,3,0:T(8,128)}) fusion(bf16[2,256,256]{2,1,0:T(8,128)(2,1)S(1)} %fusion.70, bf16[8,2,256,256]{3,2,1,0:T(8,128)(2,1)S(1)} %copy-done, bf16[8,2,256,256]{3,2,1,0:T(8,128)(2,1)} %bitcast.84, bf16[8,2,256,256]{3,2,1,0:T(8,128)(2,1)} %param.7), kind=kOutput, calls=%fused_computation.65 | convolution fusion | flops 1075576832 | bytes 7077904 | tf_op jit(solution)/shard_map/tbij,tbjk->bik/dot_general | solution.py:263
  81.3 22.6 %shard_map.78 = (f32[8,64,256]{2,1,0:T(8,128)}, f32[8,128]{1,0:T(8,128)}) custom-call(f32[8,64,256]{2,1,0:T(8,128)} %bitcast.90, f32[8,128]{1,0:T(8,128)} %broadcast_select_fusion.2.t_ref), custom_call_target="tpu_custom_call" | custom-call | tf_op jit(solution)/shard_map/pallas_call | solution.py:210
  108.6 2.6 collective-permute-start.5
  111.2 5.9 %collective-permute-done.5 = bf16[2,256,256]{2,1,0:T(8,128)(2,1)S(1)} collective-permute-done((bf16[2,256,256]{2,1,0:T(8,128)(2,1)S(1)}, bf16[2,256,256]{2,1,0:T(8,128)(2,1)S(1)}, u32[]{:S(2)}, u32[]{:S(2)}) %collective-permute-start.5) | collective-permute-done | bytes 262176 | tf_op jit(solution)/shard_map/ppermute | solution.py:27
  117.0 5.3 %collective-permute-done.4 = bf16[2,256,256]{2,1,0:T(8,128)(2,1)S(1)} collective-permute-done((bf16[2,256,256]{2,1,0:T(8,128)(2,1)S(1)}, bf16[2,256,256]{2,1,0:T(8,128)(2,1)S(1)}, u32[]{:S(2)}, u32[]{:S(2)}) %collective-permute-start.4) | collective-permute-done | bytes 262176 | tf_op jit(solution)/shard_map/ppermute | solution.py:25
  124.5 5.0 %fusion.62 = (f32[]{:T(128)}, f32[2]{0:T(128)S(1)}, f32[]{:T(128)}, f32[2,256,256,1]{2,1,3,0:T(8,128)}) fusion(bf16[2,256,256]{2,1,0:T(8,128)(2,1)S(1)} %fusion.76, bf16[8,2,256,256]{3,2,1,0:T(8,128)(2,1)S(1)} %copy-done, bf16[8,2,256,256]{3,2,1,0:T(8,128)(2,1)} %bitcast.85, bf16[8,2,256,256]{3,2,1,0:T(8,128)(2,1)} %param.7), kind=kOutput, calls=%fused_computation.67 | convolution fusion | flops 1075576832 | bytes 7077904 | tf_op jit(solution)/shard_map/tbij,tbjk->bik/dot_general | solution.py:263
  132.6 22.2 %shard_map.79 = (f32[8,64,256]{2,1,0:T(8,128)}, f32[8,128]{1,0:T(8,128)}) custom-call(f32[8,64,256]{2,1,0:T(8,128)} %bitcast.91, f32[8,128]{1,0:T(8,128)} %broadcast_select_fusion.1.t_ref), custom_call_target="tpu_custom_call" | custom-call | tf_op jit(solution)/shard_map/pallas_call | solution.py:210
  159.5 3.0 %collective-permute-start.7 = (bf16[2,256,256]{2,1,0:T(8,128)(2,1)S(1)}, bf16[2,256,256]{2,1,0:T(8,128)(2,1)S(1)}, u32[]{:S(2)}, u32[]{:S(2)}) collective-permute-start(bf16[2,256,256]{2,1,0:T(8,128)(2,1)S(1)} %fusion.82), channel_id=1, source_target_pairs={{8,0},{16,8},{24,16},{32,24},{40,32},{48,40},{56,48},{64,56},{72,6... | collective-permute-start | bytes 786440 | tf_op jit(solution)/shard_map/ppermute | solution.py:27
  162.6 5.8 %collective-permute-done.7 = bf16[2,256,256]{2,1,0:T(8,128)(2,1)S(1)} collective-permute-done((bf16[2,256,256]{2,1,0:T(8,128)(2,1)S(1)}, bf16[2,256,256]{2,1,0:T(8,128)(2,1)S(1)}, u32[]{:S(2)}, u32[]{:S(2)}) %collective-permute-start.7) | collective-permute-done | bytes 262176 | tf_op jit(solution)/shard_map/ppermute | solution.py:27
  168.3 5.3 %collective-permute-done.6 = bf16[2,256,256]{2,1,0:T(8,128)(2,1)S(1)} collective-permute-done((bf16[2,256,256]{2,1,0:T(8,128)(2,1)S(1)}, bf16[2,256,256]{2,1,0:T(8,128)(2,1)S(1)}, u32[]{:S(2)}, u32[]{:S(2)}) %collective-permute-start.6) | collective-permute-done | bytes 262176 | tf_op jit(solution)/shard_map/ppermute | solution.py:25
  175.8 5.0 %fusion.64 = (f32[]{:T(128)}, f32[2]{0:T(128)S(1)}, f32[]{:T(128)}, f32[2,256,256,1]{2,1,3,0:T(8,128)}) fusion(bf16[2,256,256]{2,1,0:T(8,128)(2,1)S(1)} %fusion.82, bf16[8,2,256,256]{3,2,1,0:T(8,128)(2,1)S(1)} %copy-done, bf16[8,2,256,256]{3,2,1,0:T(8,128)(2,1)} %bitcast.82, bf16[8,2,256,256]{3,2,1,0:T(8,128)(2,1)} %param.7), kind=kOutput, calls=%fused_computation.69 | convolution fusion | flops 1075576832 | bytes 7077904 | tf_op jit(solution)/shard_map/tbij,tbjk->bik/dot_general | solution.py:263
  184.0 22.1 %shard_map.80 = (f32[8,64,256]{2,1,0:T(8,128)}, f32[8,128]{1,0:T(8,128)}) custom-call(f32[8,64,256]{2,1,0:T(8,128)} %bitcast.88, f32[8,128]{1,0:T(8,128)} %broadcast_select_fusion.t_ref), custom_call_target="tpu_custom_call" | custom-call | tf_op jit(solution)/shard_map/pallas_call | solution.py:210
  211.9 16.4 %shard_map.81 = f32[8,128]{1,0:T(8,128)} custom-call(f32[8,128]{1,0:T(8,128)} %iota.60.x_ref), custom_call_target="tpu_custom_call" | custom-call | tf_op jit(solution)/shard_map/pallas_call | solution.py:85
  231.5 4.3 %fusion.40 = bf16[8,2,256,256]{2,3,0,1:T(8,128)(2,1)} fusion(bf16[8,2,256,256]{3,2,1,0:T(8,128)(2,1)} %param.7, bf16[2,256,256]{2,1,0:T(8,128)(2,1)S(1)} %multiply_convert_fusion.1, bf16[2,256]{1,0:T(2,128)(2,1)S(1)} %compare_convert_fusion), kind=kOutput, calls=%fused_computation.28 | convolution fusion | flops 1077542912 | bytes 4457472 | tf_op jit(solution)/shard_map/bji,tbjk->tbik/dot_general | solution.py:294
  236.2 48.7 %collective-permute-done.8 = bf16[8,2,256,256]{2,3,0,1:T(8,128)(2,1)} collective-permute-done((bf16[8,2,256,256]{2,3,0,1:T(8,128)(2,1)}, bf16[8,2,256,256]{2,3,0,1:T(8,128)(2,1)}, u32[]{:S(2)}, u32[]{:S(2)}) %collective-permute-start.8) | collective-permute-done | bytes 2097184 | tf_op jit(solution)/shard_map/ppermute | solution.py:245
  284.9 3.9 %copy.19 = bf16[8,2,256,256]{3,2,1,0:T(8,128)(2,1)} copy(bf16[8,2,256,256]{2,3,0,1:T(8,128)(2,1)} %collective-permute-done.8) | data formatting | bytes 4194304
  (53 shorter events, 29.5 us)
Async XLA Ops:
  0.6 18.0 %copy-start = (bf16[8,2,256,256]{3,2,1,0:T(8,128)(2,1)S(1)}, bf16[8,2,256,256]{3,2,1,0:T(8,128)(2,1)}, u32[]{:S(2)}) copy-start(bf16[8,2,256,256]{3,2,1,0:T(8,128)(2,1)} %param.8) | copy-start | bytes 6291460
  0.6 14.9 %collective-permute-start = (bf16[2,256,256]{2,1,0:T(8,128)(2,1)}, bf16[2,256,256]{2,1,0:T(8,128)(2,1)S(1)}, u32[]{:S(2)}, u32[]{:S(2)}) collective-permute-start(bf16[2,256,256]{2,1,0:T(8,128)(2,1)} %param.6), channel_id=1, source_target_pairs={{0,8},{8,16},{16,24},{24,32},{32,40},{40,48},{48,56},{56,64},{64,7... | collective-permute-start | bytes 786440 | tf_op jit(solution)/shard_map/ppermute | solution.py:25
  3.2 12.4 %collective-permute-start.1 = (bf16[2,256,256]{2,1,0:T(8,128)(2,1)}, bf16[2,256,256]{2,1,0:T(8,128)(2,1)S(1)}, u32[]{:S(2)}, u32[]{:S(2)}) collective-permute-start(bf16[2,256,256]{2,1,0:T(8,128)(2,1)} %param.6), channel_id=1, source_target_pairs={{8,0},{16,8},{24,16},{32,24},{40,32},{48,40},{56,48},{64,56},{72,6... | collective-permute-start | bytes 786440 | tf_op jit(solution)/shard_map/ppermute | solution.py:27
  16.6 2.0 copy-start.1
  18.6 5.0 %copy-start.3 = (f32[2]{0:T(128)S(1)}, f32[2]{0:T(128)}, u32[]{:S(2)}) copy-start(f32[2]{0:T(128)} %param.9) | copy-start | bytes 28
  57.0 8.8 %collective-permute-start.3 = (bf16[2,256,256]{2,1,0:T(8,128)(2,1)S(1)}, bf16[2,256,256]{2,1,0:T(8,128)(2,1)S(1)}, u32[]{:S(2)}, u32[]{:S(2)}) collective-permute-start(bf16[2,256,256]{2,1,0:T(8,128)(2,1)S(1)} %fusion.70), channel_id=1, source_target_pairs={{8,0},{16,8},{24,16},{32,24},{40,32},{48,40},{56,48},{64,56},{72,6... | collective-permute-start | bytes 786440 | tf_op jit(solution)/shard_map/ppermute | solution.py:27
  60.6 10.4 %collective-permute-start.2 = (bf16[2,256,256]{2,1,0:T(8,128)(2,1)S(1)}, bf16[2,256,256]{2,1,0:T(8,128)(2,1)S(1)}, u32[]{:S(2)}, u32[]{:S(2)}) collective-permute-start(bf16[2,256,256]{2,1,0:T(8,128)(2,1)S(1)} %fusion.70), channel_id=1, source_target_pairs={{0,8},{8,16},{16,24},{24,32},{32,40},{40,48},{48,56},{56,64},{64,7... | collective-permute-start | bytes 786440 | tf_op jit(solution)/shard_map/ppermute | solution.py:25
  108.6 8.5 %collective-permute-start.5 = (bf16[2,256,256]{2,1,0:T(8,128)(2,1)S(1)}, bf16[2,256,256]{2,1,0:T(8,128)(2,1)S(1)}, u32[]{:S(2)}, u32[]{:S(2)}) collective-permute-start(bf16[2,256,256]{2,1,0:T(8,128)(2,1)S(1)} %fusion.76), channel_id=1, source_target_pairs={{8,0},{16,8},{24,16},{32,24},{40,32},{48,40},{56,48},{64,56},{72,6... | collective-permute-start | bytes 786440 | tf_op jit(solution)/shard_map/ppermute | solution.py:27
  111.2 11.2 %collective-permute-start.4 = (bf16[2,256,256]{2,1,0:T(8,128)(2,1)S(1)}, bf16[2,256,256]{2,1,0:T(8,128)(2,1)S(1)}, u32[]{:S(2)}, u32[]{:S(2)}) collective-permute-start(bf16[2,256,256]{2,1,0:T(8,128)(2,1)S(1)} %fusion.76), channel_id=1, source_target_pairs={{0,8},{8,16},{16,24},{24,32},{32,40},{40,48},{48,56},{56,64},{64,7... | collective-permute-start | bytes 786440 | tf_op jit(solution)/shard_map/ppermute | solution.py:25
  124.5 38.0 %copy-start.4 = (s32[2]{0:T(128)S(1)}, s32[2]{0:T(128)}, u32[]{:S(2)}) copy-start(s32[2]{0:T(128)} %param.11) | copy-start | bytes 28
  159.5 8.9 %collective-permute-start.7 = (bf16[2,256,256]{2,1,0:T(8,128)(2,1)S(1)}, bf16[2,256,256]{2,1,0:T(8,128)(2,1)S(1)}, u32[]{:S(2)}, u32[]{:S(2)}) collective-permute-start(bf16[2,256,256]{2,1,0:T(8,128)(2,1)S(1)} %fusion.82), channel_id=1, source_target_pairs={{8,0},{16,8},{24,16},{32,24},{40,32},{48,40},{56,48},{64,56},{72,6... | collective-permute-start | bytes 786440 | tf_op jit(solution)/shard_map/ppermute | solution.py:27
  162.5 11.2 %collective-permute-start.6 = (bf16[2,256,256]{2,1,0:T(8,128)(2,1)S(1)}, bf16[2,256,256]{2,1,0:T(8,128)(2,1)S(1)}, u32[]{:S(2)}, u32[]{:S(2)}) collective-permute-start(bf16[2,256,256]{2,1,0:T(8,128)(2,1)S(1)} %fusion.82), channel_id=1, source_target_pairs={{0,8},{8,16},{16,24},{24,32},{32,40},{40,48},{48,56},{56,64},{64,7... | collective-permute-start | bytes 786440 | tf_op jit(solution)/shard_map/ppermute | solution.py:25
  231.5 4.3 %copy-start.2 = (bf16[2,256,256]{2,1,0:T(8,128)(2,1)}, bf16[2,256,256]{2,1,0:T(8,128)(2,1)S(1)}, u32[]{:S(2)}) copy-start(bf16[2,256,256]{2,1,0:T(8,128)(2,1)S(1)} %multiply_convert_fusion.1) | copy-start | bytes 786436
  235.8 49.1 %collective-permute-start.8 = (bf16[8,2,256,256]{2,3,0,1:T(8,128)(2,1)}, bf16[8,2,256,256]{2,3,0,1:T(8,128)(2,1)}, u32[]{:S(2)}, u32[]{:S(2)}) collective-permute-start(bf16[8,2,256,256]{2,3,0,1:T(8,128)(2,1)} %fusion.40), channel_id=1, source_target_pairs={{248,0},{0,8},{8,16},{16,24},{24,32},{32,40},{40,48},{48,56},{56,6... | collective-permute-start | bytes 6291464 | tf_op jit(solution)/shard_map/ppermute | solution.py:245

commit v4 on v3

--- a/solution.py
+++ b/solution.py
@@ -253,6 +253,8 @@
     first_op = lax.axis_index("op") == 0
     n_sec = lax.axis_size("sec")
     n_op = lax.axis_size("op")
+    left_prev = shifted(left_ops, "sec", 1)
+    kept_prev = shifted(kept, "sec", 1)
     state = state_start
     for iteration in range(ITERS):
         window = padded(state, (("sec", 0),), sector_local)
@@ -284,17 +286,16 @@
             factor = jnp.sqrt(count / new_norm)
         state = (updated * factor).astype(jnp.bfloat16)
     columns = jnp.arange(width, dtype=jnp.int32)
-    keep_mask = (columns[None, :] < kept[:, None]).astype(jnp.bfloat16)
-    kept_block = state * keep_mask[:, None, :]
+    keep_mask = (columns[None, :] < kept_prev[:, None]).astype(jnp.bfloat16)
+    kept_block = shifted(state, "sec", 1) * keep_mask[:, None, :]
     out_scale = 1.0 / float(width) ** 0.5
     projected = jnp.einsum(
-        "tbij,bjk->tbik", left_ops, kept_block, preferred_element_type=jnp.float32
+        "tbij,bjk->tbik", left_prev, kept_block, preferred_element_type=jnp.float32
     ).astype(jnp.bfloat16)
-    renormed = (
+    new_ops = (
         jnp.einsum("bji,tbjk->tbik", kept_block, projected, preferred_element_type=jnp.float32)
         * out_scale
     ).astype(jnp.bfloat16)
-    new_ops = shifted(renormed, "sec", 1)
     return (state, new_ops)
 
 

time: 290 us -> 268 us (0.924)
  waiting for transfers between devices: 86.7 us -> 45.6 us
  Pallas kernels: 109 us -> 126 us
    ppermute x1 -> x3, waiting for transfers between devices: 48.7 us -> 7.45 us  [shifted(): return lax.ppermute(block, axis, route)]
    pallas_call x4, Pallas kernels: 92.5 us -> 110 us  [sigma_sum(): pl.pallas_call(functools.partial(sigma_sum_kernel, n_sec, n_op), out_shap...]
  transfers between devices with their start and end apart: 9 -> 11, of which waited for: 8 -> 8; matrix products, arithmetic and copies ran while one was open for 0% -> 6% of each run, Pallas kernels for 0% -> 21%
where the time goes in v4:
time: 268 us; the launch traced here: 266 us
  Pallas kernels  126 us (47%)
  waiting for transfers between devices  45.6 us (17%)
  matrix products  24 us (9%)
  starting transfers between devices  20.2 us (8%)
  local copies, waits for them, and re-layouts  19.2 us (7%)
  between operations  17.6 us (7%)
  other arithmetic  13.7 us (5%)
    pallas_call x4, Pallas kernels, sigma_sum(): pl.pallas_call(functools.partial(sigma_sum_kernel, n_sec, n_op), out_shap...  110 us
    ppermute x4, waiting for transfers between devices, padded(): lax.ppermute(tail, axis, [(i, (i + 1) % count) for i in range(count)])  21.2 us
    dot_general x4, matrix products, per_device(): jnp.einsum('tbij,tbjk->bik', halfway, right_ops, preferred_element_type=j...  19.8 us
    ppermute x4, waiting for transfers between devices, padded(): lax.ppermute(head, axis, [((i + 1) % count, i) for i in range(count)])  16.9 us
    pallas_call x1, Pallas kernels, all_sum(): pl.pallas_call(functools.partial(all_sum_kernel, n_sec, n_op), out_shape=...  16.4 us
    ppermute x4, starting transfers between devices, padded(): lax.ppermute(head, axis, [((i + 1) % count, i) for i in range(count)])  15.4 us
    gather x4, local copies, waits for them, and re-layouts, per_device(): sources = window[partner]  8 us
    ppermute x3, waiting for transfers between devices, shifted(): return lax.ppermute(block, axis, route)  7.45 us
  transfers between devices with their start and end apart: 11, of which 8 were waited for; matrix products, arithmetic and copies ran while one was open for 6% of the time, Pallas kernels for 21%

profile of v4, /device:TPU:1, one launch (start us, length us, event | category | flops | bytes accessed | tf_op | source)
XLA Modules:
  0.0 266.5 jit_solution(13575042160889330050)
XLA Ops:
  0.6 2.5 collective-permute-start
  3.2 6.2 %collective-permute-start.1 = (bf16[2,256,256]{2,1,0:T(8,128)(2,1)}, bf16[2,256,256]{2,1,0:T(8,128)(2,1)S(1)}, u32[]{:S(2)}, u32[]{:S(2)}) collective-permute-start(bf16[2,256,256]{2,1,0:T(8,128)(2,1)} %param.6), channel_id=1, source_target_pairs={{8,0},{16,8},{24,16},{32,24},{40,32},{48,40},{56,48},{64,56},{72,6... | collective-permute-start | bytes 786440 | tf_op jit(solution)/shard_map/ppermute | solution.py:27
  10.3 5.3 %collective-permute-done = bf16[2,256,256]{2,1,0:T(8,128)(2,1)S(1)} collective-permute-done((bf16[2,256,256]{2,1,0:T(8,128)(2,1)}, bf16[2,256,256]{2,1,0:T(8,128)(2,1)S(1)}, u32[]{:S(2)}, u32[]{:S(2)}) %collective-permute-start) | collective-permute-done | bytes 262176 | tf_op jit(solution)/shard_map/ppermute | solution.py:25
  18.6 5.0 %fusion.62 = (f32[]{:T(128)}, f32[2]{0:T(128)S(1)}, f32[]{:T(128)}, f32[2,256,256,1]{2,1,3,0:T(8,128)}) fusion(bf16[2,256,256]{2,1,0:T(8,128)(2,1)S(1)} %copy-done.1, bf16[8,2,256,256]{3,2,1,0:T(8,128)(2,1)S(1)} %copy-done, bf16[8,2,256,256]{3,2,1,0:T(8,128)(2,1)} %bitcast.83, bf16[8,2,256,256]{3,2,1,0:T(8,128)(2,1)} %param.7), kind=kOutput, calls=%fused_computation.63 | convolution fusion | flops 1075576832 | bytes 7077904 | tf_op jit(solution)/shard_map/tbij,tbjk->bik/dot_general | solution.py:265
  26.8 25.6 %shard_map.77 = (f32[8,64,256]{2,1,0:T(8,128)}, f32[8,128]{1,0:T(8,128)}) custom-call(f32[8,64,256]{2,1,0:T(8,128)} %bitcast.89, f32[8,128]{1,0:T(8,128)} %broadcast_select_fusion.3.t_ref), custom_call_target="tpu_custom_call" | custom-call | tf_op jit(solution)/shard_map/pallas_call | solution.py:210
  57.0 3.6 %collective-permute-start.3 = (bf16[2,256,256]{2,1,0:T(8,128)(2,1)S(1)}, bf16[2,256,256]{2,1,0:T(8,128)(2,1)S(1)}, u32[]{:S(2)}, u32[]{:S(2)}) collective-permute-start(bf16[2,256,256]{2,1,0:T(8,128)(2,1)S(1)} %fusion.74), channel_id=1, source_target_pairs={{8,0},{16,8},{24,16},{32,24},{40,32},{48,40},{56,48},{64,56},{72,6... | collective-permute-start | bytes 786440 | tf_op jit(solution)/shard_map/ppermute | solution.py:27
  60.6 5.2 %collective-permute-done.3 = bf16[2,256,256]{2,1,0:T(8,128)(2,1)S(1)} collective-permute-done((bf16[2,256,256]{2,1,0:T(8,128)(2,1)S(1)}, bf16[2,256,256]{2,1,0:T(8,128)(2,1)S(1)}, u32[]{:S(2)}, u32[]{:S(2)}) %collective-permute-start.3) | collective-permute-done | bytes 262176 | tf_op jit(solution)/shard_map/ppermute | solution.py:27
  65.8 5.2 %collective-permute-done.2 = bf16[2,256,256]{2,1,0:T(8,128)(2,1)S(1)} collective-permute-done((bf16[2,256,256]{2,1,0:T(8,128)(2,1)S(1)}, bf16[2,256,256]{2,1,0:T(8,128)(2,1)S(1)}, u32[]{:S(2)}, u32[]{:S(2)}) %collective-permute-start.2) | collective-permute-done | bytes 262176 | tf_op jit(solution)/shard_map/ppermute | solution.py:25
  73.1 5.0 %fusion.64 = (f32[]{:T(128)}, f32[2]{0:T(128)S(1)}, f32[]{:T(128)}, f32[2,256,256,1]{2,1,3,0:T(8,128)}) fusion(bf16[2,256,256]{2,1,0:T(8,128)(2,1)S(1)} %fusion.74, bf16[8,2,256,256]{3,2,1,0:T(8,128)(2,1)S(1)} %copy-done, bf16[8,2,256,256]{3,2,1,0:T(8,128)(2,1)} %bitcast.84, bf16[8,2,256,256]{3,2,1,0:T(8,128)(2,1)} %param.7), kind=kOutput, calls=%fused_computation.65 | convolution fusion | flops 1075576832 | bytes 7077904 | tf_op jit(solution)/shard_map/tbij,tbjk->bik/dot_general | solution.py:265
  81.3 22.6 %shard_map.78 = (f32[8,64,256]{2,1,0:T(8,128)}, f32[8,128]{1,0:T(8,128)}) custom-call(f32[8,64,256]{2,1,0:T(8,128)} %bitcast.90, f32[8,128]{1,0:T(8,128)} %broadcast_select_fusion.2.t_ref), custom_call_target="tpu_custom_call" | custom-call | tf_op jit(solution)/shard_map/pallas_call | solution.py:210
  108.6 2.6 collective-permute-start.5
  111.2 5.9 %collective-permute-done.5 = bf16[2,256,256]{2,1,0:T(8,128)(2,1)S(1)} collective-permute-done((bf16[2,256,256]{2,1,0:T(8,128)(2,1)S(1)}, bf16[2,256,256]{2,1,0:T(8,128)(2,1)S(1)}, u32[]{:S(2)}, u32[]{:S(2)}) %collective-permute-start.5) | collective-permute-done | bytes 262176 | tf_op jit(solution)/shard_map/ppermute | solution.py:27
  117.0 5.3 %collective-permute-done.4 = bf16[2,256,256]{2,1,0:T(8,128)(2,1)S(1)} collective-permute-done((bf16[2,256,256]{2,1,0:T(8,128)(2,1)S(1)}, bf16[2,256,256]{2,1,0:T(8,128)(2,1)S(1)}, u32[]{:S(2)}, u32[]{:S(2)}) %collective-permute-start.4) | collective-permute-done | bytes 262176 | tf_op jit(solution)/shard_map/ppermute | solution.py:25
  124.5 5.0 %fusion.66 = (f32[]{:T(128)}, f32[2]{0:T(128)S(1)}, f32[]{:T(128)}, f32[2,256,256,1]{2,1,3,0:T(8,128)}) fusion(bf16[2,256,256]{2,1,0:T(8,128)(2,1)S(1)} %fusion.80, bf16[8,2,256,256]{3,2,1,0:T(8,128)(2,1)S(1)} %copy-done, bf16[8,2,256,256]{3,2,1,0:T(8,128)(2,1)} %bitcast.85, bf16[8,2,256,256]{3,2,1,0:T(8,128)(2,1)} %param.7), kind=kOutput, calls=%fused_computation.67 | convolution fusion | flops 1075576832 | bytes 7077904 | tf_op jit(solution)/shard_map/tbij,tbjk->bik/dot_general | solution.py:265
  132.6 22.2 %shard_map.79 = (f32[8,64,256]{2,1,0:T(8,128)}, f32[8,128]{1,0:T(8,128)}) custom-call(f32[8,64,256]{2,1,0:T(8,128)} %bitcast.91, f32[8,128]{1,0:T(8,128)} %broadcast_select_fusion.1.t_ref), custom_call_target="tpu_custom_call" | custom-call | tf_op jit(solution)/shard_map/pallas_call | solution.py:210
  159.4 3.0 %collective-permute-start.7 = (bf16[2,256,256]{2,1,0:T(8,128)(2,1)S(1)}, bf16[2,256,256]{2,1,0:T(8,128)(2,1)S(1)}, u32[]{:S(2)}, u32[]{:S(2)}) collective-permute-start(bf16[2,256,256]{2,1,0:T(8,128)(2,1)S(1)} %fusion.86), channel_id=1, source_target_pairs={{8,0},{16,8},{24,16},{32,24},{40,32},{48,40},{56,48},{64,56},{72,6... | collective-permute-start | bytes 786440 | tf_op jit(solution)/shard_map/ppermute | solution.py:27
  162.5 5.9 %collective-permute-done.7 = bf16[2,256,256]{2,1,0:T(8,128)(2,1)S(1)} collective-permute-done((bf16[2,256,256]{2,1,0:T(8,128)(2,1)S(1)}, bf16[2,256,256]{2,1,0:T(8,128)(2,1)S(1)}, u32[]{:S(2)}, u32[]{:S(2)}) %collective-permute-start.7) | collective-permute-done | bytes 262176 | tf_op jit(solution)/shard_map/ppermute | solution.py:27
  168.3 5.4 %collective-permute-done.6 = bf16[2,256,256]{2,1,0:T(8,128)(2,1)S(1)} collective-permute-done((bf16[2,256,256]{2,1,0:T(8,128)(2,1)S(1)}, bf16[2,256,256]{2,1,0:T(8,128)(2,1)S(1)}, u32[]{:S(2)}, u32[]{:S(2)}) %collective-permute-start.6) | collective-permute-done | bytes 262176 | tf_op jit(solution)/shard_map/ppermute | solution.py:25
  175.8 4.9 %fusion.68 = (f32[]{:T(128)}, f32[2]{0:T(128)S(1)}, f32[]{:T(128)}, f32[2,256,256,1]{2,1,3,0:T(8,128)}) fusion(bf16[2,256,256]{2,1,0:T(8,128)(2,1)S(1)} %fusion.86, bf16[8,2,256,256]{3,2,1,0:T(8,128)(2,1)S(1)} %copy-done, bf16[8,2,256,256]{3,2,1,0:T(8,128)(2,1)} %bitcast.82, bf16[8,2,256,256]{3,2,1,0:T(8,128)(2,1)} %param.7), kind=kOutput, calls=%fused_computation.69 | convolution fusion | flops 1075576832 | bytes 7077904 | tf_op jit(solution)/shard_map/tbij,tbjk->bik/dot_general | solution.py:265
  183.9 39.4 %shard_map.80 = (f32[8,64,256]{2,1,0:T(8,128)}, f32[8,128]{1,0:T(8,128)}) custom-call(f32[8,64,256]{2,1,0:T(8,128)} %bitcast.88, f32[8,128]{1,0:T(8,128)} %broadcast_select_fusion.t_ref), custom_call_target="tpu_custom_call" | custom-call | tf_op jit(solution)/shard_map/pallas_call | solution.py:210
  229.1 16.4 %shard_map.81 = f32[8,128]{1,0:T(8,128)} custom-call(f32[8,128]{1,0:T(8,128)} %iota.60.x_ref), custom_call_target="tpu_custom_call" | custom-call | tf_op jit(solution)/shard_map/pallas_call | solution.py:85
  250.9 7.4 %collective-permute-done.9 = s32[2]{0:T(128)S(1)} collective-permute-done((s32[2]{0:T(128)S(1)}, s32[2]{0:T(128)S(1)}, u32[]{:S(2)}, u32[]{:S(2)}) %collective-permute-start.9) | collective-permute-done | bytes 40 | tf_op jit(solution)/shard_map/ppermute | solution.py:245
  258.4 4.2 %fusion.44 = bf16[8,2,256,256]{2,3,0,1:T(8,128)(2,1)} fusion(bf16[8,2,256,256]{3,2,1,0:T(8,128)(2,1)} %collective-permute-done.10, bf16[2,256,256]{2,1,0:T(8,128)(2,1)S(1)} %collective-permute-done.8, bf16[2,256]{1,0:T(2,128)(2,1)S(1)} %compare_convert_fusion), kind=kOutput, calls=%fused_computation.29 | convolution fusion | flops 1077542912 | bytes 4457472 | tf_op jit(solution)/shard_map/bji,tbjk->tbik/dot_general | solution.py:296
  262.6 3.9 %copy.19 = bf16[8,2,256,256]{3,2,1,0:T(8,128)(2,1)} copy(bf16[8,2,256,256]{2,3,0,1:T(8,128)(2,1)} %fusion.44) | data formatting | bytes 4194304
  (57 shorter events, 31.3 us)
Async XLA Ops:
  0.6 18.0 %copy-start = (bf16[8,2,256,256]{3,2,1,0:T(8,128)(2,1)S(1)}, bf16[8,2,256,256]{3,2,1,0:T(8,128)(2,1)}, u32[]{:S(2)}) copy-start(bf16[8,2,256,256]{3,2,1,0:T(8,128)(2,1)} %param.8) | copy-start | bytes 6291460
  0.6 14.9 %collective-permute-start = (bf16[2,256,256]{2,1,0:T(8,128)(2,1)}, bf16[2,256,256]{2,1,0:T(8,128)(2,1)S(1)}, u32[]{:S(2)}, u32[]{:S(2)}) collective-permute-start(bf16[2,256,256]{2,1,0:T(8,128)(2,1)} %param.6), channel_id=1, source_target_pairs={{0,8},{8,16},{16,24},{24,32},{32,40},{40,48},{48,56},{56,64},{64,7... | collective-permute-start | bytes 786440 | tf_op jit(solution)/shard_map/ppermute | solution.py:25
  3.2 12.4 %collective-permute-start.1 = (bf16[2,256,256]{2,1,0:T(8,128)(2,1)}, bf16[2,256,256]{2,1,0:T(8,128)(2,1)S(1)}, u32[]{:S(2)}, u32[]{:S(2)}) collective-permute-start(bf16[2,256,256]{2,1,0:T(8,128)(2,1)} %param.6), channel_id=1, source_target_pairs={{8,0},{16,8},{24,16},{32,24},{40,32},{48,40},{56,48},{64,56},{72,6... | collective-permute-start | bytes 786440 | tf_op jit(solution)/shard_map/ppermute | solution.py:27
  16.6 2.0 copy-start.1
  18.6 5.0 %copy-start.3 = (f32[2]{0:T(128)S(1)}, f32[2]{0:T(128)}, u32[]{:S(2)}) copy-start(f32[2]{0:T(128)} %param.9) | copy-start | bytes 28
  57.0 8.8 %collective-permute-start.3 = (bf16[2,256,256]{2,1,0:T(8,128)(2,1)S(1)}, bf16[2,256,256]{2,1,0:T(8,128)(2,1)S(1)}, u32[]{:S(2)}, u32[]{:S(2)}) collective-permute-start(bf16[2,256,256]{2,1,0:T(8,128)(2,1)S(1)} %fusion.74), channel_id=1, source_target_pairs={{8,0},{16,8},{24,16},{32,24},{40,32},{48,40},{56,48},{64,56},{72,6... | collective-permute-start | bytes 786440 | tf_op jit(solution)/shard_map/ppermute | solution.py:27
  60.6 10.4 %collective-permute-start.2 = (bf16[2,256,256]{2,1,0:T(8,128)(2,1)S(1)}, bf16[2,256,256]{2,1,0:T(8,128)(2,1)S(1)}, u32[]{:S(2)}, u32[]{:S(2)}) collective-permute-start(bf16[2,256,256]{2,1,0:T(8,128)(2,1)S(1)} %fusion.74), channel_id=1, source_target_pairs={{0,8},{8,16},{16,24},{24,32},{32,40},{40,48},{48,56},{56,64},{64,7... | collective-permute-start | bytes 786440 | tf_op jit(solution)/shard_map/ppermute | solution.py:25
  108.6 8.5 %collective-permute-start.5 = (bf16[2,256,256]{2,1,0:T(8,128)(2,1)S(1)}, bf16[2,256,256]{2,1,0:T(8,128)(2,1)S(1)}, u32[]{:S(2)}, u32[]{:S(2)}) collective-permute-start(bf16[2,256,256]{2,1,0:T(8,128)(2,1)S(1)} %fusion.80), channel_id=1, source_target_pairs={{8,0},{16,8},{24,16},{32,24},{40,32},{48,40},{56,48},{64,56},{72,6... | collective-permute-start | bytes 786440 | tf_op jit(solution)/shard_map/ppermute | solution.py:27
  111.2 11.2 %collective-permute-start.4 = (bf16[2,256,256]{2,1,0:T(8,128)(2,1)S(1)}, bf16[2,256,256]{2,1,0:T(8,128)(2,1)S(1)}, u32[]{:S(2)}, u32[]{:S(2)}) collective-permute-start(bf16[2,256,256]{2,1,0:T(8,128)(2,1)S(1)} %fusion.80), channel_id=1, source_target_pairs={{0,8},{8,16},{16,24},{24,32},{32,40},{40,48},{48,56},{56,64},{64,7... | collective-permute-start | bytes 786440 | tf_op jit(solution)/shard_map/ppermute | solution.py:25
  159.4 8.9 %collective-permute-start.7 = (bf16[2,256,256]{2,1,0:T(8,128)(2,1)S(1)}, bf16[2,256,256]{2,1,0:T(8,128)(2,1)S(1)}, u32[]{:S(2)}, u32[]{:S(2)}) collective-permute-start(bf16[2,256,256]{2,1,0:T(8,128)(2,1)S(1)} %fusion.86), channel_id=1, source_target_pairs={{8,0},{16,8},{24,16},{32,24},{40,32},{48,40},{56,48},{64,56},{72,6... | collective-permute-start | bytes 786440 | tf_op jit(solution)/shard_map/ppermute | solution.py:27
  162.5 11.2 %collective-permute-start.6 = (bf16[2,256,256]{2,1,0:T(8,128)(2,1)S(1)}, bf16[2,256,256]{2,1,0:T(8,128)(2,1)S(1)}, u32[]{:S(2)}, u32[]{:S(2)}) collective-permute-start(bf16[2,256,256]{2,1,0:T(8,128)(2,1)S(1)} %fusion.86), channel_id=1, source_target_pairs={{0,8},{8,16},{16,24},{24,32},{32,40},{40,48},{48,56},{56,64},{64,7... | collective-permute-start | bytes 786440 | tf_op jit(solution)/shard_map/ppermute | solution.py:25
  162.5 95.9 %collective-permute-start.10 = (bf16[8,2,256,256]{3,2,1,0:T(8,128)(2,1)}, bf16[8,2,256,256]{3,2,1,0:T(8,128)(2,1)}, u32[]{:S(2)}, u32[]{:S(2)}) collective-permute-start(bf16[8,2,256,256]{3,2,1,0:T(8,128)(2,1)} %param.7), channel_id=1, source_target_pairs={{248,0},{0,8},{8,16},{16,24},{24,32},{32,40},{40,48},{48,56},{56,6... | collective-permute-start | bytes 6291464 | tf_op jit(solution)/shard_map/ppermute | solution.py:245
  180.7 68.8 %copy-start.4 = (s32[2]{0:T(128)S(1)}, s32[2]{0:T(128)}, u32[]{:S(2)}) copy-start(s32[2]{0:T(128)} %param.11) | copy-start | bytes 28
  248.6 14.0 %copy-start.2 = (bf16[2,256,256]{2,1,0:T(8,128)(2,1)}, bf16[2,256,256]{2,1,0:T(8,128)(2,1)S(1)}, u32[]{:S(2)}) copy-start(bf16[2,256,256]{2,1,0:T(8,128)(2,1)S(1)} %multiply_convert_fusion.1) | copy-start | bytes 786436
  248.6 9.8 %collective-permute-start.8 = (bf16[2,256,256]{2,1,0:T(8,128)(2,1)S(1)}, bf16[2,256,256]{2,1,0:T(8,128)(2,1)S(1)}, u32[]{:S(2)}, u32[]{:S(2)}) collective-permute-start(bf16[2,256,256]{2,1,0:T(8,128)(2,1)S(1)} %multiply_convert_fusion.1), channel_id=1, source_target_pairs={{248,0},{0,8},{8,16},{16,24},{24,32},{32,40},{40,48},{48,56},{56,6... | collective-permute-start | bytes 786440 | tf_op jit(solution)/shard_map/ppermute | solution.py:245
  249.5 8.8 %collective-permute-start.9 = (s32[2]{0:T(128)S(1)}, s32[2]{0:T(128)S(1)}, u32[]{:S(2)}, u32[]{:S(2)}) collective-permute-start(s32[2]{0:T(128)S(1)} %copy-done.4), channel_id=1, source_target_pairs={{248,0},{0,8},{8,16},{16,24},{24,32},{32,40},{40,48},{48,56},{56,6... | collective-permute-start | bytes 32 | tf_op jit(solution)/shard_map/ppermute | solution.py:245

commit v5 on v4

--- a/solution.py
+++ b/solution.py
@@ -239,6 +239,215 @@
     return total.reshape(shape), tuple(sums[0, k] for k in range(len(values)))
 
 
+def step_kernel(n_sec, n_op, count, final, x_ref, st_ref, sh_ref, t_ref, *refs):
+    if final:
+        (win_ref, rs_buf, red, op_buf, sec_buf, mid, mid_out, op_buf2, sec_buf2,
+         mid2, mid2_out, mid3, mid3_out, new_buf, new_out, win_buf, send_rs, recv_rs, send_a,
+         recv_a, send_b, recv_b, send_a2, recv_a2, send_b2, recv_b2, send_w,
+         recv_w, local_sem) = refs
+    else:
+        (win_ref, rs_buf, red, op_buf, sec_buf, mid, mid_out, new_buf, new_out,
+         win_buf, send_rs, recv_rs, send_a, recv_a, send_b, recv_b, send_w,
+         recv_w, local_sem) = refs
+    me_sec = lax.axis_index("sec")
+    me_op = lax.axis_index("op")
+    prev_sec = (me_sec + n_sec - 1) % n_sec
+    next_sec = (me_sec + 1) % n_sec
+    barrier = pltpu.get_barrier_semaphore()
+    greeted = 0
+    for d in range(1, n_op):
+        pl.semaphore_signal(barrier, 1, device_id=(me_sec, (me_op + d) % n_op),
+                            device_id_type=MESH)
+        greeted += 1
+    for d in range(1, n_sec):
+        pl.semaphore_signal(barrier, 1, device_id=((me_sec + d) % n_sec, me_op),
+                            device_id_type=MESH)
+        greeted += 1
+    for side in (prev_sec, next_sec):
+        for d in range(1, n_op):
+            pl.semaphore_signal(barrier, 1, device_id=(side, (me_op + d) % n_op),
+                                device_id_type=MESH)
+            greeted += 1
+    pl.semaphore_wait(barrier, greeted)
+
+    def op_peer(j):
+        return (me_sec, j)
+
+    def sec_peer(j):
+        return (j, me_op)
+
+    def copy_to(src, dst, send, recv, peer):
+        return pltpu.make_async_remote_copy(
+            src_ref=src, dst_ref=dst, send_sem=send, recv_sem=recv,
+            device_id=peer, device_id_type=MESH)
+
+    def ordered_sum(buf, n):
+        total = buf[0]
+        for j in range(1, n):
+            total = total + buf[j]
+        return total
+
+    def start_gather(n, me, src, buf, send, recv, peer_of):
+        for d in range(1, n):
+            copy_to(src, buf.at[me], send.at[d], recv.at[me], peer_of((me + d) % n)).start()
+        buf[me] = src[...]
+
+    def wait_gather(n, me, src, buf, send, recv, peer_of):
+        for d in range(1, n):
+            slot = (me + n - d) % n
+            copy_to(src, buf.at[slot], send.at[d], recv.at[slot], peer_of(slot)).wait_recv()
+
+    def drain_gather(n, me, src, buf, send, recv, peer_of):
+        for d in range(1, n):
+            copy_to(src, buf.at[me], send.at[d], recv.at[me], peer_of((me + d) % n)).wait_send()
+
+    def settle(src, dst, sem):
+        local = pltpu.make_async_copy(src, dst, sem)
+        local.start()
+        local.wait()
+
+    def rs_copy(d):
+        j = (me_op + d) % n_op
+        return copy_to(x_ref.at[j], rs_buf.at[me_op], send_rs.at[d], recv_rs.at[me_op], op_peer(j))
+
+    for d in range(1, n_op):
+        rs_copy(d).start()
+    a_args = (n_op, me_op, t_ref, op_buf, send_a, recv_a, op_peer)
+    start_gather(*a_args)
+    rs_buf[me_op] = x_ref[me_op]
+
+    wait_gather(*a_args)
+    mid[...] = ordered_sum(op_buf, n_op)
+    settle(mid, mid_out, local_sem.at[0])
+    b_args = (n_sec, me_sec, mid_out, sec_buf, send_b, recv_b, sec_peer)
+    start_gather(*b_args)
+
+    for d in range(1, n_op):
+        slot = (me_op + n_op - d) % n_op
+        copy_to(x_ref.at[me_op], rs_buf.at[slot], send_rs.at[d], recv_rs.at[slot],
+                op_peer(slot)).wait_recv()
+    red[...] = ordered_sum(rs_buf, n_op)
+
+    wait_gather(*b_args)
+    sums = ordered_sum(sec_buf, n_sec)
+    energy_sum = sums[0:1, 0:1]
+    norm_sum = sums[0:1, 1:2]
+    state_wide = st_ref[me_op].astype(jnp.float32)
+    sigma = red[...] + sh_ref[me_op] * state_wide
+    updated = state_wide - step_size * (sigma - (energy_sum / norm_sum) * state_wide)
+    if final:
+        square = jnp.sum(jnp.sum(updated * updated, axis=1, keepdims=True), axis=0,
+                         keepdims=True)
+        lane = lax.broadcasted_iota(jnp.int32, (8, 128), 1)
+        mid2[...] = jnp.where(lane == 0, square, 0.0)
+        settle(mid2, mid2_out, local_sem.at[1])
+        a2_args = (n_op, me_op, mid2_out, op_buf2, send_a2, recv_a2, op_peer)
+        start_gather(*a2_args)
+        wait_gather(*a2_args)
+        mid3[...] = ordered_sum(op_buf2, n_op)
+        settle(mid3, mid3_out, local_sem.at[3])
+        b2_args = (n_sec, me_sec, mid3_out, sec_buf2, send_b2, recv_b2, sec_peer)
+        start_gather(*b2_args)
+        wait_gather(*b2_args)
+        new_norm = ordered_sum(sec_buf2, n_sec)[0:1, 0:1]
+        factor = jnp.sqrt(count / new_norm)
+    else:
+        factor = jnp.sqrt(count / norm_sum)
+    new_buf[...] = (updated * factor).astype(new_buf.dtype)
+    settle(new_buf, new_out, local_sem.at[2])
+
+    sides = ((next_sec, 0),) if final else ((next_sec, 0), (prev_sec, 2 * n_op))
+    sent = 0
+    for side, base in sides:
+        for j in range(n_op):
+            copy_to(new_out, win_buf.at[base + me_op], send_w.at[sent],
+                    recv_w.at[base + me_op], (side, j)).start()
+            sent += 1
+    for d in range(1, n_op):
+        j = (me_op + d) % n_op
+        copy_to(new_out, win_buf.at[n_op + me_op], send_w.at[sent],
+                recv_w.at[n_op + me_op], op_peer(j)).start()
+        sent += 1
+    win_buf[n_op + me_op] = new_out[...]
+
+    from_sides = ((prev_sec, 0),) if final else ((prev_sec, 0), (next_sec, 2 * n_op))
+    for side, base in from_sides:
+        for j in range(n_op):
+            copy_to(new_out, win_buf.at[base + j], send_w.at[0], recv_w.at[base + j],
+                    (side, j)).wait_recv()
+    for d in range(1, n_op):
+        slot = (me_op + n_op - d) % n_op
+        copy_to(new_out, win_buf.at[n_op + slot], send_w.at[0], recv_w.at[n_op + slot],
+                op_peer(slot)).wait_recv()
+    win_ref[...] = win_buf[...]
+
+    for d in range(1, n_op):
+        rs_copy(d).wait_send()
+    drain_gather(*a_args)
+    drain_gather(*b_args)
+    if final:
+        drain_gather(*a2_args)
+        drain_gather(*b2_args)
+    for k in range(sent):
+        copy_to(new_out, win_buf.at[n_op + me_op], send_w.at[k], recv_w.at[n_op + me_op],
+                op_peer((me_op + 1) % n_op)).wait_send()
+
+
+def step(partial, state, shift, values, count, final, n_sec, n_op):
+    shape = partial.shape
+    rows = shape[0] * shape[1] // n_op
+    chunks = partial.reshape(n_op, rows, shape[2])
+    state_chunks = state.reshape(n_op, rows, shape[2])
+    shift_chunks = jnp.repeat(shift, n_op // shape[0])[:, None, None]
+    lane = lax.broadcasted_iota(jnp.int32, (8, 128), 1)
+    tile = jnp.zeros((8, 128), jnp.float32)
+    for k, v in enumerate(values):
+        tile = jnp.where(lane == k, v, tile)
+    slots = (2 if final else 3) * n_op
+    tile_shape = (rows, shape[2])
+    scalar_bufs = [
+        pltpu.VMEM((n_op, 8, 128), jnp.float32),
+        pltpu.VMEM((n_sec, 8, 128), jnp.float32),
+        pltpu.VMEM((8, 128), jnp.float32),
+        pltpu.VMEM((8, 128), jnp.float32),
+    ]
+    scratch = [
+        pltpu.VMEM(chunks.shape, jnp.float32),
+        pltpu.VMEM(tile_shape, jnp.float32),
+    ] + scalar_bufs + (scalar_bufs + scalar_bufs[2:] if final else []) + [
+        pltpu.VMEM(tile_shape, jnp.bfloat16),
+        pltpu.VMEM(tile_shape, jnp.bfloat16),
+        pltpu.VMEM((slots, rows, shape[2]), jnp.bfloat16),
+        pltpu.SemaphoreType.DMA((n_op,)),
+        pltpu.SemaphoreType.DMA((n_op,)),
+        pltpu.SemaphoreType.DMA((n_op,)),
+        pltpu.SemaphoreType.DMA((n_op,)),
+        pltpu.SemaphoreType.DMA((n_sec,)),
+        pltpu.SemaphoreType.DMA((n_sec,)),
+    ] + ([
+        pltpu.SemaphoreType.DMA((n_op,)),
+        pltpu.SemaphoreType.DMA((n_op,)),
+        pltpu.SemaphoreType.DMA((n_sec,)),
+        pltpu.SemaphoreType.DMA((n_sec,)),
+    ] if final else []) + [
+        pltpu.SemaphoreType.DMA((slots + n_op,)),
+        pltpu.SemaphoreType.DMA((slots,)),
+        pltpu.SemaphoreType.DMA((4,)),
+    ]
+    vmem = pl.BlockSpec(memory_space=pltpu.VMEM)
+    window = pl.pallas_call(
+        functools.partial(step_kernel, n_sec, n_op, count, final),
+        out_shape=jax.ShapeDtypeStruct((slots, rows, shape[2]), jnp.bfloat16),
+        in_specs=[vmem, vmem, vmem, vmem],
+        out_specs=vmem,
+        scratch_shapes=scratch,
+        compiler_params=pltpu.CompilerParams(
+            collective_id=3 if final else 2, has_side_effects=True
+        ),
+    )(chunks, state_chunks, shift_chunks, tile)
+    return window.reshape(slots // (n_op // shape[0]), shape[1], shape[2])
+
+
 def shifted(block, axis, distance):
     devices = range(lax.axis_size(axis))
     route = [((i - distance) % len(devices), i) for i in devices]
@@ -256,8 +465,8 @@
     left_prev = shifted(left_ops, "sec", 1)
     kept_prev = shifted(kept, "sec", 1)
     state = state_start
+    window = padded(state, (("sec", 0),), sector_local)
     for iteration in range(ITERS):
-        window = padded(state, (("sec", 0),), sector_local)
         sources = window[partner]
         halfway = jnp.einsum(
             "tbij,tbjk->tbik", left_ops, sources, preferred_element_type=jnp.float32
@@ -271,23 +480,16 @@
             first_op, jnp.sum(shift * own_square), 0.0
         )
         norm_part = jnp.where(first_op, jnp.sum(own_square), 0.0)
-        sigma_terms, (energy_sum, norm_sum) = sigma_sum(
-            partial_sigma, (energy_part, norm_part), n_sec, n_op
+        final = iteration == ITERS - 1
+        window = step(
+            partial_sigma, state, shift, (energy_part, norm_part), count, final,
+            n_sec, n_op,
         )
-        sigma = sigma_terms + shift_col * state_wide
-        ratio = energy_sum / norm_sum
-        updated = state_wide - step_size * (sigma - ratio * state_wide)
-        if iteration < ITERS - 1:
-            factor = jnp.sqrt(count / norm_sum)
-        else:
-            (new_norm,) = all_sum(
-                (jnp.where(first_op, jnp.sum(updated * updated), 0.0),), n_sec, n_op
-            )
-            factor = jnp.sqrt(count / new_norm)
-        state = (updated * factor).astype(jnp.bfloat16)
+        state = window[sector_local : 2 * sector_local]
+    state_prev = window[:sector_local]
     columns = jnp.arange(width, dtype=jnp.int32)
     keep_mask = (columns[None, :] < kept_prev[:, None]).astype(jnp.bfloat16)
-    kept_block = shifted(state, "sec", 1) * keep_mask[:, None, :]
+    kept_block = state_prev * keep_mask[:, None, :]
     out_scale = 1.0 / float(width) ** 0.5
     projected = jnp.einsum(
         "tbij,bjk->tbik", left_prev, kept_block, preferred_element_type=jnp.float32

time: 268 us -> 245 us (0.914)
  waiting for transfers between devices: 45.6 us -> 8.1 us
  Pallas kernels: 126 us -> 163 us
  starting transfers between devices: 20.2 us -> 8.69 us
  between operations: 17.6 us -> 8.54 us
  other arithmetic: 13.7 us -> 19.7 us
  matrix products: 24 us -> 19.6 us
    pallas_call x5 -> x4, Pallas kernels: 126 us -> 163 us  [step(): pl.pallas_call(functools.partial(step_kernel, n_sec, n_op, count, final),...]
    ppermute x4 -> x1, waiting for transfers between devices: 21.2 us -> 0.01 us  [padded(): lax.ppermute(tail, axis, [(i, (i + 1) % count) for i in range(count)])]
    ppermute x4 -> x1, waiting for transfers between devices: 16.9 us -> 0.01 us  [padded(): lax.ppermute(head, axis, [((i + 1) % count, i) for i in range(count)])]
    ppermute x4 -> x1, starting transfers between devices: 15.4 us -> 8.68 us  [padded(): lax.ppermute(head, axis, [((i + 1) % count, i) for i in range(count)])]
    reduce_sum x1 -> x9, other arithmetic: 1.86 us -> 7.95 us  [the longest x3 5.36 us: per_device(): norm_part = jnp.where(first_op, jnp.sum(own_square), 0.0)]
    slice x5 -> x1, local copies, waits for them, and re-layouts: 6.53 us -> 1.77 us  [per_device(): state_prev = window[:sector_local]]
    dot_general x4, matrix products: 19.8 us -> 15.4 us  [per_device(): jnp.einsum('tbij,tbjk->bik', halfway, right_ops, preferred_element_type=j...]
    ppermute x3 -> x2, waiting for transfers between devices: 7.45 us -> 8.1 us  [shifted(): return lax.ppermute(block, axis, route)]
  transfers between devices with their start and end apart: 11 -> 4, of which waited for: 8 -> 1; matrix products, arithmetic and copies ran while one was open for 6% -> 20% of each run, Pallas kernels for 21% -> 67%
where the time goes in v5:
time: 245 us; the launch traced here: 244 us
  Pallas kernels  163 us (67%)
  other arithmetic  19.7 us (8%)
  matrix products  19.6 us (8%)
  local copies, waits for them, and re-layouts  16.7 us (7%)
  starting transfers between devices  8.69 us (4%)
  between operations  8.54 us (3%)
  waiting for transfers between devices  8.1 us (3%)
    pallas_call x4, Pallas kernels, step(): pl.pallas_call(functools.partial(step_kernel, n_sec, n_op, count, final),...  163 us
    dot_general x4, matrix products, per_device(): jnp.einsum('tbij,tbjk->bik', halfway, right_ops, preferred_element_type=j...  15.4 us
    gather x4, local copies, waits for them, and re-layouts, per_device(): sources = window[partner]  9.13 us
    ppermute x1, starting transfers between devices, padded(): lax.ppermute(head, axis, [((i + 1) % count, i) for i in range(count)])  8.68 us
    ppermute x2, waiting for transfers between devices, shifted(): return lax.ppermute(block, axis, route)  8.1 us
    reduce_sum x3, other arithmetic, per_device(): norm_part = jnp.where(first_op, jnp.sum(own_square), 0.0)  5.36 us
    convert_element_type x3, other arithmetic, per_device(): state_wide = state.astype(jnp.float32)  5.13 us
  transfers between devices with their start and end apart: 4, of which 1 were waited for; matrix products, arithmetic and copies ran while one was open for 20% of the time, Pallas kernels for 67%

profile of v5, /device:TPU:1, one launch (start us, length us, event | category | flops | bytes accessed | tf_op | source)
XLA Modules:
  0.0 244.2 jit_solution(18273610095464534832)
XLA Ops:
  0.6 8.7 %collective-permute-start.1 = (bf16[2,256,256]{2,1,0:T(8,128)(2,1)}, bf16[2,256,256]{2,1,0:T(8,128)(2,1)S(1)}, u32[]{:S(2)}, u32[]{:S(2)}) collective-permute-start(bf16[2,256,256]{2,1,0:T(8,128)(2,1)} %param.6), channel_id=1, source_target_pairs={{8,0},{16,8},{24,16},{32,24},{40,32},{48,40},{56,48},{64,56},{72,6... | collective-permute-start | bytes 786440 | tf_op jit(solution)/shard_map/ppermute | solution.py:27
  11.6 8.1 %collective-permute-done.2 = s32[2]{0:T(128)S(1)} collective-permute-done((s32[2]{0:T(128)}, s32[2]{0:T(128)S(1)}, u32[]{:S(2)}, u32[]{:S(2)}) %collective-permute-start.2) | collective-permute-done | bytes 40 | tf_op jit(solution)/shard_map/ppermute | solution.py:454
  19.8 1.0 pad_maximum_fusion
  20.8 2.0 gather_fusion
  22.9 4.9 %fusion.62 = (f32[]{:T(128)}, f32[2]{0:T(128)S(1)}, f32[]{:T(128)}, f32[2,256,256,1]{2,1,3,0:T(8,128)}) fusion(bf16[2,256,256]{2,1,0:T(8,128)(2,1)S(1)} %copy-done.6, bf16[8,2,256,256]{3,2,1,0:T(8,128)(2,1)S(1)} %copy-done, bf16[8,2,256,256]{3,2,1,0:T(8,128)(2,1)} %bitcast.77, bf16[8,2,256,256]{3,2,1,0:T(8,128)(2,1)} %param.7), kind=kOutput, calls=%fused_computation.42 | convolution fusion | flops 1075576832 | bytes 7077904 | tf_op jit(solution)/shard_map/tbij,tbjk->bik/dot_general | solution.py:474
  30.9 51.1 %shard_map.77 = bf16[24,64,256]{2,1,0:T(8,128)(2,1)} custom-call(f32[8,64,256]{2,1,0:T(8,128)} %bitcast.89, bf16[8,64,256]{2,1,0:T(8,128)(2,1)} %bitcast.88, f32[8,1,1]{2,1,0:T(1,128)} %broadcast_in_dim_reshape.3.sh_ref, f32[8,128]{1,0:T(8,128)} %broadcast_select_fusion.3.t_ref), custom_call_target="tpu_custom_call" | custom-call | tf_op jit(solution)/shard_map/pallas_call | solution.py:438
  82.0 1.8 multiply_reduce_fusion.5
  83.8 1.7 slice_convert_fusion.2
  87.6 2.0 gather_fusion.1
  89.6 3.5 %fusion.5 = f32[2,256,256,1]{2,1,3,0:T(8,128)S(1)} fusion(bf16[8,2,256,256]{3,2,1,0:T(8,128)(2,1)} %bitcast.79, bf16[8,2,256,256]{3,2,1,0:T(8,128)(2,1)} %param.7, bf16[8,2,256,256]{3,2,1,0:T(8,128)(2,1)S(1)} %copy-done), kind=kOutput, calls=%fused_computation.10 | convolution fusion | flops 1074790400 | bytes 6815744 | tf_op jit(solution)/shard_map/tbij,tbjk->bik/dot_general | solution.py:474
  95.1 35.5 %shard_map.78 = bf16[24,64,256]{2,1,0:T(8,128)(2,1)} custom-call(f32[8,64,256]{2,1,0:T(8,128)} %bitcast.81, bf16[8,64,256]{2,1,0:T(8,128)(2,1)} %get-tuple-element.20.st_ref, f32[8,1,1]{2,1,0:T(1,128)} %broadcast_in_dim_reshape.3.sh_ref, f32[8,128]{1,0:T(8,128)} %broadcast_select_fusion.2.t_ref), custom_call_target="tpu_custom_call" | custom-call | tf_op jit(solution)/shard_map/pallas_call | solution.py:438
  130.7 1.8 multiply_reduce_fusion.3
  132.5 1.7 slice_convert_fusion.1
  136.3 2.0 gather_fusion.2
  138.3 3.5 %fusion.3 = f32[2,256,256,1]{2,1,3,0:T(8,128)S(1)} fusion(bf16[8,2,256,256]{3,2,1,0:T(8,128)(2,1)} %bitcast.80, bf16[8,2,256,256]{3,2,1,0:T(8,128)(2,1)} %param.7, bf16[8,2,256,256]{3,2,1,0:T(8,128)(2,1)S(1)} %copy-done), kind=kOutput, calls=%fused_computation.8 | convolution fusion | flops 1074790400 | bytes 6815744 | tf_op jit(solution)/shard_map/tbij,tbjk->bik/dot_general | solution.py:474
  143.8 34.6 %shard_map.79 = bf16[24,64,256]{2,1,0:T(8,128)(2,1)} custom-call(f32[8,64,256]{2,1,0:T(8,128)} %bitcast.82, bf16[8,64,256]{2,1,0:T(8,128)(2,1)} %get-tuple-element.18.st_ref, f32[8,1,1]{2,1,0:T(1,128)} %broadcast_in_dim_reshape.3.sh_ref, f32[8,128]{1,0:T(8,128)} %broadcast_select_fusion.1.t_ref), custom_call_target="tpu_custom_call" | custom-call | tf_op jit(solution)/shard_map/pallas_call | solution.py:438
  178.4 1.7 multiply_reduce_fusion.1
  182.3 3.1 %gather_fusion.3 = bf16[16,256,256]{2,1,0:T(8,128)(2,1)} fusion(bf16[6,256,256]{2,1,0:T(8,128)(2,1)} %bitcast.74, s32[1024]{0:T(1024)S(1)} %pad_clamp_fusion), kind=kCustom, calls=%fused_computation.3 | custom fusion | bytes 4194368 | tf_op jit(solution)/shard_map/gather | solution.py:470
  185.4 1.7 slice_convert_fusion
  187.1 3.5 %fusion.1 = f32[2,256,256,1]{2,1,3,0:T(8,128)S(1)} fusion(bf16[8,2,256,256]{3,2,1,0:T(8,128)(2,1)} %bitcast.78, bf16[8,2,256,256]{3,2,1,0:T(8,128)(2,1)} %param.7, bf16[8,2,256,256]{3,2,1,0:T(8,128)(2,1)S(1)} %copy-done), kind=kOutput, calls=%fused_computation.6 | convolution fusion | flops 1074790400 | bytes 6815744 | tf_op jit(solution)/shard_map/tbij,tbjk->bik/dot_general | solution.py:474
  192.6 41.7 %shard_map.80 = bf16[16,64,256]{2,1,0:T(8,128)(2,1)} custom-call(f32[8,64,256]{2,1,0:T(8,128)} %bitcast.85, bf16[8,64,256]{2,1,0:T(8,128)(2,1)} %get-tuple-element.16.st_ref, f32[8,1,1]{2,1,0:T(1,128)} %broadcast_in_dim_reshape.3.sh_ref, f32[8,128]{1,0:T(8,128)} %broadcast_select_fusion.t_ref), custom_call_target="tpu_custom_call" | custom-call | tf_op jit(solution)/shard_map/pallas_call | solution.py:438
  234.3 1.8 fusion.73
  236.1 4.2 %fusion.44 = bf16[8,2,256,256]{2,3,0,1:T(8,128)(2,1)} fusion(bf16[8,2,256,256]{3,2,1,0:T(8,128)(2,1)} %collective-permute-done.3, bf16[2,256,256]{2,1,0:T(8,128)(2,1)S(1)} %bitcast_multiply_fusion.3), kind=kOutput, calls=%fused_computation.29 | convolution fusion | flops 1076887552 | bytes 4456448 | tf_op jit(solution)/shard_map/bji,tbjk->tbik/dot_general | solution.py:498
  240.3 3.9 %copy.27 = bf16[8,2,256,256]{3,2,1,0:T(8,128)(2,1)} copy(bf16[8,2,256,256]{2,3,0,1:T(8,128)(2,1)} %fusion.44) | data formatting | bytes 4194304
  (52 shorter events, 10.1 us)
Async XLA Ops:
  0.6 22.2 %copy-start = (bf16[8,2,256,256]{3,2,1,0:T(8,128)(2,1)S(1)}, bf16[8,2,256,256]{3,2,1,0:T(8,128)(2,1)}, u32[]{:S(2)}) copy-start(bf16[8,2,256,256]{3,2,1,0:T(8,128)(2,1)} %param.8) | copy-start | bytes 6291460
  0.6 19.1 %collective-permute-start.1 = (bf16[2,256,256]{2,1,0:T(8,128)(2,1)}, bf16[2,256,256]{2,1,0:T(8,128)(2,1)S(1)}, u32[]{:S(2)}, u32[]{:S(2)}) collective-permute-start(bf16[2,256,256]{2,1,0:T(8,128)(2,1)} %param.6), channel_id=1, source_target_pairs={{8,0},{16,8},{24,16},{32,24},{40,32},{48,40},{56,48},{64,56},{72,6... | collective-permute-start | bytes 786440 | tf_op jit(solution)/shard_map/ppermute | solution.py:27
  9.3 10.5 %collective-permute-start = (bf16[2,256,256]{2,1,0:T(8,128)(2,1)}, bf16[2,256,256]{2,1,0:T(8,128)(2,1)S(1)}, u32[]{:S(2)}, u32[]{:S(2)}) collective-permute-start(bf16[2,256,256]{2,1,0:T(8,128)(2,1)} %param.6), channel_id=1, source_target_pairs={{0,8},{8,16},{16,24},{24,32},{32,40},{40,48},{48,56},{56,64},{64,7... | collective-permute-start | bytes 786440 | tf_op jit(solution)/shard_map/ppermute | solution.py:25
  9.3 10.4 %collective-permute-start.2 = (s32[2]{0:T(128)}, s32[2]{0:T(128)S(1)}, u32[]{:S(2)}, u32[]{:S(2)}) collective-permute-start(s32[2]{0:T(128)} %param.11), channel_id=1, source_target_pairs={{248,0},{0,8},{8,16},{16,24},{24,32},{32,40},{40,48},{48,56},{56,6... | collective-permute-start | bytes 32 | tf_op jit(solution)/shard_map/ppermute | solution.py:454
  9.3 226.8 %collective-permute-start.3 = (bf16[8,2,256,256]{3,2,1,0:T(8,128)(2,1)}, bf16[8,2,256,256]{3,2,1,0:T(8,128)(2,1)}, u32[]{:S(2)}, u32[]{:S(2)}) collective-permute-start(bf16[8,2,256,256]{3,2,1,0:T(8,128)(2,1)} %param.7), channel_id=1, source_target_pairs={{248,0},{0,8},{8,16},{16,24},{24,32},{32,40},{40,48},{48,56},{56,6... | collective-permute-start | bytes 6291464 | tf_op jit(solution)/shard_map/ppermute | solution.py:454
  20.8 2.0 copy-start.6
  22.8 4.9 %copy-start.7 = (f32[2]{0:T(128)S(1)}, f32[2]{0:T(128)}, u32[]{:S(2)}) copy-start(f32[2]{0:T(128)} %param.9) | copy-start | bytes 28
  82.0 5.6 %copy-start.2 = (bf16[24,64,256]{2,1,0:T(8,128)(2,1)S(1)}, bf16[24,64,256]{2,1,0:T(8,128)(2,1)}, u32[]{:S(2)}) copy-start(bf16[24,64,256]{2,1,0:T(8,128)(2,1)} %shard_map.77) | copy-start | bytes 2359300
  93.1 2.0 copy-start.3
  130.7 5.6 %copy-start.1 = (bf16[24,64,256]{2,1,0:T(8,128)(2,1)S(1)}, bf16[24,64,256]{2,1,0:T(8,128)(2,1)}, u32[]{:S(2)}) copy-start(bf16[24,64,256]{2,1,0:T(8,128)(2,1)} %shard_map.78) | copy-start | bytes 2359300
  141.8 2.0 copy-start.4
  190.6 2.0 copy-start.5

commit v6 on v5

--- a/solution.py
+++ b/solution.py
@@ -124,6 +124,18 @@
     def sec_peer(j):
         return (j, me_op)
 
+    def total_of(v):
+        return jnp.sum(jnp.sum(v, axis=1, keepdims=True), axis=0, keepdims=True)
+
+    lane = lax.broadcasted_iota(jnp.int32, (8, 128), 1)
+    own = st_ref[me_op].astype(jnp.float32)
+    own_square = total_of(own * own)
+    energy = sh_ref[me_op] * own_square
+    for j in range(n_op):
+        energy = energy + total_of(x_ref[j] * st_ref[j].astype(jnp.float32))
+    t_ref[...] = jnp.where(lane == 0, energy, jnp.where(lane == 1, own_square, 0.0))
+    settle(t_ref, t_out, local_sem.at[4])
+
     def rs_copy(d):
         j = (me_op + d) % n_op
         return pltpu.make_async_remote_copy(
@@ -155,7 +167,7 @@
 
     for d in range(1, n_op):
         rs_copy(d).start()
-    a_args = (n_op, me_op, t_ref, op_buf, send_a, recv_a, op_peer)
+    a_args = (n_op, me_op, t_out, op_buf, send_a, recv_a, op_peer)
     for d in range(1, n_op):
         gather_copy(*a_args, d).start()
     rs_buf[me_op] = x_ref[me_op]
@@ -239,15 +251,15 @@
     return total.reshape(shape), tuple(sums[0, k] for k in range(len(values)))
 
 
-def step_kernel(n_sec, n_op, count, final, x_ref, st_ref, sh_ref, t_ref, *refs):
+def step_kernel(n_sec, n_op, count, final, x_ref, st_ref, sh_ref, *refs):
     if final:
-        (win_ref, rs_buf, red, op_buf, sec_buf, mid, mid_out, op_buf2, sec_buf2,
-         mid2, mid2_out, mid3, mid3_out, new_buf, new_out, win_buf, send_rs, recv_rs, send_a,
+        (win_ref, t_ref, t_out, rs_buf, red, op_buf, sec_buf, mid, mid_out, op_buf2,
+         sec_buf2, mid2, mid2_out, mid3, mid3_out, new_buf, new_out, win_buf, send_rs, recv_rs, send_a,
          recv_a, send_b, recv_b, send_a2, recv_a2, send_b2, recv_b2, send_w,
          recv_w, local_sem) = refs
     else:
-        (win_ref, rs_buf, red, op_buf, sec_buf, mid, mid_out, new_buf, new_out,
-         win_buf, send_rs, recv_rs, send_a, recv_a, send_b, recv_b, send_w,
+        (win_ref, t_ref, t_out, rs_buf, red, op_buf, sec_buf, mid, mid_out, new_buf,
+         new_out, win_buf, send_rs, recv_rs, send_a, recv_a, send_b, recv_b, send_w,
          recv_w, local_sem) = refs
     me_sec = lax.axis_index("sec")
     me_op = lax.axis_index("op")
@@ -306,13 +318,25 @@
         local.start()
         local.wait()
 
+    def total_of(v):
+        return jnp.sum(jnp.sum(v, axis=1, keepdims=True), axis=0, keepdims=True)
+
+    lane = lax.broadcasted_iota(jnp.int32, (8, 128), 1)
+    own = st_ref[me_op].astype(jnp.float32)
+    own_square = total_of(own * own)
+    energy = sh_ref[me_op] * own_square
+    for j in range(n_op):
+        energy = energy + total_of(x_ref[j] * st_ref[j].astype(jnp.float32))
+    t_ref[...] = jnp.where(lane == 0, energy, jnp.where(lane == 1, own_square, 0.0))
+    settle(t_ref, t_out, local_sem.at[4])
+
     def rs_copy(d):
         j = (me_op + d) % n_op
         return copy_to(x_ref.at[j], rs_buf.at[me_op], send_rs.at[d], recv_rs.at[me_op], op_peer(j))
 
     for d in range(1, n_op):
         rs_copy(d).start()
-    a_args = (n_op, me_op, t_ref, op_buf, send_a, recv_a, op_peer)
+    a_args = (n_op, me_op, t_out, op_buf, send_a, recv_a, op_peer)
     start_gather(*a_args)
     rs_buf[me_op] = x_ref[me_op]
 
@@ -336,9 +360,7 @@
     sigma = red[...] + sh_ref[me_op] * state_wide
     updated = state_wide - step_size * (sigma - (energy_sum / norm_sum) * state_wide)
     if final:
-        square = jnp.sum(jnp.sum(updated * updated, axis=1, keepdims=True), axis=0,
-                         keepdims=True)
-        lane = lax.broadcasted_iota(jnp.int32, (8, 128), 1)
+        square = total_of(updated * updated)
         mid2[...] = jnp.where(lane == 0, square, 0.0)
         settle(mid2, mid2_out, local_sem.at[1])
         a2_args = (n_op, me_op, mid2_out, op_buf2, send_a2, recv_a2, op_peer)
@@ -393,16 +415,12 @@
                 op_peer((me_op + 1) % n_op)).wait_send()
 
 
-def step(partial, state, shift, values, count, final, n_sec, n_op):
+def step(partial, state, shift, count, final, n_sec, n_op):
     shape = partial.shape
     rows = shape[0] * shape[1] // n_op
     chunks = partial.reshape(n_op, rows, shape[2])
     state_chunks = state.reshape(n_op, rows, shape[2])
     shift_chunks = jnp.repeat(shift, n_op // shape[0])[:, None, None]
-    lane = lax.broadcasted_iota(jnp.int32, (8, 128), 1)
-    tile = jnp.zeros((8, 128), jnp.float32)
-    for k, v in enumerate(values):
-        tile = jnp.where(lane == k, v, tile)
     slots = (2 if final else 3) * n_op
     tile_shape = (rows, shape[2])
     scalar_bufs = [
@@ -412,6 +430,8 @@
         pltpu.VMEM((8, 128), jnp.float32),
     ]
     scratch = [
+        pltpu.VMEM((8, 128), jnp.float32),
+        pltpu.VMEM((8, 128), jnp.float32),
         pltpu.VMEM(chunks.shape, jnp.float32),
         pltpu.VMEM(tile_shape, jnp.float32),
     ] + scalar_bufs + (scalar_bufs + scalar_bufs[2:] if final else []) + [
@@ -432,19 +452,19 @@
     ] if final else []) + [
         pltpu.SemaphoreType.DMA((slots + n_op,)),
         pltpu.SemaphoreType.DMA((slots,)),
-        pltpu.SemaphoreType.DMA((4,)),
+        pltpu.SemaphoreType.DMA((5,)),
     ]
     vmem = pl.BlockSpec(memory_space=pltpu.VMEM)
     window = pl.pallas_call(
         functools.partial(step_kernel, n_sec, n_op, count, final),
         out_shape=jax.ShapeDtypeStruct((slots, rows, shape[2]), jnp.bfloat16),
-        in_specs=[vmem, vmem, vmem, vmem],
+        in_specs=[vmem, vmem, vmem],
         out_specs=vmem,
         scratch_shapes=scratch,
         compiler_params=pltpu.CompilerParams(
             collective_id=3 if final else 2, has_side_effects=True
         ),
-    )(chunks, state_chunks, shift_chunks, tile)
+    )(chunks, state_chunks, shift_chunks)
     return window.reshape(slots // (n_op // shape[0]), shape[1], shape[2])
 
 
@@ -458,8 +478,6 @@
     sector_local = state_start.shape[0]
     width = state_start.shape[1]
     count = float(sector_local * lax.axis_size("sec") * width * width)
-    shift_col = shift[:, None, None]
-    first_op = lax.axis_index("op") == 0
     n_sec = lax.axis_size("sec")
     n_op = lax.axis_size("op")
     left_prev = shifted(left_ops, "sec", 1)
@@ -474,17 +492,8 @@
         partial_sigma = jnp.einsum(
             "tbij,tbjk->bik", halfway, right_ops, preferred_element_type=jnp.float32
         )
-        state_wide = state.astype(jnp.float32)
-        own_square = jnp.sum(state_wide * state_wide, axis=(1, 2))
-        energy_part = jnp.sum(state_wide * partial_sigma) + jnp.where(
-            first_op, jnp.sum(shift * own_square), 0.0
-        )
-        norm_part = jnp.where(first_op, jnp.sum(own_square), 0.0)
         final = iteration == ITERS - 1
-        window = step(
-            partial_sigma, state, shift, (energy_part, norm_part), count, final,
-            n_sec, n_op,
-        )
+        window = step(partial_sigma, state, shift, count, final, n_sec, n_op)
         state = window[sector_local : 2 * sector_local]
     state_prev = window[:sector_local]
     columns = jnp.arange(width, dtype=jnp.int32)
@@ -494,8 +503,11 @@
     projected = jnp.einsum(
         "tbij,bjk->tbik", left_prev, kept_block, preferred_element_type=jnp.float32
     ).astype(jnp.bfloat16)
+    kept_turned = jnp.broadcast_to(
+        jnp.swapaxes(kept_block, 1, 2)[None], left_prev.shape
+    )
     new_ops = (
-        jnp.einsum("bji,tbjk->tbik", kept_block, projected, preferred_element_type=jnp.float32)
+        jnp.einsum("tbij,tbjk->tbik", kept_turned, projected, preferred_element_type=jnp.float32)
         * out_scale
     ).astype(jnp.bfloat16)
     return (state, new_ops)

time: 245 us -> 229 us (0.935)
  other arithmetic: 19.7 us -> 1.85 us
  between operations: 8.54 us -> 0.72 us
  Pallas kernels: 163 us -> 168 us
  local copies, waits for them, and re-layouts: 16.7 us -> 19.9 us
    reduce_sum x13 -> x0, other arithmetic: 10.4 us -> none  [the longest x3 5.36 us: per_device(): norm_part = jnp.where(first_op, jnp.sum(own_square), 0.0)]
    convert_element_type x3 -> x0, other arithmetic: 5.13 us -> none  [per_device(): state_wide = state.astype(jnp.float32)]
    slice x0 -> x3, local copies, waits for them, and re-layouts: none -> 5.01 us  [per_device(): state = window[sector_local:2 * sector_local]]
    pallas_call x4, Pallas kernels: 163 us -> 168 us  [step(): pl.pallas_call(functools.partial(step_kernel, n_sec, n_op, count, final),...]
    unnamed x17 -> x2, local copies, waits for them, and re-layouts: 3.96 us -> 0.01 us
  transfers between devices with their start and end apart: 4 -> 4, of which waited for: 1 -> 1; matrix products, arithmetic and copies ran while one was open for 20% -> 17% of each run, Pallas kernels for 67% -> 73%
where the time goes in v6:
time: 229 us; the launch traced here: 228 us
  Pallas kernels  168 us (73%)
  matrix products  21.3 us (9%)
  local copies, waits for them, and re-layouts  19.9 us (9%)
  starting transfers between devices  8.69 us (4%)
  waiting for transfers between devices  8.11 us (4%)
    pallas_call x4, Pallas kernels, step(): pl.pallas_call(functools.partial(step_kernel, n_sec, n_op, count, final),...  168 us
    dot_general x4, matrix products, per_device(): jnp.einsum('tbij,tbjk->bik', halfway, right_ops, preferred_element_type=j...  17.1 us
    gather x4, local copies, waits for them, and re-layouts, per_device(): sources = window[partner]  11.4 us
    ppermute x1, starting transfers between devices, padded(): lax.ppermute(head, axis, [((i + 1) % count, i) for i in range(count)])  8.68 us
    ppermute x2, waiting for transfers between devices, shifted(): return lax.ppermute(block, axis, route)  8.11 us
    slice x3, local copies, waits for them, and re-layouts, per_device(): state = window[sector_local:2 * sector_local]  5.01 us
  transfers between devices with their start and end apart: 4, of which 1 were waited for; matrix products, arithmetic and copies ran while one was open for 17% of the time, Pallas kernels for 73%

profile of v6, /device:TPU:1, one launch (start us, length us, event | category | flops | bytes accessed | tf_op | source)
XLA Modules:
  0.0 228.4 jit_solution(8508033659008737169)
XLA Ops:
  0.6 8.7 %collective-permute-start.1 = (bf16[2,256,256]{2,1,0:T(8,128)(2,1)}, bf16[2,256,256]{2,1,0:T(8,128)(2,1)S(1)}, u32[]{:S(2)}, u32[]{:S(2)}) collective-permute-start(bf16[2,256,256]{2,1,0:T(8,128)(2,1)} %param.6), channel_id=1, source_target_pairs={{8,0},{16,8},{24,16},{32,24},{40,32},{48,40},{56,48},{64,56},{72,6... | collective-permute-start | bytes 786440 | tf_op jit(solution)/shard_map/ppermute | solution.py:27
  9.3 0.7 compare_select_fusion
  10.2 0.7 broadcast_in_dim.7
  10.9 0.7 broadcast_in_dim_reshape.3.sh_ref
  11.6 8.1 %collective-permute-done.2 = s32[2]{0:T(128)S(1)} collective-permute-done((s32[2]{0:T(128)}, s32[2]{0:T(128)S(1)}, u32[]{:S(2)}, u32[]{:S(2)}) %collective-permute-start.2) | collective-permute-done | bytes 40 | tf_op jit(solution)/shard_map/ppermute | solution.py:474
  19.8 1.0 pad_maximum_fusion
  20.8 2.0 gather_fusion
  22.8 4.3 %fusion.7 = f32[2,256,256,1]{2,1,3,0:T(8,128)} fusion(bf16[8,2,256,256]{3,2,1,0:T(8,128)(2,1)} %bitcast.59, bf16[8,2,256,256]{3,2,1,0:T(8,128)(2,1)} %param.7, bf16[8,2,256,256]{3,2,1,0:T(8,128)(2,1)S(1)} %copy-done), kind=kOutput, calls=%fused_computation.12 | convolution fusion | flops 1074790400 | bytes 6815744 | tf_op jit(solution)/shard_map/tbij,tbjk->bik/dot_general | solution.py:492
  27.1 54.9 %shard_map.77 = bf16[24,64,256]{2,1,0:T(8,128)(2,1)} custom-call(f32[8,64,256]{2,1,0:T(8,128)} %bitcast.65, bf16[8,64,256]{2,1,0:T(8,128)(2,1)} %bitcast.62, f32[8,1,1]{2,1,0:T(1,128)} %broadcast_in_dim_reshape.3.sh_ref), custom_call_target="tpu_custom_call" | custom-call | tf_op jit(solution)/shard_map/pallas_call | solution.py:458
  82.0 3.1 %gather_fusion.1 = bf16[16,256,256]{2,1,0:T(8,128)(2,1)} fusion(bf16[6,256,256]{2,1,0:T(8,128)(2,1)} %bitcast.53, s32[1024]{0:T(1024)S(1)} %pad_clamp_fusion), kind=kCustom, calls=%fused_computation.1 | custom fusion | bytes 4194368 | tf_op jit(solution)/shard_map/gather | solution.py:488
  85.1 4.3 %fusion.5 = f32[2,256,256,1]{2,1,3,0:T(8,128)} fusion(bf16[8,2,256,256]{3,2,1,0:T(8,128)(2,1)} %bitcast.61, bf16[8,2,256,256]{3,2,1,0:T(8,128)(2,1)} %param.7, bf16[8,2,256,256]{3,2,1,0:T(8,128)(2,1)S(1)} %copy-done), kind=kOutput, calls=%fused_computation.10 | convolution fusion | flops 1074790400 | bytes 6815744 | tf_op jit(solution)/shard_map/tbij,tbjk->bik/dot_general | solution.py:492
  89.4 1.7 slice.24.st_ref
  91.1 35.8 %shard_map.78 = bf16[24,64,256]{2,1,0:T(8,128)(2,1)} custom-call(f32[8,64,256]{2,1,0:T(8,128)} %bitcast.63, bf16[8,64,256]{2,1,0:T(8,128)(2,1)} %slice.24.st_ref, f32[8,1,1]{2,1,0:T(1,128)} %broadcast_in_dim_reshape.3.sh_ref), custom_call_target="tpu_custom_call" | custom-call | tf_op jit(solution)/shard_map/pallas_call | solution.py:458
  126.8 1.7 slice.25.st_ref
  128.5 3.1 %gather_fusion.2 = bf16[16,256,256]{2,1,0:T(8,128)(2,1)} fusion(bf16[6,256,256]{2,1,0:T(8,128)(2,1)} %bitcast.55, s32[1024]{0:T(1024)S(1)} %pad_clamp_fusion), kind=kCustom, calls=%fused_computation.2 | custom fusion | bytes 4194368 | tf_op jit(solution)/shard_map/gather | solution.py:488
  131.6 4.3 %fusion.3 = f32[2,256,256,1]{2,1,3,0:T(8,128)} fusion(bf16[8,2,256,256]{3,2,1,0:T(8,128)(2,1)} %bitcast.60, bf16[8,2,256,256]{3,2,1,0:T(8,128)(2,1)} %param.7, bf16[8,2,256,256]{3,2,1,0:T(8,128)(2,1)S(1)} %copy-done), kind=kOutput, calls=%fused_computation.8 | convolution fusion | flops 1074790400 | bytes 6815744 | tf_op jit(solution)/shard_map/tbij,tbjk->bik/dot_general | solution.py:492
  135.9 34.0 %shard_map.79 = bf16[24,64,256]{2,1,0:T(8,128)(2,1)} custom-call(f32[8,64,256]{2,1,0:T(8,128)} %bitcast.64, bf16[8,64,256]{2,1,0:T(8,128)(2,1)} %slice.25.st_ref, f32[8,1,1]{2,1,0:T(1,128)} %broadcast_in_dim_reshape.3.sh_ref), custom_call_target="tpu_custom_call" | custom-call | tf_op jit(solution)/shard_map/pallas_call | solution.py:458
  169.9 1.7 slice.26.st_ref
  171.6 3.1 %gather_fusion.3 = bf16[16,256,256]{2,1,0:T(8,128)(2,1)} fusion(bf16[6,256,256]{2,1,0:T(8,128)(2,1)} %bitcast.54, s32[1024]{0:T(1024)S(1)} %pad_clamp_fusion), kind=kCustom, calls=%fused_computation.3 | custom fusion | bytes 4194368 | tf_op jit(solution)/shard_map/gather | solution.py:488
  174.7 4.3 %fusion.1 = f32[2,256,256,1]{2,1,3,0:T(8,128)} fusion(bf16[8,2,256,256]{3,2,1,0:T(8,128)(2,1)} %bitcast.58, bf16[8,2,256,256]{3,2,1,0:T(8,128)(2,1)} %param.7, bf16[8,2,256,256]{3,2,1,0:T(8,128)(2,1)S(1)} %copy-done), kind=kOutput, calls=%fused_computation.6 | convolution fusion | flops 1074790400 | bytes 6815744 | tf_op jit(solution)/shard_map/tbij,tbjk->bik/dot_general | solution.py:492
  179.0 43.2 %shard_map.80 = bf16[16,64,256]{2,1,0:T(8,128)(2,1)} custom-call(f32[8,64,256]{2,1,0:T(8,128)} %bitcast.66, bf16[8,64,256]{2,1,0:T(8,128)(2,1)} %slice.26.st_ref, f32[8,1,1]{2,1,0:T(1,128)} %broadcast_in_dim_reshape.3.sh_ref), custom_call_target="tpu_custom_call" | custom-call | tf_op jit(solution)/shard_map/pallas_call | solution.py:458
  222.2 1.8 fusion.55
  224.0 0.1 copy.27
  224.2 4.2 %multiply_convert_fusion = bf16[8,2,256,256]{3,2,1,0:T(8,128)(2,1)} fusion(bf16[8,2,256,256]{3,2,1,0:T(8,128)(2,1)} %collective-permute-done.3, bf16[2,256,256]{2,1,0:T(8,128)(2,1)S(1)} %copy.27, bf16[2,256,256]{2,1,0:T(8,128)(2,1)S(1)} %bitcast_multiply_fusion), kind=kOutput, calls=%fused_computation.4 | convolution fusion | flops 1076887552 | bytes 4718592 | tf_op jit(solution)/shard_map/tbij,tbjk->tbik/dot_general | solution.py:510
  (14 shorter events, 0.3 us)
Async XLA Ops:
  0.6 22.2 %copy-start = (bf16[8,2,256,256]{3,2,1,0:T(8,128)(2,1)S(1)}, bf16[8,2,256,256]{3,2,1,0:T(8,128)(2,1)}, u32[]{:S(2)}) copy-start(bf16[8,2,256,256]{3,2,1,0:T(8,128)(2,1)} %param.8) | copy-start | bytes 6291460
  0.6 19.1 %collective-permute-start.1 = (bf16[2,256,256]{2,1,0:T(8,128)(2,1)}, bf16[2,256,256]{2,1,0:T(8,128)(2,1)S(1)}, u32[]{:S(2)}, u32[]{:S(2)}) collective-permute-start(bf16[2,256,256]{2,1,0:T(8,128)(2,1)} %param.6), channel_id=1, source_target_pairs={{8,0},{16,8},{24,16},{32,24},{40,32},{48,40},{56,48},{64,56},{72,6... | collective-permute-start | bytes 786440 | tf_op jit(solution)/shard_map/ppermute | solution.py:27
  9.3 10.5 %collective-permute-start = (bf16[2,256,256]{2,1,0:T(8,128)(2,1)}, bf16[2,256,256]{2,1,0:T(8,128)(2,1)S(1)}, u32[]{:S(2)}, u32[]{:S(2)}) collective-permute-start(bf16[2,256,256]{2,1,0:T(8,128)(2,1)} %param.6), channel_id=1, source_target_pairs={{0,8},{8,16},{16,24},{24,32},{32,40},{40,48},{48,56},{56,64},{64,7... | collective-permute-start | bytes 786440 | tf_op jit(solution)/shard_map/ppermute | solution.py:25
  9.3 10.4 %collective-permute-start.2 = (s32[2]{0:T(128)}, s32[2]{0:T(128)S(1)}, u32[]{:S(2)}, u32[]{:S(2)}) collective-permute-start(s32[2]{0:T(128)} %param.11), channel_id=1, source_target_pairs={{248,0},{0,8},{8,16},{16,24},{24,32},{32,40},{40,48},{48,56},{56,6... | collective-permute-start | bytes 32 | tf_op jit(solution)/shard_map/ppermute | solution.py:474
  9.3 214.9 %collective-permute-start.3 = (bf16[8,2,256,256]{3,2,1,0:T(8,128)(2,1)}, bf16[8,2,256,256]{3,2,1,0:T(8,128)(2,1)}, u32[]{:S(2)}, u32[]{:S(2)}) collective-permute-start(bf16[8,2,256,256]{3,2,1,0:T(8,128)(2,1)} %param.7), channel_id=1, source_target_pairs={{248,0},{0,8},{8,16},{16,24},{24,32},{32,40},{40,48},{48,56},{56,6... | collective-permute-start | bytes 6291464 | tf_op jit(solution)/shard_map/ppermute | solution.py:474

commit v7 on v6

--- a/solution.py
+++ b/solution.py
@@ -480,11 +480,17 @@
     count = float(sector_local * lax.axis_size("sec") * width * width)
     n_sec = lax.axis_size("sec")
     n_op = lax.axis_size("op")
-    left_prev = shifted(left_ops, "sec", 1)
     kept_prev = shifted(kept, "sec", 1)
+    terms = left_ops.shape[0]
+    cuts = [terms * k // ITERS for k in range(ITERS + 1)]
+    left_pieces = []
     state = state_start
     window = padded(state, (("sec", 0),), sector_local)
     for iteration in range(ITERS):
+        piece, window = lax.optimization_barrier(
+            (left_ops[cuts[iteration] : cuts[iteration + 1]], window)
+        )
+        left_pieces.append(shifted(piece, "sec", 1))
         sources = window[partner]
         halfway = jnp.einsum(
             "tbij,tbjk->tbik", left_ops, sources, preferred_element_type=jnp.float32
@@ -493,9 +499,13 @@
             "tbij,tbjk->bik", halfway, right_ops, preferred_element_type=jnp.float32
         )
         final = iteration == ITERS - 1
+        left_pieces[-1], partial_sigma = lax.optimization_barrier(
+            (left_pieces[-1], partial_sigma)
+        )
         window = step(partial_sigma, state, shift, count, final, n_sec, n_op)
         state = window[sector_local : 2 * sector_local]
     state_prev = window[:sector_local]
+    left_prev = jnp.concatenate(left_pieces, axis=0)
     columns = jnp.arange(width, dtype=jnp.int32)
     keep_mask = (columns[None, :] < kept_prev[:, None]).astype(jnp.bfloat16)
     kept_block = state_prev * keep_mask[:, None, :]

time: 229 us -> 247 us (1.079)
  waiting for transfers between devices: 8.11 us -> 41.5 us
  Pallas kernels: 168 us -> 148 us
    ppermute x2 -> x5, waiting for transfers between devices: 8.11 us -> 41.5 us  [shifted(): return lax.ppermute(block, axis, route)]
    pallas_call x4, Pallas kernels: 168 us -> 148 us  [step(): pl.pallas_call(functools.partial(step_kernel, n_sec, n_op, count, final),...]
    slice x0 -> x1, local copies, waits for them, and re-layouts: none -> 2.95 us  [per_device(): left_ops[cuts[iteration]:cuts[iteration + 1]]]
  transfers between devices with their start and end apart: 4 -> 7, of which waited for: 1 -> 5; matrix products, arithmetic and copies ran while one was open for 17% -> 14% of each run, Pallas kernels for 73% -> 0%
where the time goes in v7:
time: 247 us; the launch traced here: 245 us
  Pallas kernels  148 us (60%)
  waiting for transfers between devices  41.5 us (17%)
  local copies, waits for them, and re-layouts  22.2 us (9%)
  matrix products  21 us (9%)
  starting transfers between devices  9.56 us (4%)
    pallas_call x4, Pallas kernels, step(): pl.pallas_call(functools.partial(step_kernel, n_sec, n_op, count, final),...  148 us
    ppermute x5, waiting for transfers between devices, shifted(): return lax.ppermute(block, axis, route)  41.5 us
    dot_general x4, matrix products, per_device(): jnp.einsum('tbij,tbjk->bik', halfway, right_ops, preferred_element_type=j...  17.1 us
    gather x4, local copies, waits for them, and re-layouts, per_device(): sources = window[partner]  11.4 us
    ppermute x1, starting transfers between devices, padded(): lax.ppermute(head, axis, [((i + 1) % count, i) for i in range(count)])  8.68 us
    slice x3, local copies, waits for them, and re-layouts, per_device(): state = window[sector_local:2 * sector_local]  5.01 us
  transfers between devices with their start and end apart: 7, of which 5 were waited for; matrix products, arithmetic and copies ran while one was open for 14% of the time, Pallas kernels for 0%

profile of v7, /device:TPU:1, one launch (start us, length us, event | category | flops | bytes accessed | tf_op | source)
XLA Modules:
  0.0 245.1 jit_solution(6173356889907058961)
XLA Ops:
  0.6 8.7 %collective-permute-start.1 = (bf16[2,256,256]{2,1,0:T(8,128)(2,1)}, bf16[2,256,256]{2,1,0:T(8,128)(2,1)S(1)}, u32[]{:S(2)}, u32[]{:S(2)}) collective-permute-start(bf16[2,256,256]{2,1,0:T(8,128)(2,1)} %param.6), channel_id=1, source_target_pairs={{8,0},{16,8},{24,16},{32,24},{40,32},{48,40},{56,48},{64,56},{72,6... | collective-permute-start | bytes 786440 | tf_op jit(solution)/shard_map/ppermute | solution.py:27
  10.2 2.9 %fusion.103 = (bf16[2,2,256,256]{3,2,1,0:T(8,128)(2,1)}, bf16[2,2,256,256]{3,2,1,0:T(8,128)(2,1)}, bf16[2,2,256,256]{3,2,1,0:T(8,128)(2,1)}, bf16[2,2,256,256]{3,2,1,0:T(8,128)(2,1)}) fusion(bf16[8,2,256,256]{3,2,1,0:T(8,128)(2,1)} %param.7), kind=kLoop, calls=%fused_computation.55 | loop fusion | bytes 4194304 | tf_op jit(solution)/shard_map/slice | solution.py:491
  13.9 5.9 %collective-permute-done.6 = s32[2]{0:T(128)S(1)} collective-permute-done((s32[2]{0:T(128)}, s32[2]{0:T(128)S(1)}, u32[]{:S(2)}, u32[]{:S(2)}) %collective-permute-start.6) | collective-permute-done | bytes 40 | tf_op jit(solution)/shard_map/ppermute | solution.py:474
  21.0 2.0 gather_fusion
  23.0 4.3 %fusion.62 = f32[2,256,256]{2,1,0:T(8,128)} fusion(bf16[8,2,256,256]{3,2,1,0:T(8,128)(2,1)S(1)} %copy-done, bf16[8,2,256,256]{3,2,1,0:T(8,128)(2,1)} %bitcast.66, bf16[8,2,256,256]{3,2,1,0:T(8,128)(2,1)} %param.7), kind=kOutput, calls=%fused_computation.43 | convolution fusion | flops 1074790400 | bytes 6815744 | tf_op jit(solution)/shard_map/tbij,tbjk->bik/dot_general | solution.py:498
  27.3 8.8 %collective-permute-done.2 = bf16[2,2,256,256]{3,2,1,0:T(8,128)(2,1)S(1)} collective-permute-done((bf16[2,2,256,256]{3,2,1,0:T(8,128)(2,1)}, bf16[2,2,256,256]{3,2,1,0:T(8,128)(2,1)S(1)}, u32[]{:S(2)}, u32[]{:S(2)}) %collective-permute-start.2) | collective-permute-done | bytes 524320 | tf_op jit(solution)/shard_map/ppermute | solution.py:474
  36.1 37.3 %shard_map.77 = bf16[24,64,256]{2,1,0:T(8,128)(2,1)} custom-call(f32[8,64,256]{2,1,0:T(8,128)} %bitcast.72, bf16[8,64,256]{2,1,0:T(8,128)(2,1)} %bitcast.69, f32[8,1,1]{2,1,0:T(1,128)} %broadcast_in_dim_reshape.3.sh_ref), custom_call_target="tpu_custom_call" | custom-call | tf_op jit(solution)/shard_map/pallas_call | solution.py:458
  73.4 1.7 slice.40.st_ref
  75.1 3.1 %gather_fusion.1 = bf16[16,256,256]{2,1,0:T(8,128)(2,1)} fusion(bf16[6,256,256]{2,1,0:T(8,128)(2,1)} %bitcast.62, s32[1024]{0:T(1024)S(1)} %pad_clamp_fusion), kind=kCustom, calls=%fused_computation.1 | custom fusion | bytes 4194368 | tf_op jit(solution)/shard_map/gather | solution.py:494
  78.3 4.3 %fusion.71 = f32[2,256,256]{2,1,0:T(8,128)} fusion(bf16[8,2,256,256]{3,2,1,0:T(8,128)(2,1)S(1)} %copy-done, bf16[8,2,256,256]{3,2,1,0:T(8,128)(2,1)} %bitcast.67, bf16[8,2,256,256]{3,2,1,0:T(8,128)(2,1)} %param.7), kind=kOutput, calls=%fused_computation.44 | convolution fusion | flops 1074790400 | bytes 6815744 | tf_op jit(solution)/shard_map/tbij,tbjk->bik/dot_general | solution.py:498
  82.5 9.1 %collective-permute-done.3 = bf16[2,2,256,256]{3,2,1,0:T(8,128)(2,1)} collective-permute-done((bf16[2,2,256,256]{3,2,1,0:T(8,128)(2,1)S(1)}, bf16[2,2,256,256]{3,2,1,0:T(8,128)(2,1)}, u32[]{:S(2)}, u32[]{:S(2)}) %collective-permute-start.3) | collective-permute-done | bytes 524320 | tf_op jit(solution)/shard_map/ppermute | solution.py:474
  91.7 34.6 %shard_map.78 = bf16[24,64,256]{2,1,0:T(8,128)(2,1)} custom-call(f32[8,64,256]{2,1,0:T(8,128)} %bitcast.70, bf16[8,64,256]{2,1,0:T(8,128)(2,1)} %slice.40.st_ref, f32[8,1,1]{2,1,0:T(1,128)} %broadcast_in_dim_reshape.3.sh_ref), custom_call_target="tpu_custom_call" | custom-call | tf_op jit(solution)/shard_map/pallas_call | solution.py:458
  126.2 1.7 slice.41.st_ref
  128.2 3.1 %gather_fusion.2 = bf16[16,256,256]{2,1,0:T(8,128)(2,1)} fusion(bf16[6,256,256]{2,1,0:T(8,128)(2,1)} %bitcast.61, s32[1024]{0:T(1024)S(1)} %pad_clamp_fusion), kind=kCustom, calls=%fused_computation.2 | custom fusion | bytes 4194368 | tf_op jit(solution)/shard_map/gather | solution.py:494
  131.4 4.3 %fusion.80 = f32[2,256,256]{2,1,0:T(8,128)} fusion(bf16[8,2,256,256]{3,2,1,0:T(8,128)(2,1)S(1)} %copy-done, bf16[8,2,256,256]{3,2,1,0:T(8,128)(2,1)} %bitcast.68, bf16[8,2,256,256]{3,2,1,0:T(8,128)(2,1)} %param.7), kind=kOutput, calls=%fused_computation.45 | convolution fusion | flops 1074790400 | bytes 6815744 | tf_op jit(solution)/shard_map/tbij,tbjk->bik/dot_general | solution.py:498
  135.6 8.9 %collective-permute-done.4 = bf16[2,2,256,256]{3,2,1,0:T(8,128)(2,1)} collective-permute-done((bf16[2,2,256,256]{3,2,1,0:T(8,128)(2,1)S(1)}, bf16[2,2,256,256]{3,2,1,0:T(8,128)(2,1)}, u32[]{:S(2)}, u32[]{:S(2)}) %collective-permute-start.4) | collective-permute-done | bytes 524320 | tf_op jit(solution)/shard_map/ppermute | solution.py:474
  144.5 34.5 %shard_map.79 = bf16[24,64,256]{2,1,0:T(8,128)(2,1)} custom-call(f32[8,64,256]{2,1,0:T(8,128)} %bitcast.71, bf16[8,64,256]{2,1,0:T(8,128)(2,1)} %slice.41.st_ref, f32[8,1,1]{2,1,0:T(1,128)} %broadcast_in_dim_reshape.3.sh_ref), custom_call_target="tpu_custom_call" | custom-call | tf_op jit(solution)/shard_map/pallas_call | solution.py:458
  179.0 1.7 slice.42.st_ref
  181.1 3.1 %gather_fusion.3 = bf16[16,256,256]{2,1,0:T(8,128)(2,1)} fusion(bf16[6,256,256]{2,1,0:T(8,128)(2,1)} %bitcast.60, s32[1024]{0:T(1024)S(1)} %pad_clamp_fusion), kind=kCustom, calls=%fused_computation.3 | custom fusion | bytes 4194368 | tf_op jit(solution)/shard_map/gather | solution.py:494
  184.2 4.3 %fusion.89 = f32[2,256,256]{2,1,0:T(8,128)} fusion(bf16[8,2,256,256]{3,2,1,0:T(8,128)(2,1)S(1)} %copy-done, bf16[8,2,256,256]{3,2,1,0:T(8,128)(2,1)} %bitcast.65, bf16[8,2,256,256]{3,2,1,0:T(8,128)(2,1)} %param.7), kind=kOutput, calls=%fused_computation.46 | convolution fusion | flops 1074790400 | bytes 6815744 | tf_op jit(solution)/shard_map/tbij,tbjk->bik/dot_general | solution.py:498
  188.5 8.8 %collective-permute-done.5 = bf16[2,2,256,256]{3,2,1,0:T(8,128)(2,1)} collective-permute-done((bf16[2,2,256,256]{3,2,1,0:T(8,128)(2,1)S(1)}, bf16[2,2,256,256]{3,2,1,0:T(8,128)(2,1)}, u32[]{:S(2)}, u32[]{:S(2)}) %collective-permute-start.5) | collective-permute-done | bytes 524320 | tf_op jit(solution)/shard_map/ppermute | solution.py:474
  197.3 41.9 %shard_map.80 = bf16[16,64,256]{2,1,0:T(8,128)(2,1)} custom-call(f32[8,64,256]{2,1,0:T(8,128)} %bitcast.73, bf16[8,64,256]{2,1,0:T(8,128)(2,1)} %slice.42.st_ref, f32[8,1,1]{2,1,0:T(1,128)} %broadcast_in_dim_reshape.3.sh_ref), custom_call_target="tpu_custom_call" | custom-call | tf_op jit(solution)/shard_map/pallas_call | solution.py:458
  239.2 1.8 fusion.104
  241.2 3.9 %multiply_convert_fusion = bf16[8,2,256,256]{3,2,1,0:T(8,128)(2,1)} fusion(bf16[2,2,256,256]{3,2,1,0:T(8,128)(2,1)} %collective-permute-done.5, bf16[2,2,256,256]{3,2,1,0:T(8,128)(2,1)} %collective-permute-done.4, bf16[2,2,256,256]{3,2,1,0:T(8,128)(2,1)} %collective-permute-done.3, bf16[2,2,256,256]{3,2,1,0:T(8,128)(2,1)S(1)} %copy-done.6, ...), kind=kOutput, calls=%fused_computation.4 | convolution fusion | flops 1085276160 | bytes 4718592 | tf_op jit(solution)/shard_map/tbij,tbjk->tbik/dot_general | solution.py:520
  (35 shorter events, 3.8 us)
Async XLA Ops:
  0.6 22.4 %copy-start = (bf16[8,2,256,256]{3,2,1,0:T(8,128)(2,1)S(1)}, bf16[8,2,256,256]{3,2,1,0:T(8,128)(2,1)}, u32[]{:S(2)}) copy-start(bf16[8,2,256,256]{3,2,1,0:T(8,128)(2,1)} %param.8) | copy-start | bytes 6291460
  0.6 19.2 %collective-permute-start.1 = (bf16[2,256,256]{2,1,0:T(8,128)(2,1)}, bf16[2,256,256]{2,1,0:T(8,128)(2,1)S(1)}, u32[]{:S(2)}, u32[]{:S(2)}) collective-permute-start(bf16[2,256,256]{2,1,0:T(8,128)(2,1)} %param.6), channel_id=1, source_target_pairs={{8,0},{16,8},{24,16},{32,24},{40,32},{48,40},{56,48},{64,56},{72,6... | collective-permute-start | bytes 786440 | tf_op jit(solution)/shard_map/ppermute | solution.py:27
  9.3 10.6 %collective-permute-start = (bf16[2,256,256]{2,1,0:T(8,128)(2,1)}, bf16[2,256,256]{2,1,0:T(8,128)(2,1)}, u32[]{:S(2)}, u32[]{:S(2)}) collective-permute-start(bf16[2,256,256]{2,1,0:T(8,128)(2,1)} %param.6), channel_id=1, source_target_pairs={{0,8},{8,16},{16,24},{24,32},{32,40},{40,48},{48,56},{56,64},{64,7... | collective-permute-start | bytes 786440 | tf_op jit(solution)/shard_map/ppermute | solution.py:25
  9.3 10.5 %collective-permute-start.6 = (s32[2]{0:T(128)}, s32[2]{0:T(128)S(1)}, u32[]{:S(2)}, u32[]{:S(2)}) collective-permute-start(s32[2]{0:T(128)} %param.11), channel_id=1, source_target_pairs={{248,0},{0,8},{8,16},{16,24},{24,32},{32,40},{40,48},{48,56},{56,6... | collective-permute-start | bytes 32 | tf_op jit(solution)/shard_map/ppermute | solution.py:474
  10.2 3.0 %copy-start.7 = (f32[2]{0:T(128)S(1)}, f32[2]{0:T(128)}, u32[]{:S(2)}) copy-start(f32[2]{0:T(128)} %param.9) | copy-start | bytes 28
  10.2 9.7 %copy-start.1 = (bf16[2,256,256]{2,1,0:T(8,128)(2,1)S(1)}, bf16[2,256,256]{2,1,0:T(8,128)(2,1)}, u32[]{:S(2)}) copy-start(bf16[2,256,256]{2,1,0:T(8,128)(2,1)} %param.6) | copy-start | bytes 786436
  20.9 15.2 %collective-permute-start.2 = (bf16[2,2,256,256]{3,2,1,0:T(8,128)(2,1)}, bf16[2,2,256,256]{3,2,1,0:T(8,128)(2,1)S(1)}, u32[]{:S(2)}, u32[]{:S(2)}) collective-permute-start(bf16[2,2,256,256]{3,2,1,0:T(8,128)(2,1)} %get-tuple-element.18), channel_id=1, source_target_pairs={{248,0},{0,8},{8,16},{16,24},{24,32},{32,40},{40,48},{48,56},{56,6... | collective-permute-start | bytes 1572872 | tf_op jit(solution)/shard_map/ppermute | solution.py:474
  27.3 47.8 %copy-start.4 = (bf16[2,2,256,256]{3,2,1,0:T(8,128)(2,1)S(1)}, bf16[2,2,256,256]{3,2,1,0:T(8,128)(2,1)}, u32[]{:S(2)}) copy-start(bf16[2,2,256,256]{3,2,1,0:T(8,128)(2,1)} %get-tuple-element.21) | copy-start | bytes 1572868
  36.1 42.2 %copy-start.5 = (bf16[2,2,256,256]{3,2,1,0:T(8,128)(2,1)}, bf16[2,2,256,256]{3,2,1,0:T(8,128)(2,1)S(1)}, u32[]{:S(2)}) copy-start(bf16[2,2,256,256]{3,2,1,0:T(8,128)(2,1)S(1)} %collective-permute-done.2) | copy-start | bytes 1572868
  75.1 16.6 %collective-permute-start.3 = (bf16[2,2,256,256]{3,2,1,0:T(8,128)(2,1)S(1)}, bf16[2,2,256,256]{3,2,1,0:T(8,128)(2,1)}, u32[]{:S(2)}, u32[]{:S(2)}) collective-permute-start(bf16[2,2,256,256]{3,2,1,0:T(8,128)(2,1)S(1)} %copy-done.4), channel_id=1, source_target_pairs={{248,0},{0,8},{8,16},{16,24},{24,32},{32,40},{40,48},{48,56},{56,6... | collective-permute-start | bytes 1572872 | tf_op jit(solution)/shard_map/ppermute | solution.py:474
  82.5 45.4 %copy-start.3 = (bf16[2,2,256,256]{3,2,1,0:T(8,128)(2,1)S(1)}, bf16[2,2,256,256]{3,2,1,0:T(8,128)(2,1)}, u32[]{:S(2)}) copy-start(bf16[2,2,256,256]{3,2,1,0:T(8,128)(2,1)} %get-tuple-element.24) | copy-start | bytes 1572868
  127.9 16.6 %collective-permute-start.4 = (bf16[2,2,256,256]{3,2,1,0:T(8,128)(2,1)S(1)}, bf16[2,2,256,256]{3,2,1,0:T(8,128)(2,1)}, u32[]{:S(2)}, u32[]{:S(2)}) collective-permute-start(bf16[2,2,256,256]{3,2,1,0:T(8,128)(2,1)S(1)} %copy-done.3), channel_id=1, source_target_pairs={{248,0},{0,8},{8,16},{16,24},{24,32},{32,40},{40,48},{48,56},{56,6... | collective-permute-start | bytes 1572872 | tf_op jit(solution)/shard_map/ppermute | solution.py:474
  135.6 45.1 %copy-start.2 = (bf16[2,2,256,256]{3,2,1,0:T(8,128)(2,1)S(1)}, bf16[2,2,256,256]{3,2,1,0:T(8,128)(2,1)}, u32[]{:S(2)}) copy-start(bf16[2,2,256,256]{3,2,1,0:T(8,128)(2,1)} %get-tuple-element.27) | copy-start | bytes 1572868
  180.7 16.6 %collective-permute-start.5 = (bf16[2,2,256,256]{3,2,1,0:T(8,128)(2,1)S(1)}, bf16[2,2,256,256]{3,2,1,0:T(8,128)(2,1)}, u32[]{:S(2)}, u32[]{:S(2)}) collective-permute-start(bf16[2,2,256,256]{3,2,1,0:T(8,128)(2,1)S(1)} %copy-done.2), channel_id=1, source_target_pairs={{248,0},{0,8},{8,16},{16,24},{24,32},{32,40},{40,48},{48,56},{56,6... | collective-permute-start | bytes 1572872 | tf_op jit(solution)/shard_map/ppermute | solution.py:474
  188.5 52.6 %copy-start.6 = (bf16[2,2,256,256]{3,2,1,0:T(8,128)(2,1)S(1)}, bf16[2,2,256,256]{3,2,1,0:T(8,128)(2,1)}, u32[]{:S(2)}) copy-start(bf16[2,2,256,256]{3,2,1,0:T(8,128)(2,1)} %copy-done.5) | copy-start | bytes 1572868

commit v8 on v6

--- a/solution.py
+++ b/solution.py
@@ -128,11 +128,11 @@
         return jnp.sum(jnp.sum(v, axis=1, keepdims=True), axis=0, keepdims=True)
 
     lane = lax.broadcasted_iota(jnp.int32, (8, 128), 1)
-    own = st_ref[me_op].astype(jnp.float32)
+    own = st_ref[n_op + me_op].astype(jnp.float32)
     own_square = total_of(own * own)
     energy = sh_ref[me_op] * own_square
     for j in range(n_op):
-        energy = energy + total_of(x_ref[j] * st_ref[j].astype(jnp.float32))
+        energy = energy + total_of(x_ref[j] * st_ref[n_op + j].astype(jnp.float32))
     t_ref[...] = jnp.where(lane == 0, energy, jnp.where(lane == 1, own_square, 0.0))
     settle(t_ref, t_out, local_sem.at[4])
 
@@ -322,11 +322,11 @@
         return jnp.sum(jnp.sum(v, axis=1, keepdims=True), axis=0, keepdims=True)
 
     lane = lax.broadcasted_iota(jnp.int32, (8, 128), 1)
-    own = st_ref[me_op].astype(jnp.float32)
+    own = st_ref[n_op + me_op].astype(jnp.float32)
     own_square = total_of(own * own)
     energy = sh_ref[me_op] * own_square
     for j in range(n_op):
-        energy = energy + total_of(x_ref[j] * st_ref[j].astype(jnp.float32))
+        energy = energy + total_of(x_ref[j] * st_ref[n_op + j].astype(jnp.float32))
     t_ref[...] = jnp.where(lane == 0, energy, jnp.where(lane == 1, own_square, 0.0))
     settle(t_ref, t_out, local_sem.at[4])
 
@@ -356,7 +356,7 @@
     sums = ordered_sum(sec_buf, n_sec)
     energy_sum = sums[0:1, 0:1]
     norm_sum = sums[0:1, 1:2]
-    state_wide = st_ref[me_op].astype(jnp.float32)
+    state_wide = st_ref[n_op + me_op].astype(jnp.float32)
     sigma = red[...] + sh_ref[me_op] * state_wide
     updated = state_wide - step_size * (sigma - (energy_sum / norm_sum) * state_wide)
     if final:
@@ -415,11 +415,11 @@
                 op_peer((me_op + 1) % n_op)).wait_send()
 
 
-def step(partial, state, shift, count, final, n_sec, n_op):
+def step(partial, window, shift, count, final, n_sec, n_op):
     shape = partial.shape
     rows = shape[0] * shape[1] // n_op
     chunks = partial.reshape(n_op, rows, shape[2])
-    state_chunks = state.reshape(n_op, rows, shape[2])
+    state_chunks = window.reshape(-1, rows, shape[2])
     shift_chunks = jnp.repeat(shift, n_op // shape[0])[:, None, None]
     slots = (2 if final else 3) * n_op
     tile_shape = (rows, shape[2])
@@ -468,6 +468,41 @@
     return window.reshape(slots // (n_op // shape[0]), shape[1], shape[2])
 
 
+def sigma_part_kernel(partner_ref, win_ref, left_ref, right_ref, o_ref):
+    b = pl.program_id(0)
+    total = jnp.zeros(o_ref.shape[1:], jnp.float32)
+    for t in range(left_ref.shape[0]):
+        source = win_ref[partner_ref[t, b]]
+        halfway = jnp.dot(left_ref[t, 0], source, preferred_element_type=jnp.float32)
+        total = total + jnp.dot(halfway.astype(jnp.bfloat16), right_ref[t, 0],
+                                preferred_element_type=jnp.float32)
+    o_ref[0] = total
+
+
+def sigma_part(window, left_ops, right_ops, partner):
+    terms, sectors, m, _ = left_ops.shape
+    op_spec = pl.BlockSpec((terms, 1, m, m), lambda b, p: (0, b, 0, 0))
+    return pl.pallas_call(
+        sigma_part_kernel,
+        out_shape=jax.ShapeDtypeStruct((sectors, m, m), jnp.float32),
+        grid_spec=pltpu.PrefetchScalarGridSpec(
+            num_scalar_prefetch=1,
+            grid=(sectors,),
+            in_specs=[
+                pl.BlockSpec(window.shape, lambda b, p: (0, 0, 0)),
+                op_spec,
+                op_spec,
+            ],
+            out_specs=pl.BlockSpec((1, m, m), lambda b, p: (b, 0, 0)),
+        ),
+        cost_estimate=pl.CostEstimate(
+            flops=4 * terms * sectors * m * m * m,
+            bytes_accessed=2 * left_ops.size * 2 + window.size * 2 + sectors * m * m * 4,
+            transcendentals=0,
+        ),
+    )(partner, window, left_ops, right_ops)
+
+
 def shifted(block, axis, distance):
     devices = range(lax.axis_size(axis))
     route = [((i - distance) % len(devices), i) for i in devices]
@@ -485,15 +520,9 @@
     state = state_start
     window = padded(state, (("sec", 0),), sector_local)
     for iteration in range(ITERS):
-        sources = window[partner]
-        halfway = jnp.einsum(
-            "tbij,tbjk->tbik", left_ops, sources, preferred_element_type=jnp.float32
-        ).astype(jnp.bfloat16)
-        partial_sigma = jnp.einsum(
-            "tbij,tbjk->bik", halfway, right_ops, preferred_element_type=jnp.float32
-        )
+        partial_sigma = sigma_part(window, left_ops, right_ops, partner)
         final = iteration == ITERS - 1
-        window = step(partial_sigma, state, shift, count, final, n_sec, n_op)
+        window = step(partial_sigma, window, shift, count, final, n_sec, n_op)
         state = window[sector_local : 2 * sector_local]
     state_prev = window[:sector_local]
     columns = jnp.arange(width, dtype=jnp.int32)

time: 229 us -> 238 us (1.039)
  waiting for transfers between devices: 8.11 us -> 48.3 us
  matrix products: 21.3 us -> 2.59 us
  local copies, waits for them, and re-layouts: 19.9 us -> 6.53 us
  Pallas kernels: 168 us -> 171 us
    ppermute x2, waiting for transfers between devices: 8.11 us -> 48.3 us  [shifted(): return lax.ppermute(block, axis, route)]
    pallas_call x0 -> x4, Pallas kernels: none -> 20 us  [sigma_part(): pl.pallas_call(sigma_part_kernel, out_shape=jax.ShapeDtypeStruct((sectors...]
    dot_general x4 -> x0, matrix products: 17.1 us -> none  [per_device(): jnp.einsum('tbij,tbjk->bik', halfway, right_ops, preferred_element_type=j...]
    pallas_call x4, Pallas kernels: 168 us -> 151 us  [step(): pl.pallas_call(functools.partial(step_kernel, n_sec, n_op, count, final),...]
    gather x4 -> x0, local copies, waits for them, and re-layouts: 11.4 us -> none  [per_device(): sources = window[partner]]
    slice x3 -> x0, local copies, waits for them, and re-layouts: 5.01 us -> none  [per_device(): state = window[sector_local:2 * sector_local]]
    ppermute x1, starting transfers between devices: 8.68 us -> 4.68 us  [padded(): lax.ppermute(head, axis, [((i + 1) % count, i) for i in range(count)])]
    unnamed x2 -> x5, local copies, waits for them, and re-layouts: 0.01 us -> 3.21 us
  transfers between devices with their start and end apart: 4 -> 4, of which waited for: 1 -> 1; matrix products, arithmetic and copies ran while one was open for 17% -> 2% of each run, Pallas kernels for 73% -> 72%
where the time goes in v8:
time: 238 us
  Pallas kernels  171 us (72%)
  waiting for transfers between devices  48.3 us (20%)
  starting transfers between devices  8.86 us (4%)
  local copies, waits for them, and re-layouts  6.53 us (3%)
  matrix products  2.59 us (1%)
    pallas_call x4, Pallas kernels, step(): pl.pallas_call(functools.partial(step_kernel, n_sec, n_op, count, final),...  151 us
    ppermute x2, waiting for transfers between devices, shifted(): return lax.ppermute(block, axis, route)  48.3 us
    pallas_call x4, Pallas kernels, sigma_part(): pl.pallas_call(sigma_part_kernel, out_shape=jax.ShapeDtypeStruct((sectors...  20 us
  transfers between devices with their start and end apart: 4, of which 1 were waited for; matrix products, arithmetic and copies ran while one was open for 2% of the time, Pallas kernels for 72%

profile of v8, /device:TPU:1, one launch (start us, length us, event | category | flops | bytes accessed | tf_op | source)
XLA Modules:
  0.0 238.1 jit_solution(12064048535076658591)
XLA Ops:
  0.6 2.5 %collective-permute-start.3 = (bf16[8,2,256,256]{3,2,1,0:T(8,128)(2,1)}, bf16[8,2,256,256]{3,2,1,0:T(8,128)(2,1)S(1)}, u32[]{:S(2)}, u32[]{:S(2)}) collective-permute-start(bf16[8,2,256,256]{3,2,1,0:T(8,128)(2,1)} %left_ref.7), channel_id=1, source_target_pairs={{248,0},{0,8},{8,16},{16,24},{24,32},{32,40},{40,48},{48,56},{56,6... | collective-permute-start | bytes 6291464 | tf_op jit(solution)/shard_map/ppermute | solution.py:509
  3.2 1.6 collective-permute-start
  4.8 4.7 %collective-permute-start.1 = (bf16[2,256,256]{2,1,0:T(8,128)(2,1)}, bf16[2,256,256]{2,1,0:T(8,128)(2,1)S(1)}, u32[]{:S(2)}, u32[]{:S(2)}) collective-permute-start(bf16[2,256,256]{2,1,0:T(8,128)(2,1)} %param.6), channel_id=1, source_target_pairs={{8,0},{16,8},{24,16},{32,24},{40,32},{48,40},{56,48},{64,56},{72,6... | collective-permute-start | bytes 786440 | tf_op jit(solution)/shard_map/ppermute | solution.py:27
  9.5 0.0 collective-permute-start.2
  9.5 0.7 broadcast_in_dim.4
  10.2 0.7 broadcast_in_dim_reshape.3.sh_ref
  10.9 1.3 copy.14.partner_ref
  12.2 48.3 %collective-permute-done.2 = s32[2]{0:T(128)S(1)} collective-permute-done((s32[2]{0:T(128)}, s32[2]{0:T(128)S(1)}, u32[]{:S(2)}, u32[]{:S(2)}) %collective-permute-start.2) | collective-permute-done | bytes 40 | tf_op jit(solution)/shard_map/ppermute | solution.py:509
  60.5 0.1 compare_convert_fusion
  60.6 1.0 constant_dynamic-update-slice_fusion.1
  61.6 0.0 collective-permute-done.1
  61.6 0.0 copy-start
  61.6 0.9 copy-done
  62.5 5.0 %shard_map.77 = f32[2,256,256]{2,1,0:T(8,128)} custom-call(s32[8,2]{1,0:T(8,128)} %copy.14.partner_ref, bf16[6,256,256]{2,1,0:T(8,128)(2,1)} %copy-done, bf16[8,2,256,256]{3,2,1,0:T(8,128)(2,1)} %left_ref.7, bf16[8,2,256,256]{3,2,1,0:T(8,128)(2,1)} %right_ref.7), custom_call_target="tpu_custom_call" | custom-call | flops 1073741824 | bytes 5505024 | tf_op jit(solution)/shard_map/pallas_call | solution.py:485
  67.5 35.3 %shard_map.78.st_ref = bf16[24,64,256]{2,1,0:T(8,128)(2,1)} custom-call(f32[8,64,256]{2,1,0:T(8,128)} %bitcast.32, bf16[24,64,256]{2,1,0:T(8,128)(2,1)} %bitcast.28, f32[8,1,1]{2,1,0:T(1,128)} %broadcast_in_dim_reshape.3.sh_ref), custom_call_target="tpu_custom_call" | custom-call | tf_op jit(solution)/shard_map/pallas_call | solution.py:458
  102.8 5.0 %shard_map.79 = f32[2,256,256]{2,1,0:T(8,128)} custom-call(s32[8,2]{1,0:T(8,128)} %copy.14.partner_ref, bf16[6,256,256]{2,1,0:T(8,128)(2,1)} %bitcast.26, bf16[8,2,256,256]{3,2,1,0:T(8,128)(2,1)} %left_ref.7, bf16[8,2,256,256]{3,2,1,0:T(8,128)(2,1)} %right_ref.7), custom_call_target="tpu_custom_call" | custom-call | flops 1073741824 | bytes 5505024 | tf_op jit(solution)/shard_map/pallas_call | solution.py:485
  107.8 33.9 %shard_map.80.st_ref = bf16[24,64,256]{2,1,0:T(8,128)(2,1)} custom-call(f32[8,64,256]{2,1,0:T(8,128)} %bitcast.33, bf16[24,64,256]{2,1,0:T(8,128)(2,1)} %shard_map.78.st_ref, f32[8,1,1]{2,1,0:T(1,128)} %broadcast_in_dim_reshape.3.sh_ref), custom_call_target="tpu_custom_call" | custom-call | tf_op jit(solution)/shard_map/pallas_call | solution.py:458
  141.7 5.0 %shard_map.81 = f32[2,256,256]{2,1,0:T(8,128)} custom-call(s32[8,2]{1,0:T(8,128)} %copy.14.partner_ref, bf16[6,256,256]{2,1,0:T(8,128)(2,1)} %bitcast.27, bf16[8,2,256,256]{3,2,1,0:T(8,128)(2,1)} %left_ref.7, bf16[8,2,256,256]{3,2,1,0:T(8,128)(2,1)} %right_ref.7), custom_call_target="tpu_custom_call" | custom-call | flops 1073741824 | bytes 5505024 | tf_op jit(solution)/shard_map/pallas_call | solution.py:485
  146.7 35.5 %shard_map.82.st_ref = bf16[24,64,256]{2,1,0:T(8,128)(2,1)} custom-call(f32[8,64,256]{2,1,0:T(8,128)} %bitcast.34, bf16[24,64,256]{2,1,0:T(8,128)(2,1)} %shard_map.80.st_ref, f32[8,1,1]{2,1,0:T(1,128)} %broadcast_in_dim_reshape.3.sh_ref), custom_call_target="tpu_custom_call" | custom-call | tf_op jit(solution)/shard_map/pallas_call | solution.py:458
  182.2 5.0 %shard_map.83 = f32[2,256,256]{2,1,0:T(8,128)} custom-call(s32[8,2]{1,0:T(8,128)} %copy.14.partner_ref, bf16[6,256,256]{2,1,0:T(8,128)(2,1)} %bitcast.25, bf16[8,2,256,256]{3,2,1,0:T(8,128)(2,1)} %left_ref.7, bf16[8,2,256,256]{3,2,1,0:T(8,128)(2,1)} %right_ref.7), custom_call_target="tpu_custom_call" | custom-call | flops 1073741824 | bytes 5505024 | tf_op jit(solution)/shard_map/pallas_call | solution.py:485
  187.2 46.3 %shard_map.84 = bf16[16,64,256]{2,1,0:T(8,128)(2,1)} custom-call(f32[8,64,256]{2,1,0:T(8,128)} %bitcast.31, bf16[24,64,256]{2,1,0:T(8,128)(2,1)} %shard_map.82.st_ref, f32[8,1,1]{2,1,0:T(1,128)} %broadcast_in_dim_reshape.3.sh_ref), custom_call_target="tpu_custom_call" | custom-call | tf_op jit(solution)/shard_map/pallas_call | solution.py:458
  233.5 1.8 fusion.7
  235.3 0.1 copy.16
  235.5 2.6 %multiply_convert_fusion = bf16[8,2,256,256]{3,2,1,0:T(8,128)(2,1)} fusion(bf16[8,2,256,256]{3,2,1,0:T(8,128)(2,1)S(1)} %collective-permute-done.3, bf16[2,256,256]{2,1,0:T(8,128)(2,1)S(1)} %copy.16, bf16[2,256,256]{2,1,0:T(8,128)(2,1)S(1)} %bitcast_multiply_fusion), kind=kOutput, calls=%fused_computation | convolution fusion | flops 1076887552 | bytes 4718592 | tf_op jit(solution)/shard_map/tbij,tbjk->tbik/dot_general | solution.py:539
  (6 shorter events, 0.1 us)
Async XLA Ops:
  0.6 234.8 %collective-permute-start.3 = (bf16[8,2,256,256]{3,2,1,0:T(8,128)(2,1)}, bf16[8,2,256,256]{3,2,1,0:T(8,128)(2,1)S(1)}, u32[]{:S(2)}, u32[]{:S(2)}) collective-permute-start(bf16[8,2,256,256]{3,2,1,0:T(8,128)(2,1)} %left_ref.7), channel_id=1, source_target_pairs={{248,0},{0,8},{8,16},{16,24},{24,32},{32,40},{40,48},{48,56},{56,6... | collective-permute-start | bytes 6291464 | tf_op jit(solution)/shard_map/ppermute | solution.py:509
  3.2 57.4 %collective-permute-start = (bf16[2,256,256]{2,1,0:T(8,128)(2,1)}, bf16[2,256,256]{2,1,0:T(8,128)(2,1)S(1)}, u32[]{:S(2)}, u32[]{:S(2)}) collective-permute-start(bf16[2,256,256]{2,1,0:T(8,128)(2,1)} %param.6), channel_id=1, source_target_pairs={{0,8},{8,16},{16,24},{24,32},{32,40},{40,48},{48,56},{56,64},{64,7... | collective-permute-start | bytes 786440 | tf_op jit(solution)/shard_map/ppermute | solution.py:25
  4.8 56.8 %collective-permute-start.1 = (bf16[2,256,256]{2,1,0:T(8,128)(2,1)}, bf16[2,256,256]{2,1,0:T(8,128)(2,1)S(1)}, u32[]{:S(2)}, u32[]{:S(2)}) collective-permute-start(bf16[2,256,256]{2,1,0:T(8,128)(2,1)} %param.6), channel_id=1, source_target_pairs={{8,0},{16,8},{24,16},{32,24},{40,32},{48,40},{56,48},{64,56},{72,6... | collective-permute-start | bytes 786440 | tf_op jit(solution)/shard_map/ppermute | solution.py:27
  9.5 51.0 %collective-permute-start.2 = (s32[2]{0:T(128)}, s32[2]{0:T(128)S(1)}, u32[]{:S(2)}, u32[]{:S(2)}) collective-permute-start(s32[2]{0:T(128)} %param.11), channel_id=1, source_target_pairs={{248,0},{0,8},{8,16},{16,24},{24,32},{32,40},{40,48},{48,56},{56,6... | collective-permute-start | bytes 32 | tf_op jit(solution)/shard_map/ppermute | solution.py:509
  61.6 0.9 copy-start

commit v9 on v8

--- a/solution.py
+++ b/solution.py
@@ -515,10 +515,13 @@
     count = float(sector_local * lax.axis_size("sec") * width * width)
     n_sec = lax.axis_size("sec")
     n_op = lax.axis_size("op")
-    left_prev = shifted(left_ops, "sec", 1)
     kept_prev = shifted(kept, "sec", 1)
     state = state_start
     window = padded(state, (("sec", 0),), sector_local)
+    left_after, window, kept_prev = lax.optimization_barrier(
+        (left_ops, window, kept_prev)
+    )
+    left_prev = shifted(left_after, "sec", 1)
     for iteration in range(ITERS):
         partial_sigma = sigma_part(window, left_ops, right_ops, partner)
         final = iteration == ITERS - 1

time: 238 us -> 218 us (0.916)
  waiting for transfers between devices: 48.3 us -> 6.16 us
  Pallas kernels: 171 us -> 193 us
    ppermute x2, waiting for transfers between devices: 48.3 us -> 0.01 us  [shifted(): return lax.ppermute(block, axis, route)]
    pallas_call x4, Pallas kernels: 151 us -> 173 us  [step(): pl.pallas_call(functools.partial(step_kernel, n_sec, n_op, count, final),...]
    ppermute x1, waiting for transfers between devices: 0.01 us -> 6.15 us  [padded(): lax.ppermute(tail, axis, [(i, (i + 1) % count) for i in range(count)])]
    ppermute x2, starting transfers between devices: 2.55 us -> 0.01 us  [shifted(): return lax.ppermute(block, axis, route)]
  transfers between devices with their start and end apart: 4 -> 4, of which waited for: 1 -> 1; matrix products, arithmetic and copies ran while one was open for 2% -> 3% of each run, Pallas kernels for 72% -> 89%
where the time goes in v9:
time: 218 us
  Pallas kernels  193 us (89%)
  starting transfers between devices  8.77 us (4%)
  waiting for transfers between devices  6.16 us (3%)
  local copies, waits for them, and re-layouts  4.65 us (2%)
  matrix products  2.59 us (1%)
    pallas_call x4, Pallas kernels, step(): pl.pallas_call(functools.partial(step_kernel, n_sec, n_op, count, final),...  173 us
    pallas_call x4, Pallas kernels, sigma_part(): pl.pallas_call(sigma_part_kernel, out_shape=jax.ShapeDtypeStruct((sectors...  20 us
    ppermute x1, starting transfers between devices, padded(): lax.ppermute(head, axis, [((i + 1) % count, i) for i in range(count)])  6.22 us
    ppermute x1, waiting for transfers between devices, padded(): lax.ppermute(tail, axis, [(i, (i + 1) % count) for i in range(count)])  6.15 us
  transfers between devices with their start and end apart: 4, of which 1 were waited for; matrix products, arithmetic and copies ran while one was open for 3% of the time, Pallas kernels for 89%

profile of v9, /device:TPU:1, one launch (start us, length us, event | category | flops | bytes accessed | tf_op | source)
XLA Modules:
  0.0 217.8 jit_solution(2093284634343409289)
XLA Ops:
  0.6 2.5 %collective-permute-start = (bf16[2,256,256]{2,1,0:T(8,128)(2,1)}, bf16[2,256,256]{2,1,0:T(8,128)(2,1)S(1)}, u32[]{:S(2)}, u32[]{:S(2)}) collective-permute-start(bf16[2,256,256]{2,1,0:T(8,128)(2,1)} %param.6), channel_id=1, source_target_pairs={{0,8},{8,16},{16,24},{24,32},{32,40},{40,48},{48,56},{56,64},{64,7... | collective-permute-start | bytes 786440 | tf_op jit(solution)/shard_map/ppermute | solution.py:25
  3.2 6.2 %collective-permute-start.1 = (bf16[2,256,256]{2,1,0:T(8,128)(2,1)}, bf16[2,256,256]{2,1,0:T(8,128)(2,1)S(1)}, u32[]{:S(2)}, u32[]{:S(2)}) collective-permute-start(bf16[2,256,256]{2,1,0:T(8,128)(2,1)} %param.6), channel_id=1, source_target_pairs={{8,0},{16,8},{24,16},{32,24},{40,32},{48,40},{56,48},{64,56},{72,6... | collective-permute-start | bytes 786440 | tf_op jit(solution)/shard_map/ppermute | solution.py:27
  9.4 0.0 collective-permute-start.2
  9.4 6.1 %collective-permute-done = bf16[2,256,256]{2,1,0:T(8,128)(2,1)S(1)} collective-permute-done((bf16[2,256,256]{2,1,0:T(8,128)(2,1)}, bf16[2,256,256]{2,1,0:T(8,128)(2,1)S(1)}, u32[]{:S(2)}, u32[]{:S(2)}) %collective-permute-start) | collective-permute-done | bytes 262176 | tf_op jit(solution)/shard_map/ppermute | solution.py:25
  15.5 0.0 collective-permute-done.1
  15.6 1.9 pad_maximum_fusion.win_ref
  17.5 0.0 collective-permute-done.2
  17.5 0.0 collective-permute-start.3
  17.5 0.7 broadcast_in_dim.4
  18.2 0.7 broadcast_in_dim_reshape.3.sh_ref
  18.9 1.3 copy.14.partner_ref
  20.2 5.0 %shard_map.77 = f32[2,256,256]{2,1,0:T(8,128)} custom-call(s32[8,2]{1,0:T(8,128)} %copy.14.partner_ref, bf16[6,256,256]{2,1,0:T(8,128)(2,1)} %pad_maximum_fusion.win_ref, bf16[8,2,256,256]{3,2,1,0:T(8,128)(2,1)} %left_ref.7, bf16[8,2,256,256]{3,2,1,0:T(8,128)(2,1)} %right_ref.7), custom_call_target="tpu_custom_call" | custom-call | flops 1073741824 | bytes 5505024 | tf_op jit(solution)/shard_map/pallas_call | solution.py:485
  25.2 59.1 %shard_map.78.st_ref = bf16[24,64,256]{2,1,0:T(8,128)(2,1)} custom-call(f32[8,64,256]{2,1,0:T(8,128)} %bitcast.32, bf16[24,64,256]{2,1,0:T(8,128)(2,1)} %bitcast.25, f32[8,1,1]{2,1,0:T(1,128)} %broadcast_in_dim_reshape.3.sh_ref), custom_call_target="tpu_custom_call" | custom-call | tf_op jit(solution)/shard_map/pallas_call | solution.py:458
  84.3 5.0 %shard_map.79 = f32[2,256,256]{2,1,0:T(8,128)} custom-call(s32[8,2]{1,0:T(8,128)} %copy.14.partner_ref, bf16[6,256,256]{2,1,0:T(8,128)(2,1)} %bitcast.27, bf16[8,2,256,256]{3,2,1,0:T(8,128)(2,1)} %left_ref.7, bf16[8,2,256,256]{3,2,1,0:T(8,128)(2,1)} %right_ref.7), custom_call_target="tpu_custom_call" | custom-call | flops 1073741824 | bytes 5505024 | tf_op jit(solution)/shard_map/pallas_call | solution.py:485
  89.3 35.1 %shard_map.80.st_ref = bf16[24,64,256]{2,1,0:T(8,128)(2,1)} custom-call(f32[8,64,256]{2,1,0:T(8,128)} %bitcast.33, bf16[24,64,256]{2,1,0:T(8,128)(2,1)} %shard_map.78.st_ref, f32[8,1,1]{2,1,0:T(1,128)} %broadcast_in_dim_reshape.3.sh_ref), custom_call_target="tpu_custom_call" | custom-call | tf_op jit(solution)/shard_map/pallas_call | solution.py:458
  124.4 5.0 %shard_map.81 = f32[2,256,256]{2,1,0:T(8,128)} custom-call(s32[8,2]{1,0:T(8,128)} %copy.14.partner_ref, bf16[6,256,256]{2,1,0:T(8,128)(2,1)} %bitcast.28, bf16[8,2,256,256]{3,2,1,0:T(8,128)(2,1)} %left_ref.7, bf16[8,2,256,256]{3,2,1,0:T(8,128)(2,1)} %right_ref.7), custom_call_target="tpu_custom_call" | custom-call | flops 1073741824 | bytes 5505024 | tf_op jit(solution)/shard_map/pallas_call | solution.py:485
  129.4 33.6 %shard_map.82.st_ref = bf16[24,64,256]{2,1,0:T(8,128)(2,1)} custom-call(f32[8,64,256]{2,1,0:T(8,128)} %bitcast.34, bf16[24,64,256]{2,1,0:T(8,128)(2,1)} %shard_map.80.st_ref, f32[8,1,1]{2,1,0:T(1,128)} %broadcast_in_dim_reshape.3.sh_ref), custom_call_target="tpu_custom_call" | custom-call | tf_op jit(solution)/shard_map/pallas_call | solution.py:458
  163.0 5.0 %shard_map.83 = f32[2,256,256]{2,1,0:T(8,128)} custom-call(s32[8,2]{1,0:T(8,128)} %copy.14.partner_ref, bf16[6,256,256]{2,1,0:T(8,128)(2,1)} %bitcast.26, bf16[8,2,256,256]{3,2,1,0:T(8,128)(2,1)} %left_ref.7, bf16[8,2,256,256]{3,2,1,0:T(8,128)(2,1)} %right_ref.7), custom_call_target="tpu_custom_call" | custom-call | flops 1073741824 | bytes 5505024 | tf_op jit(solution)/shard_map/pallas_call | solution.py:485
  168.0 45.1 %shard_map.84 = bf16[16,64,256]{2,1,0:T(8,128)(2,1)} custom-call(f32[8,64,256]{2,1,0:T(8,128)} %bitcast.31, bf16[24,64,256]{2,1,0:T(8,128)(2,1)} %shard_map.82.st_ref, f32[8,1,1]{2,1,0:T(1,128)} %broadcast_in_dim_reshape.3.sh_ref), custom_call_target="tpu_custom_call" | custom-call | tf_op jit(solution)/shard_map/pallas_call | solution.py:458
  213.1 0.1 compare_convert_fusion
  213.2 1.8 fusion.7
  215.0 0.1 copy.16
  215.2 0.0 collective-permute-done.3
  215.2 2.6 %multiply_convert_fusion = bf16[8,2,256,256]{3,2,1,0:T(8,128)(2,1)} fusion(bf16[8,2,256,256]{3,2,1,0:T(8,128)(2,1)S(1)} %collective-permute-done.3, bf16[2,256,256]{2,1,0:T(8,128)(2,1)S(1)} %copy.16, bf16[2,256,256]{2,1,0:T(8,128)(2,1)S(1)} %bitcast_multiply_fusion), kind=kOutput, calls=%fused_computation | convolution fusion | flops 1076887552 | bytes 4718592 | tf_op jit(solution)/shard_map/tbij,tbjk->tbik/dot_general | solution.py:542
  (2 shorter events, 0.0 us)
Async XLA Ops:
  0.6 14.9 %collective-permute-start = (bf16[2,256,256]{2,1,0:T(8,128)(2,1)}, bf16[2,256,256]{2,1,0:T(8,128)(2,1)S(1)}, u32[]{:S(2)}, u32[]{:S(2)}) collective-permute-start(bf16[2,256,256]{2,1,0:T(8,128)(2,1)} %param.6), channel_id=1, source_target_pairs={{0,8},{8,16},{16,24},{24,32},{32,40},{40,48},{48,56},{56,64},{64,7... | collective-permute-start | bytes 786440 | tf_op jit(solution)/shard_map/ppermute | solution.py:25
  3.2 12.4 %collective-permute-start.1 = (bf16[2,256,256]{2,1,0:T(8,128)(2,1)}, bf16[2,256,256]{2,1,0:T(8,128)(2,1)S(1)}, u32[]{:S(2)}, u32[]{:S(2)}) collective-permute-start(bf16[2,256,256]{2,1,0:T(8,128)(2,1)} %param.6), channel_id=1, source_target_pairs={{8,0},{16,8},{24,16},{32,24},{40,32},{48,40},{56,48},{64,56},{72,6... | collective-permute-start | bytes 786440 | tf_op jit(solution)/shard_map/ppermute | solution.py:27
  9.4 8.1 %collective-permute-start.2 = (s32[2]{0:T(128)}, s32[2]{0:T(128)S(1)}, u32[]{:S(2)}, u32[]{:S(2)}) collective-permute-start(s32[2]{0:T(128)} %param.11), channel_id=1, source_target_pairs={{248,0},{0,8},{8,16},{16,24},{24,32},{32,40},{40,48},{48,56},{56,6... | collective-permute-start | bytes 32 | tf_op jit(solution)/shard_map/ppermute | solution.py:509
  17.5 197.7 %collective-permute-start.3 = (bf16[8,2,256,256]{3,2,1,0:T(8,128)(2,1)}, bf16[8,2,256,256]{3,2,1,0:T(8,128)(2,1)S(1)}, u32[]{:S(2)}, u32[]{:S(2)}) collective-permute-start(bf16[8,2,256,256]{3,2,1,0:T(8,128)(2,1)} %left_ref.7), channel_id=1, source_target_pairs={{248,0},{0,8},{8,16},{16,24},{24,32},{32,40},{40,48},{48,56},{56,6... | collective-permute-start | bytes 6291464 | tf_op jit(solution)/shard_map/ppermute | solution.py:509

commit v10 on v8

--- a/solution.py
+++ b/solution.py
@@ -251,15 +251,15 @@
     return total.reshape(shape), tuple(sums[0, k] for k in range(len(values)))
 
 
-def step_kernel(n_sec, n_op, count, final, x_ref, st_ref, sh_ref, *refs):
+def step_kernel(n_sec, n_op, count, final, x_ref, st_ref, sh_ref, piece_ref, *refs):
     if final:
-        (win_ref, t_ref, t_out, rs_buf, red, op_buf, sec_buf, mid, mid_out, op_buf2,
-         sec_buf2, mid2, mid2_out, mid3, mid3_out, new_buf, new_out, win_buf, send_rs, recv_rs, send_a,
-         recv_a, send_b, recv_b, send_a2, recv_a2, send_b2, recv_b2, send_w,
-         recv_w, local_sem) = refs
+        (win_ref, got_ref, t_ref, t_out, rs_buf, red, op_buf, sec_buf, mid, mid_out,
+         op_buf2, sec_buf2, mid2, mid2_out, mid3, mid3_out, new_buf, new_out, win_buf,
+         send_rs, recv_rs, send_a, recv_a, send_b, recv_b, send_a2, recv_a2, send_b2,
+         recv_b2, send_w, recv_w, local_sem) = refs
     else:
-        (win_ref, t_ref, t_out, rs_buf, red, op_buf, sec_buf, mid, mid_out, new_buf,
-         new_out, win_buf, send_rs, recv_rs, send_a, recv_a, send_b, recv_b, send_w,
+        (win_ref, got_ref, t_ref, t_out, rs_buf, red, op_buf, sec_buf, mid, mid_out,
+         new_buf, new_out, win_buf, send_rs, recv_rs, send_a, recv_a, send_b, recv_b, send_w,
          recv_w, local_sem) = refs
     me_sec = lax.axis_index("sec")
     me_op = lax.axis_index("op")
@@ -339,6 +339,10 @@
     a_args = (n_op, me_op, t_out, op_buf, send_a, recv_a, op_peer)
     start_gather(*a_args)
     rs_buf[me_op] = x_ref[me_op]
+
+    operators = copy_to(piece_ref, got_ref, send_w.at[send_w.shape[0] - 1],
+                        recv_w.at[recv_w.shape[0] - 1], (next_sec, me_op))
+    operators.start()
 
     wait_gather(*a_args)
     mid[...] = ordered_sum(op_buf, n_op)
@@ -402,7 +406,9 @@
         copy_to(new_out, win_buf.at[n_op + slot], send_w.at[0], recv_w.at[n_op + slot],
                 op_peer(slot)).wait_recv()
     win_ref[...] = win_buf[...]
-
+    operators.wait_recv()
+
+    operators.wait_send()
     for d in range(1, n_op):
         rs_copy(d).wait_send()
     drain_gather(*a_args)
@@ -415,7 +421,7 @@
                 op_peer((me_op + 1) % n_op)).wait_send()
 
 
-def step(partial, window, shift, count, final, n_sec, n_op):
+def step(partial, window, shift, piece, count, final, n_sec, n_op):
     shape = partial.shape
     rows = shape[0] * shape[1] // n_op
     chunks = partial.reshape(n_op, rows, shape[2])
@@ -450,22 +456,26 @@
         pltpu.SemaphoreType.DMA((n_sec,)),
         pltpu.SemaphoreType.DMA((n_sec,)),
     ] if final else []) + [
-        pltpu.SemaphoreType.DMA((slots + n_op,)),
-        pltpu.SemaphoreType.DMA((slots,)),
+        pltpu.SemaphoreType.DMA((slots + n_op + 1,)),
+        pltpu.SemaphoreType.DMA((slots + 1,)),
         pltpu.SemaphoreType.DMA((5,)),
     ]
     vmem = pl.BlockSpec(memory_space=pltpu.VMEM)
-    window = pl.pallas_call(
+    anywhere = pl.BlockSpec(memory_space=pl.ANY)
+    window, got = pl.pallas_call(
         functools.partial(step_kernel, n_sec, n_op, count, final),
-        out_shape=jax.ShapeDtypeStruct((slots, rows, shape[2]), jnp.bfloat16),
-        in_specs=[vmem, vmem, vmem],
-        out_specs=vmem,
+        out_shape=(
+            jax.ShapeDtypeStruct((slots, rows, shape[2]), jnp.bfloat16),
+            jax.ShapeDtypeStruct(piece.shape, piece.dtype),
+        ),
+        in_specs=[vmem, vmem, vmem, anywhere],
+        out_specs=(vmem, anywhere),
         scratch_shapes=scratch,
         compiler_params=pltpu.CompilerParams(
             collective_id=3 if final else 2, has_side_effects=True
         ),
-    )(chunks, state_chunks, shift_chunks)
-    return window.reshape(slots // (n_op // shape[0]), shape[1], shape[2])
+    )(chunks, state_chunks, shift_chunks, piece)
+    return window.reshape(slots // (n_op // shape[0]), shape[1], shape[2]), got
 
 
 def sigma_part_kernel(partner_ref, win_ref, left_ref, right_ref, o_ref):
@@ -515,16 +525,23 @@
     count = float(sector_local * lax.axis_size("sec") * width * width)
     n_sec = lax.axis_size("sec")
     n_op = lax.axis_size("op")
-    left_prev = shifted(left_ops, "sec", 1)
     kept_prev = shifted(kept, "sec", 1)
     state = state_start
     window = padded(state, (("sec", 0),), sector_local)
+    terms = left_ops.shape[0]
+    cuts = [terms * k // ITERS for k in range(ITERS + 1)]
+    left_pieces = []
     for iteration in range(ITERS):
         partial_sigma = sigma_part(window, left_ops, right_ops, partner)
         final = iteration == ITERS - 1
-        window = step(partial_sigma, window, shift, count, final, n_sec, n_op)
+        window, got = step(
+            partial_sigma, window, shift,
+            left_ops[cuts[iteration] : cuts[iteration + 1]], count, final, n_sec, n_op,
+        )
+        left_pieces.append(got)
         state = window[sector_local : 2 * sector_local]
     state_prev = window[:sector_local]
+    left_prev = jnp.concatenate(left_pieces, axis=0)
     columns = jnp.arange(width, dtype=jnp.int32)
     keep_mask = (columns[None, :] < kept_prev[:, None]).astype(jnp.bfloat16)
     kept_block = state_prev * keep_mask[:, None, :]

time: 238 us -> 203 us (0.85)
  waiting for transfers between devices: 48.3 us -> 1.88 us
  Pallas kernels: 171 us -> 180 us
    ppermute x2 -> x1, waiting for transfers between devices: 48.3 us -> 1.87 us  [shifted(): return lax.ppermute(block, axis, route)]
    pallas_call x4, Pallas kernels: 151 us -> 160 us  [step(): pl.pallas_call(functools.partial(step_kernel, n_sec, n_op, count, final),...]
    slice x0 -> x1, local copies, waits for them, and re-layouts: none -> 2.91 us  [per_device(): left_ops[cuts[iteration]:cuts[iteration + 1]]]
    ppermute x2 -> x1, starting transfers between devices: 2.55 us -> 0.01 us  [shifted(): return lax.ppermute(block, axis, route)]
  transfers between devices with their start and end apart: 4 -> 3, of which waited for: 1 -> 1; matrix products, arithmetic and copies ran while one was open for 2% -> 2% of each run, Pallas kernels for 72% -> 0%
where the time goes in v10:
time: 203 us; the launch traced here: 202 us
  Pallas kernels  180 us (89%)
  starting transfers between devices  8.77 us (4%)
  local copies, waits for them, and re-layouts  7.25 us (4%)
  matrix products  3.23 us (2%)
    pallas_call x4, Pallas kernels, step(): pl.pallas_call(functools.partial(step_kernel, n_sec, n_op, count, final),...  160 us
    pallas_call x4, Pallas kernels, sigma_part(): pl.pallas_call(sigma_part_kernel, out_shape=jax.ShapeDtypeStruct((sectors...  20 us
    ppermute x1, starting transfers between devices, padded(): lax.ppermute(head, axis, [((i + 1) % count, i) for i in range(count)])  6.22 us
  transfers between devices with their start and end apart: 3, of which 1 were waited for; matrix products, arithmetic and copies ran while one was open for 2% of the time, Pallas kernels for 0%

profile of v10, /device:TPU:1, one launch (start us, length us, event | category | flops | bytes accessed | tf_op | source)
XLA Modules:
  0.0 202.3 jit_solution(409007057731847950)
XLA Ops:
  0.7 2.5 %collective-permute-start = (bf16[2,256,256]{2,1,0:T(8,128)(2,1)}, bf16[2,256,256]{2,1,0:T(8,128)(2,1)S(1)}, u32[]{:S(2)}, u32[]{:S(2)}) collective-permute-start(bf16[2,256,256]{2,1,0:T(8,128)(2,1)} %param.6), channel_id=1, source_target_pairs={{0,8},{8,16},{16,24},{24,32},{32,40},{40,48},{48,56},{56,64},{64,7... | collective-permute-start | bytes 786440 | tf_op jit(solution)/shard_map/ppermute | solution.py:25
  3.2 6.2 %collective-permute-start.1 = (bf16[2,256,256]{2,1,0:T(8,128)(2,1)}, bf16[2,256,256]{2,1,0:T(8,128)(2,1)S(1)}, u32[]{:S(2)}, u32[]{:S(2)}) collective-permute-start(bf16[2,256,256]{2,1,0:T(8,128)(2,1)} %param.6), channel_id=1, source_target_pairs={{8,0},{16,8},{24,16},{32,24},{40,32},{48,40},{56,48},{64,56},{72,6... | collective-permute-start | bytes 786440 | tf_op jit(solution)/shard_map/ppermute | solution.py:27
  9.4 0.0 collective-permute-start.2
  9.4 2.9 %fusion.19 = (bf16[2,2,256,256]{3,2,1,0:T(8,128)(2,1)}, bf16[2,2,256,256]{3,2,1,0:T(8,128)(2,1)}, bf16[2,2,256,256]{3,2,1,0:T(8,128)(2,1)}, bf16[2,2,256,256]{3,2,1,0:T(8,128)(2,1)}) fusion(bf16[8,2,256,256]{3,2,1,0:T(8,128)(2,1)} %left_ref.7), kind=kLoop, calls=%fused_computation.19 | loop fusion | bytes 4194304 | tf_op jit(solution)/shard_map/slice | solution.py:539
  12.3 0.1 broadcast_in_dim.4
  12.4 0.7 broadcast_in_dim_reshape.3.sh_ref
  13.1 0.7 copy.14.partner_ref
  13.8 1.9 collective-permute-done.2
  15.6 0.1 compare_convert_fusion
  15.7 0.0 collective-permute-done
  15.8 0.0 collective-permute-done.1
  15.8 0.0 copy-start
  15.8 0.9 copy-done
  16.7 5.0 %shard_map.77 = f32[2,256,256]{2,1,0:T(8,128)} custom-call(s32[8,2]{1,0:T(8,128)} %copy.14.partner_ref, bf16[6,256,256]{2,1,0:T(8,128)(2,1)} %copy-done, bf16[8,2,256,256]{3,2,1,0:T(8,128)(2,1)} %left_ref.7, bf16[8,2,256,256]{3,2,1,0:T(8,128)(2,1)} %right_ref.7), custom_call_target="tpu_custom_call" | custom-call | flops 1073741824 | bytes 5505024 | tf_op jit(solution)/shard_map/pallas_call | solution.py:495
  21.7 39.2 %shard_map.78 = (bf16[24,64,256]{2,1,0:T(8,128)(2,1)}, bf16[2,2,256,256]{3,2,1,0:T(8,128)(2,1)}) custom-call(f32[8,64,256]{2,1,0:T(8,128)} %bitcast.31, bf16[24,64,256]{2,1,0:T(8,128)(2,1)} %bitcast.24, f32[8,1,1]{2,1,0:T(1,128)} %broadcast_in_dim_reshape.3.sh_ref, bf16[2,2,256,256]{3,2,1,0:T(8,128)(2,1)} %get-tuple-element.21.piece_ref), custom_call_target="tpu_custom_call" | custom-call | tf_op jit(solution)/shard_map/pallas_call | solution.py:465
  60.9 5.0 %shard_map.79 = f32[2,256,256]{2,1,0:T(8,128)} custom-call(s32[8,2]{1,0:T(8,128)} %copy.14.partner_ref, bf16[6,256,256]{2,1,0:T(8,128)(2,1)} %bitcast.26, bf16[8,2,256,256]{3,2,1,0:T(8,128)(2,1)} %left_ref.7, bf16[8,2,256,256]{3,2,1,0:T(8,128)(2,1)} %right_ref.7), custom_call_target="tpu_custom_call" | custom-call | flops 1073741824 | bytes 5505024 | tf_op jit(solution)/shard_map/pallas_call | solution.py:495
  65.9 37.9 %shard_map.80 = (bf16[24,64,256]{2,1,0:T(8,128)(2,1)}, bf16[2,2,256,256]{3,2,1,0:T(8,128)(2,1)}) custom-call(f32[8,64,256]{2,1,0:T(8,128)} %bitcast.32, bf16[24,64,256]{2,1,0:T(8,128)(2,1)} %get-tuple-element.10.st_ref, f32[8,1,1]{2,1,0:T(1,128)} %broadcast_in_dim_reshape.3.sh_ref, bf16[2,2,256,256]{3,2,1,0:T(8,128)(2,1)} %get-tuple-element.20.piece_ref), custom_call_target="tpu_custom_call" | custom-call | tf_op jit(solution)/shard_map/pallas_call | solution.py:465
  103.9 5.0 %shard_map.81 = f32[2,256,256]{2,1,0:T(8,128)} custom-call(s32[8,2]{1,0:T(8,128)} %copy.14.partner_ref, bf16[6,256,256]{2,1,0:T(8,128)(2,1)} %bitcast.27, bf16[8,2,256,256]{3,2,1,0:T(8,128)(2,1)} %left_ref.7, bf16[8,2,256,256]{3,2,1,0:T(8,128)(2,1)} %right_ref.7), custom_call_target="tpu_custom_call" | custom-call | flops 1073741824 | bytes 5505024 | tf_op jit(solution)/shard_map/pallas_call | solution.py:495
  108.9 36.5 %shard_map.82 = (bf16[24,64,256]{2,1,0:T(8,128)(2,1)}, bf16[2,2,256,256]{3,2,1,0:T(8,128)(2,1)}) custom-call(f32[8,64,256]{2,1,0:T(8,128)} %bitcast.33, bf16[24,64,256]{2,1,0:T(8,128)(2,1)} %get-tuple-element.11.st_ref, f32[8,1,1]{2,1,0:T(1,128)} %broadcast_in_dim_reshape.3.sh_ref, bf16[2,2,256,256]{3,2,1,0:T(8,128)(2,1)} %get-tuple-element.19.piece_ref), custom_call_target="tpu_custom_call" | custom-call | tf_op jit(solution)/shard_map/pallas_call | solution.py:465
  145.4 5.0 %shard_map.83 = f32[2,256,256]{2,1,0:T(8,128)} custom-call(s32[8,2]{1,0:T(8,128)} %copy.14.partner_ref, bf16[6,256,256]{2,1,0:T(8,128)(2,1)} %bitcast.25, bf16[8,2,256,256]{3,2,1,0:T(8,128)(2,1)} %left_ref.7, bf16[8,2,256,256]{3,2,1,0:T(8,128)(2,1)} %right_ref.7), custom_call_target="tpu_custom_call" | custom-call | flops 1073741824 | bytes 5505024 | tf_op jit(solution)/shard_map/pallas_call | solution.py:495
  150.4 46.5 %shard_map.84 = (bf16[16,64,256]{2,1,0:T(8,128)(2,1)}, bf16[2,2,256,256]{3,2,1,0:T(8,128)(2,1)}) custom-call(f32[8,64,256]{2,1,0:T(8,128)} %bitcast.30, bf16[24,64,256]{2,1,0:T(8,128)(2,1)} %get-tuple-element.12.st_ref, f32[8,1,1]{2,1,0:T(1,128)} %broadcast_in_dim_reshape.3.sh_ref, bf16[2,2,256,256]{3,2,1,0:T(8,128)(2,1)} %get-tuple-element.18.piece_ref), custom_call_target="tpu_custom_call" | custom-call | tf_op jit(solution)/shard_map/pallas_call | solution.py:465
  197.0 1.8 fusion.20
  198.9 0.1 copy.16
  199.0 3.2 %multiply_convert_fusion = bf16[8,2,256,256]{3,2,1,0:T(8,128)(2,1)} fusion(bf16[2,2,256,256]{3,2,1,0:T(8,128)(2,1)S(1)} %copy-done.6, bf16[2,2,256,256]{3,2,1,0:T(8,128)(2,1)S(1)} %copy-done.5, bf16[2,2,256,256]{3,2,1,0:T(8,128)(2,1)S(1)} %copy-done.4, bf16[2,2,256,256]{3,2,1,0:T(8,128)(2,1)S(1)} %copy-done.3, bf16[2,256,256]{2,1,0:T(8,128)(2,1)S(1)} %copy.16, ...), kind=kOutput, calls=%fused_computation | convolution fusion | flops 1085276160 | bytes 4718592 | tf_op jit(solution)/shard_map/tbij,tbjk->tbik/dot_general | solution.py:556
  (19 shorter events, 0.1 us)
Async XLA Ops:
  0.6 15.1 %copy-start.1 = (bf16[2,256,256]{2,1,0:T(8,128)(2,1)S(1)}, bf16[2,256,256]{2,1,0:T(8,128)(2,1)}, u32[]{:S(2)}) copy-start(bf16[2,256,256]{2,1,0:T(8,128)(2,1)} %param.6) | copy-start | bytes 786436
  0.6 11.7 %copy-start.7 = (f32[2]{0:T(128)S(1)}, f32[2]{0:T(128)}, u32[]{:S(2)}) copy-start(f32[2]{0:T(128)} %param.9) | copy-start | bytes 28
  0.7 12.4 %copy-start.2 = (s32[8,2]{0,1:T(2,128)S(1)}, s32[8,2]{0,1:T(2,128)}, u32[]{:S(2)}) copy-start(s32[8,2]{0,1:T(2,128)} %param.10) | copy-start | bytes 196
  0.7 15.0 %collective-permute-start = (bf16[2,256,256]{2,1,0:T(8,128)(2,1)}, bf16[2,256,256]{2,1,0:T(8,128)(2,1)S(1)}, u32[]{:S(2)}, u32[]{:S(2)}) collective-permute-start(bf16[2,256,256]{2,1,0:T(8,128)(2,1)} %param.6), channel_id=1, source_target_pairs={{0,8},{8,16},{16,24},{24,32},{32,40},{40,48},{48,56},{56,64},{64,7... | collective-permute-start | bytes 786440 | tf_op jit(solution)/shard_map/ppermute | solution.py:25
  3.2 12.6 %collective-permute-start.1 = (bf16[2,256,256]{2,1,0:T(8,128)(2,1)}, bf16[2,256,256]{2,1,0:T(8,128)(2,1)S(1)}, u32[]{:S(2)}, u32[]{:S(2)}) collective-permute-start(bf16[2,256,256]{2,1,0:T(8,128)(2,1)} %param.6), channel_id=1, source_target_pairs={{8,0},{16,8},{24,16},{32,24},{40,32},{48,40},{56,48},{64,56},{72,6... | collective-permute-start | bytes 786440 | tf_op jit(solution)/shard_map/ppermute | solution.py:27
  9.4 6.2 %collective-permute-start.2 = (s32[2]{0:T(128)}, s32[2]{0:T(128)S(1)}, u32[]{:S(2)}, u32[]{:S(2)}) collective-permute-start(s32[2]{0:T(128)} %param.11), channel_id=1, source_target_pairs={{248,0},{0,8},{8,16},{16,24},{24,32},{32,40},{40,48},{48,56},{56,6... | collective-permute-start | bytes 32 | tf_op jit(solution)/shard_map/ppermute | solution.py:519
  15.8 0.9 copy-start
  150.4 48.6 %copy-start.3 = (bf16[2,2,256,256]{3,2,1,0:T(8,128)(2,1)S(1)}, bf16[2,2,256,256]{3,2,1,0:T(8,128)(2,1)}, u32[]{:S(2)}) copy-start(bf16[2,2,256,256]{3,2,1,0:T(8,128)(2,1)} %get-tuple-element.14) | copy-start | bytes 1572868
  150.4 48.6 %copy-start.4 = (bf16[2,2,256,256]{3,2,1,0:T(8,128)(2,1)S(1)}, bf16[2,2,256,256]{3,2,1,0:T(8,128)(2,1)}, u32[]{:S(2)}) copy-start(bf16[2,2,256,256]{3,2,1,0:T(8,128)(2,1)} %get-tuple-element.15) | copy-start | bytes 1572868
  150.4 48.6 %copy-start.5 = (bf16[2,2,256,256]{3,2,1,0:T(8,128)(2,1)S(1)}, bf16[2,2,256,256]{3,2,1,0:T(8,128)(2,1)}, u32[]{:S(2)}) copy-start(bf16[2,2,256,256]{3,2,1,0:T(8,128)(2,1)} %get-tuple-element.16) | copy-start | bytes 1572868
  197.0 2.1 %copy-start.6 = (bf16[2,2,256,256]{3,2,1,0:T(8,128)(2,1)S(1)}, bf16[2,2,256,256]{3,2,1,0:T(8,128)(2,1)}, u32[]{:S(2)}) copy-start(bf16[2,2,256,256]{3,2,1,0:T(8,128)(2,1)} %get-tuple-element.17) | copy-start | bytes 1572868

commit v11 on v10

--- a/solution.py
+++ b/solution.py
@@ -255,31 +255,29 @@
     if final:
         (win_ref, got_ref, t_ref, t_out, rs_buf, red, op_buf, sec_buf, mid, mid_out,
          op_buf2, sec_buf2, mid2, mid2_out, mid3, mid3_out, new_buf, new_out, win_buf,
+         part, part_out, part2, part2_out,
          send_rs, recv_rs, send_a, recv_a, send_b, recv_b, send_a2, recv_a2, send_b2,
          recv_b2, send_w, recv_w, local_sem) = refs
     else:
         (win_ref, got_ref, t_ref, t_out, rs_buf, red, op_buf, sec_buf, mid, mid_out,
-         new_buf, new_out, win_buf, send_rs, recv_rs, send_a, recv_a, send_b, recv_b, send_w,
+         new_buf, new_out, win_buf, part, part_out, send_rs, recv_rs, send_a, recv_a, send_b, recv_b, send_w,
          recv_w, local_sem) = refs
     me_sec = lax.axis_index("sec")
     me_op = lax.axis_index("op")
     prev_sec = (me_sec + n_sec - 1) % n_sec
     next_sec = (me_sec + 1) % n_sec
     barrier = pltpu.get_barrier_semaphore()
-    greeted = 0
-    for d in range(1, n_op):
-        pl.semaphore_signal(barrier, 1, device_id=(me_sec, (me_op + d) % n_op),
-                            device_id_type=MESH)
-        greeted += 1
-    for d in range(1, n_sec):
-        pl.semaphore_signal(barrier, 1, device_id=((me_sec + d) % n_sec, me_op),
-                            device_id_type=MESH)
-        greeted += 1
-    for side in (prev_sec, next_sec):
-        for d in range(1, n_op):
-            pl.semaphore_signal(barrier, 1, device_id=(side, (me_op + d) % n_op),
-                                device_id_type=MESH)
-            greeted += 1
+    row_len = 8 if n_sec % 8 == 0 else (2 if n_sec % 2 == 0 else n_sec)
+    n_rows = n_sec // row_len
+    row = me_sec // row_len
+    col = me_sec % row_len
+    greet = [(me_sec, (me_op + d) % n_op) for d in range(1, n_op)]
+    greet += [(row * row_len + (col + d) % row_len, me_op) for d in range(1, row_len)]
+    greet += [(((row + d) % n_rows) * row_len + col, me_op) for d in range(1, n_rows)]
+    greet += [(side, j) for side in (prev_sec, next_sec) for j in range(n_op)]
+    for peer in greet:
+        pl.semaphore_signal(barrier, 1, device_id=peer, device_id_type=MESH)
+    greeted = len(greet)
     pl.semaphore_wait(barrier, greeted)
 
     def op_peer(j):
@@ -330,6 +328,45 @@
     t_ref[...] = jnp.where(lane == 0, energy, jnp.where(lane == 1, own_square, 0.0))
     settle(t_ref, t_out, local_sem.at[4])
 
+    def row_peer(c):
+        return (row * row_len + c, me_op)
+
+    def col_peer(r):
+        return (r * row_len + col, me_op)
+
+    def start_rows(src, buf, send, recv):
+        for d in range(1, row_len):
+            copy_to(src, buf.at[col], send.at[d], recv.at[col],
+                    row_peer((col + d) % row_len)).start()
+        buf[col] = src[...]
+
+    def finish_sec(src, buf, send, recv, mid_sum, mid_out, sem):
+        for d in range(1, row_len):
+            slot = (col + row_len - d) % row_len
+            copy_to(src, buf.at[slot], send.at[d], recv.at[slot], row_peer(slot)).wait_recv()
+        mid_sum[...] = ordered_sum(buf, row_len)
+        settle(mid_sum, mid_out, sem)
+        for d in range(1, n_rows):
+            copy_to(mid_out, buf.at[row_len + row], send.at[row_len + d],
+                    recv.at[row_len + row], col_peer((row + d) % n_rows)).start()
+        buf[row_len + row] = mid_out[...]
+        for d in range(1, n_rows):
+            slot = (row + n_rows - d) % n_rows
+            copy_to(mid_out, buf.at[row_len + slot], send.at[row_len + d],
+                    recv.at[row_len + slot], col_peer(slot)).wait_recv()
+        total = buf[row_len]
+        for r in range(1, n_rows):
+            total = total + buf[row_len + r]
+        return total
+
+    def drain_sec(src, buf, send, recv, mid_out):
+        for d in range(1, row_len):
+            copy_to(src, buf.at[col], send.at[d], recv.at[col],
+                    row_peer((col + d) % row_len)).wait_send()
+        for d in range(1, n_rows):
+            copy_to(mid_out, buf.at[row_len + row], send.at[row_len + d],
+                    recv.at[row_len + row], col_peer((row + d) % n_rows)).wait_send()
+
     def rs_copy(d):
         j = (me_op + d) % n_op
         return copy_to(x_ref.at[j], rs_buf.at[me_op], send_rs.at[d], recv_rs.at[me_op], op_peer(j))
@@ -347,8 +384,7 @@
     wait_gather(*a_args)
     mid[...] = ordered_sum(op_buf, n_op)
     settle(mid, mid_out, local_sem.at[0])
-    b_args = (n_sec, me_sec, mid_out, sec_buf, send_b, recv_b, sec_peer)
-    start_gather(*b_args)
+    start_rows(mid_out, sec_buf, send_b, recv_b)
 
     for d in range(1, n_op):
         slot = (me_op + n_op - d) % n_op
@@ -356,8 +392,7 @@
                 op_peer(slot)).wait_recv()
     red[...] = ordered_sum(rs_buf, n_op)
 
-    wait_gather(*b_args)
-    sums = ordered_sum(sec_buf, n_sec)
+    sums = finish_sec(mid_out, sec_buf, send_b, recv_b, part, part_out, local_sem.at[5])
     energy_sum = sums[0:1, 0:1]
     norm_sum = sums[0:1, 1:2]
     state_wide = st_ref[n_op + me_op].astype(jnp.float32)
@@ -372,10 +407,9 @@
         wait_gather(*a2_args)
         mid3[...] = ordered_sum(op_buf2, n_op)
         settle(mid3, mid3_out, local_sem.at[3])
-        b2_args = (n_sec, me_sec, mid3_out, sec_buf2, send_b2, recv_b2, sec_peer)
-        start_gather(*b2_args)
-        wait_gather(*b2_args)
-        new_norm = ordered_sum(sec_buf2, n_sec)[0:1, 0:1]
+        start_rows(mid3_out, sec_buf2, send_b2, recv_b2)
+        new_norm = finish_sec(mid3_out, sec_buf2, send_b2, recv_b2, part2, part2_out,
+                              local_sem.at[6])[0:1, 0:1]
         factor = jnp.sqrt(count / new_norm)
     else:
         factor = jnp.sqrt(count / norm_sum)
@@ -412,10 +446,10 @@
     for d in range(1, n_op):
         rs_copy(d).wait_send()
     drain_gather(*a_args)
-    drain_gather(*b_args)
+    drain_sec(mid_out, sec_buf, send_b, recv_b, part_out)
     if final:
         drain_gather(*a2_args)
-        drain_gather(*b2_args)
+        drain_sec(mid3_out, sec_buf2, send_b2, recv_b2, part2_out)
     for k in range(sent):
         copy_to(new_out, win_buf.at[n_op + me_op], send_w.at[k], recv_w.at[n_op + me_op],
                 op_peer((me_op + 1) % n_op)).wait_send()
@@ -444,6 +478,7 @@
         pltpu.VMEM(tile_shape, jnp.bfloat16),
         pltpu.VMEM(tile_shape, jnp.bfloat16),
         pltpu.VMEM((slots, rows, shape[2]), jnp.bfloat16),
+    ] + [pltpu.VMEM((8, 128), jnp.float32)] * (4 if final else 2) + [
         pltpu.SemaphoreType.DMA((n_op,)),
         pltpu.SemaphoreType.DMA((n_op,)),
         pltpu.SemaphoreType.DMA((n_op,)),
@@ -458,7 +493,7 @@
     ] if final else []) + [
         pltpu.SemaphoreType.DMA((slots + n_op + 1,)),
         pltpu.SemaphoreType.DMA((slots + 1,)),
-        pltpu.SemaphoreType.DMA((5,)),
+        pltpu.SemaphoreType.DMA((7,)),
     ]
     vmem = pl.BlockSpec(memory_space=pltpu.VMEM)
     anywhere = pl.BlockSpec(memory_space=pl.ANY)

time: 203 us -> 201 us (level)
  no operation moved by 1% of the time
where the time goes in v11:
time: 201 us; the launch traced here: 200 us
  Pallas kernels  178 us (89%)
  starting transfers between devices  8.77 us (4%)
  local copies, waits for them, and re-layouts  7.25 us (4%)
  matrix products  3.23 us (2%)
    pallas_call x4, Pallas kernels, step(): pl.pallas_call(functools.partial(step_kernel, n_sec, n_op, count, final),...  158 us
    pallas_call x4, Pallas kernels, sigma_part(): pl.pallas_call(sigma_part_kernel, out_shape=jax.ShapeDtypeStruct((sectors...  20 us
    ppermute x1, starting transfers between devices, padded(): lax.ppermute(head, axis, [((i + 1) % count, i) for i in range(count)])  6.22 us
  transfers between devices with their start and end apart: 3, of which 1 were waited for; matrix products, arithmetic and copies ran while one was open for 2% of the time, Pallas kernels for 0%

profile of v11, /device:TPU:1, one launch (start us, length us, event | category | flops | bytes accessed | tf_op | source)
XLA Modules:
  0.0 200.4 jit_solution(9248174889880468163)
XLA Ops:
  0.7 2.5 %collective-permute-start = (bf16[2,256,256]{2,1,0:T(8,128)(2,1)}, bf16[2,256,256]{2,1,0:T(8,128)(2,1)S(1)}, u32[]{:S(2)}, u32[]{:S(2)}) collective-permute-start(bf16[2,256,256]{2,1,0:T(8,128)(2,1)} %param.6), channel_id=1, source_target_pairs={{0,8},{8,16},{16,24},{24,32},{32,40},{40,48},{48,56},{56,64},{64,7... | collective-permute-start | bytes 786440 | tf_op jit(solution)/shard_map/ppermute | solution.py:25
  3.2 6.2 %collective-permute-start.1 = (bf16[2,256,256]{2,1,0:T(8,128)(2,1)}, bf16[2,256,256]{2,1,0:T(8,128)(2,1)S(1)}, u32[]{:S(2)}, u32[]{:S(2)}) collective-permute-start(bf16[2,256,256]{2,1,0:T(8,128)(2,1)} %param.6), channel_id=1, source_target_pairs={{8,0},{16,8},{24,16},{32,24},{40,32},{48,40},{56,48},{64,56},{72,6... | collective-permute-start | bytes 786440 | tf_op jit(solution)/shard_map/ppermute | solution.py:27
  9.4 0.0 collective-permute-start.2
  9.4 2.9 %fusion.19 = (bf16[2,2,256,256]{3,2,1,0:T(8,128)(2,1)}, bf16[2,2,256,256]{3,2,1,0:T(8,128)(2,1)}, bf16[2,2,256,256]{3,2,1,0:T(8,128)(2,1)}, bf16[2,2,256,256]{3,2,1,0:T(8,128)(2,1)}) fusion(bf16[8,2,256,256]{3,2,1,0:T(8,128)(2,1)} %left_ref.7), kind=kLoop, calls=%fused_computation.19 | loop fusion | bytes 4194304 | tf_op jit(solution)/shard_map/slice | solution.py:574
  12.3 0.1 broadcast_in_dim.4
  12.4 0.7 broadcast_in_dim_reshape.3.sh_ref
  13.1 0.7 copy.14.partner_ref
  13.8 1.9 collective-permute-done.2
  15.6 0.1 compare_convert_fusion
  15.7 0.0 collective-permute-done
  15.8 0.0 collective-permute-done.1
  15.8 0.0 copy-start
  15.8 0.9 copy-done
  16.7 5.0 %shard_map.77 = f32[2,256,256]{2,1,0:T(8,128)} custom-call(s32[8,2]{1,0:T(8,128)} %copy.14.partner_ref, bf16[6,256,256]{2,1,0:T(8,128)(2,1)} %copy-done, bf16[8,2,256,256]{3,2,1,0:T(8,128)(2,1)} %left_ref.7, bf16[8,2,256,256]{3,2,1,0:T(8,128)(2,1)} %right_ref.7), custom_call_target="tpu_custom_call" | custom-call | flops 1073741824 | bytes 5505024 | tf_op jit(solution)/shard_map/pallas_call | solution.py:530
  21.7 39.0 %shard_map.78 = (bf16[24,64,256]{2,1,0:T(8,128)(2,1)}, bf16[2,2,256,256]{3,2,1,0:T(8,128)(2,1)}) custom-call(f32[8,64,256]{2,1,0:T(8,128)} %bitcast.31, bf16[24,64,256]{2,1,0:T(8,128)(2,1)} %bitcast.24, f32[8,1,1]{2,1,0:T(1,128)} %broadcast_in_dim_reshape.3.sh_ref, bf16[2,2,256,256]{3,2,1,0:T(8,128)(2,1)} %get-tuple-element.21.piece_ref), custom_call_target="tpu_custom_call" | custom-call | tf_op jit(solution)/shard_map/pallas_call | solution.py:500
  60.7 5.0 %shard_map.79 = f32[2,256,256]{2,1,0:T(8,128)} custom-call(s32[8,2]{1,0:T(8,128)} %copy.14.partner_ref, bf16[6,256,256]{2,1,0:T(8,128)(2,1)} %bitcast.26, bf16[8,2,256,256]{3,2,1,0:T(8,128)(2,1)} %left_ref.7, bf16[8,2,256,256]{3,2,1,0:T(8,128)(2,1)} %right_ref.7), custom_call_target="tpu_custom_call" | custom-call | flops 1073741824 | bytes 5505024 | tf_op jit(solution)/shard_map/pallas_call | solution.py:530
  65.7 37.0 %shard_map.80 = (bf16[24,64,256]{2,1,0:T(8,128)(2,1)}, bf16[2,2,256,256]{3,2,1,0:T(8,128)(2,1)}) custom-call(f32[8,64,256]{2,1,0:T(8,128)} %bitcast.32, bf16[24,64,256]{2,1,0:T(8,128)(2,1)} %get-tuple-element.10.st_ref, f32[8,1,1]{2,1,0:T(1,128)} %broadcast_in_dim_reshape.3.sh_ref, bf16[2,2,256,256]{3,2,1,0:T(8,128)(2,1)} %get-tuple-element.20.piece_ref), custom_call_target="tpu_custom_call" | custom-call | tf_op jit(solution)/shard_map/pallas_call | solution.py:500
  102.7 5.0 %shard_map.81 = f32[2,256,256]{2,1,0:T(8,128)} custom-call(s32[8,2]{1,0:T(8,128)} %copy.14.partner_ref, bf16[6,256,256]{2,1,0:T(8,128)(2,1)} %bitcast.27, bf16[8,2,256,256]{3,2,1,0:T(8,128)(2,1)} %left_ref.7, bf16[8,2,256,256]{3,2,1,0:T(8,128)(2,1)} %right_ref.7), custom_call_target="tpu_custom_call" | custom-call | flops 1073741824 | bytes 5505024 | tf_op jit(solution)/shard_map/pallas_call | solution.py:530
  107.7 35.9 %shard_map.82 = (bf16[24,64,256]{2,1,0:T(8,128)(2,1)}, bf16[2,2,256,256]{3,2,1,0:T(8,128)(2,1)}) custom-call(f32[8,64,256]{2,1,0:T(8,128)} %bitcast.33, bf16[24,64,256]{2,1,0:T(8,128)(2,1)} %get-tuple-element.11.st_ref, f32[8,1,1]{2,1,0:T(1,128)} %broadcast_in_dim_reshape.3.sh_ref, bf16[2,2,256,256]{3,2,1,0:T(8,128)(2,1)} %get-tuple-element.19.piece_ref), custom_call_target="tpu_custom_call" | custom-call | tf_op jit(solution)/shard_map/pallas_call | solution.py:500
  143.6 5.0 %shard_map.83 = f32[2,256,256]{2,1,0:T(8,128)} custom-call(s32[8,2]{1,0:T(8,128)} %copy.14.partner_ref, bf16[6,256,256]{2,1,0:T(8,128)(2,1)} %bitcast.25, bf16[8,2,256,256]{3,2,1,0:T(8,128)(2,1)} %left_ref.7, bf16[8,2,256,256]{3,2,1,0:T(8,128)(2,1)} %right_ref.7), custom_call_target="tpu_custom_call" | custom-call | flops 1073741824 | bytes 5505024 | tf_op jit(solution)/shard_map/pallas_call | solution.py:530
  148.7 46.5 %shard_map.84 = (bf16[16,64,256]{2,1,0:T(8,128)(2,1)}, bf16[2,2,256,256]{3,2,1,0:T(8,128)(2,1)}) custom-call(f32[8,64,256]{2,1,0:T(8,128)} %bitcast.30, bf16[24,64,256]{2,1,0:T(8,128)(2,1)} %get-tuple-element.12.st_ref, f32[8,1,1]{2,1,0:T(1,128)} %broadcast_in_dim_reshape.3.sh_ref, bf16[2,2,256,256]{3,2,1,0:T(8,128)(2,1)} %get-tuple-element.18.piece_ref), custom_call_target="tpu_custom_call" | custom-call | tf_op jit(solution)/shard_map/pallas_call | solution.py:500
  195.1 1.8 fusion.20
  197.0 0.1 copy.16
  197.2 3.2 %multiply_convert_fusion = bf16[8,2,256,256]{3,2,1,0:T(8,128)(2,1)} fusion(bf16[2,2,256,256]{3,2,1,0:T(8,128)(2,1)S(1)} %copy-done.6, bf16[2,2,256,256]{3,2,1,0:T(8,128)(2,1)S(1)} %copy-done.5, bf16[2,2,256,256]{3,2,1,0:T(8,128)(2,1)S(1)} %copy-done.4, bf16[2,2,256,256]{3,2,1,0:T(8,128)(2,1)S(1)} %copy-done.3, bf16[2,256,256]{2,1,0:T(8,128)(2,1)S(1)} %copy.16, ...), kind=kOutput, calls=%fused_computation | convolution fusion | flops 1085276160 | bytes 4718592 | tf_op jit(solution)/shard_map/tbij,tbjk->tbik/dot_general | solution.py:591
  (19 shorter events, 0.1 us)
Async XLA Ops:
  0.6 15.1 %copy-start.1 = (bf16[2,256,256]{2,1,0:T(8,128)(2,1)S(1)}, bf16[2,256,256]{2,1,0:T(8,128)(2,1)}, u32[]{:S(2)}) copy-start(bf16[2,256,256]{2,1,0:T(8,128)(2,1)} %param.6) | copy-start | bytes 786436
  0.6 11.7 %copy-start.7 = (f32[2]{0:T(128)S(1)}, f32[2]{0:T(128)}, u32[]{:S(2)}) copy-start(f32[2]{0:T(128)} %param.9) | copy-start | bytes 28
  0.7 12.4 %copy-start.2 = (s32[8,2]{0,1:T(2,128)S(1)}, s32[8,2]{0,1:T(2,128)}, u32[]{:S(2)}) copy-start(s32[8,2]{0,1:T(2,128)} %param.10) | copy-start | bytes 196
  0.7 15.0 %collective-permute-start = (bf16[2,256,256]{2,1,0:T(8,128)(2,1)}, bf16[2,256,256]{2,1,0:T(8,128)(2,1)S(1)}, u32[]{:S(2)}, u32[]{:S(2)}) collective-permute-start(bf16[2,256,256]{2,1,0:T(8,128)(2,1)} %param.6), channel_id=1, source_target_pairs={{0,8},{8,16},{16,24},{24,32},{32,40},{40,48},{48,56},{56,64},{64,7... | collective-permute-start | bytes 786440 | tf_op jit(solution)/shard_map/ppermute | solution.py:25
  3.2 12.6 %collective-permute-start.1 = (bf16[2,256,256]{2,1,0:T(8,128)(2,1)}, bf16[2,256,256]{2,1,0:T(8,128)(2,1)S(1)}, u32[]{:S(2)}, u32[]{:S(2)}) collective-permute-start(bf16[2,256,256]{2,1,0:T(8,128)(2,1)} %param.6), channel_id=1, source_target_pairs={{8,0},{16,8},{24,16},{32,24},{40,32},{48,40},{56,48},{64,56},{72,6... | collective-permute-start | bytes 786440 | tf_op jit(solution)/shard_map/ppermute | solution.py:27
  9.4 6.2 %collective-permute-start.2 = (s32[2]{0:T(128)}, s32[2]{0:T(128)S(1)}, u32[]{:S(2)}, u32[]{:S(2)}) collective-permute-start(s32[2]{0:T(128)} %param.11), channel_id=1, source_target_pairs={{248,0},{0,8},{8,16},{16,24},{24,32},{32,40},{40,48},{48,56},{56,6... | collective-permute-start | bytes 32 | tf_op jit(solution)/shard_map/ppermute | solution.py:554
  15.8 0.9 copy-start
  148.6 48.5 %copy-start.3 = (bf16[2,2,256,256]{3,2,1,0:T(8,128)(2,1)S(1)}, bf16[2,2,256,256]{3,2,1,0:T(8,128)(2,1)}, u32[]{:S(2)}) copy-start(bf16[2,2,256,256]{3,2,1,0:T(8,128)(2,1)} %get-tuple-element.14) | copy-start | bytes 1572868
  148.6 48.5 %copy-start.4 = (bf16[2,2,256,256]{3,2,1,0:T(8,128)(2,1)S(1)}, bf16[2,2,256,256]{3,2,1,0:T(8,128)(2,1)}, u32[]{:S(2)}) copy-start(bf16[2,2,256,256]{3,2,1,0:T(8,128)(2,1)} %get-tuple-element.15) | copy-start | bytes 1572868
  148.6 48.5 %copy-start.5 = (bf16[2,2,256,256]{3,2,1,0:T(8,128)(2,1)S(1)}, bf16[2,2,256,256]{3,2,1,0:T(8,128)(2,1)}, u32[]{:S(2)}) copy-start(bf16[2,2,256,256]{3,2,1,0:T(8,128)(2,1)} %get-tuple-element.16) | copy-start | bytes 1572868
  195.1 2.1 %copy-start.6 = (bf16[2,2,256,256]{3,2,1,0:T(8,128)(2,1)S(1)}, bf16[2,2,256,256]{3,2,1,0:T(8,128)(2,1)}, u32[]{:S(2)}) copy-start(bf16[2,2,256,256]{3,2,1,0:T(8,128)(2,1)} %get-tuple-element.17) | copy-start | bytes 1572868

commit v12 on v11

--- a/solution.py
+++ b/solution.py
@@ -398,8 +398,27 @@
     state_wide = st_ref[n_op + me_op].astype(jnp.float32)
     sigma = red[...] + sh_ref[me_op] * state_wide
     updated = state_wide - step_size * (sigma - (energy_sum / norm_sum) * state_wide)
+    factor = jnp.sqrt(count / norm_sum)
     if final:
         square = total_of(updated * updated)
+    new_buf[...] = (updated * factor).astype(new_buf.dtype)
+    settle(new_buf, new_out, local_sem.at[2])
+
+    sides = ((next_sec, 0),) if final else ((next_sec, 0), (prev_sec, 2 * n_op))
+    sent = 0
+    for side, base in sides:
+        for j in range(n_op):
+            copy_to(new_out, win_buf.at[base + me_op], send_w.at[sent],
+                    recv_w.at[base + me_op], (side, j)).start()
+            sent += 1
+    for d in range(1, n_op):
+        j = (me_op + d) % n_op
+        copy_to(new_out, win_buf.at[n_op + me_op], send_w.at[sent],
+                recv_w.at[n_op + me_op], op_peer(j)).start()
+        sent += 1
+    win_buf[n_op + me_op] = new_out[...]
+
+    if final:
         mid2[...] = jnp.where(lane == 0, square, 0.0)
         settle(mid2, mid2_out, local_sem.at[1])
         a2_args = (n_op, me_op, mid2_out, op_buf2, send_a2, recv_a2, op_peer)
@@ -410,25 +429,7 @@
         start_rows(mid3_out, sec_buf2, send_b2, recv_b2)
         new_norm = finish_sec(mid3_out, sec_buf2, send_b2, recv_b2, part2, part2_out,
                               local_sem.at[6])[0:1, 0:1]
-        factor = jnp.sqrt(count / new_norm)
-    else:
-        factor = jnp.sqrt(count / norm_sum)
-    new_buf[...] = (updated * factor).astype(new_buf.dtype)
-    settle(new_buf, new_out, local_sem.at[2])
-
-    sides = ((next_sec, 0),) if final else ((next_sec, 0), (prev_sec, 2 * n_op))
-    sent = 0
-    for side, base in sides:
-        for j in range(n_op):
-            copy_to(new_out, win_buf.at[base + me_op], send_w.at[sent],
-                    recv_w.at[base + me_op], (side, j)).start()
-            sent += 1
-    for d in range(1, n_op):
-        j = (me_op + d) % n_op
-        copy_to(new_out, win_buf.at[n_op + me_op], send_w.at[sent],
-                recv_w.at[n_op + me_op], op_peer(j)).start()
-        sent += 1
-    win_buf[n_op + me_op] = new_out[...]
+        rescale = jnp.sqrt(count / new_norm) / factor
 
     from_sides = ((prev_sec, 0),) if final else ((prev_sec, 0), (next_sec, 2 * n_op))
     for side, base in from_sides:
@@ -439,7 +440,11 @@
         slot = (me_op + n_op - d) % n_op
         copy_to(new_out, win_buf.at[n_op + slot], send_w.at[0], recv_w.at[n_op + slot],
                 op_peer(slot)).wait_recv()
-    win_ref[...] = win_buf[...]
+    if final:
+        for k in range(win_ref.shape[0]):
+            win_ref[k] = (win_buf[k].astype(jnp.float32) * rescale).astype(win_ref.dtype)
+    else:
+        win_ref[...] = win_buf[...]
     operators.wait_recv()
 
     operators.wait_send()

time: 201 us -> 195 us (0.970)
  Pallas kernels: 178 us -> 173 us
    pallas_call x4, Pallas kernels: 158 us -> 153 us  [step(): pl.pallas_call(functools.partial(step_kernel, n_sec, n_op, count, final),...]
where the time goes in v12:
time: 195 us
  Pallas kernels  173 us (89%)
  starting transfers between devices  8.77 us (4%)
  local copies, waits for them, and re-layouts  7.25 us (4%)
  matrix products  3.23 us (2%)
    pallas_call x4, Pallas kernels, step(): pl.pallas_call(functools.partial(step_kernel, n_sec, n_op, count, final),...  153 us
    pallas_call x4, Pallas kernels, sigma_part(): pl.pallas_call(sigma_part_kernel, out_shape=jax.ShapeDtypeStruct((sectors...  20 us
    ppermute x1, starting transfers between devices, padded(): lax.ppermute(head, axis, [((i + 1) % count, i) for i in range(count)])  6.22 us
  transfers between devices with their start and end apart: 3, of which 1 were waited for; matrix products, arithmetic and copies ran while one was open for 2% of the time, Pallas kernels for 0%

profile of v12, /device:TPU:1, one launch (start us, length us, event | category | flops | bytes accessed | tf_op | source)
XLA Modules:
  0.0 194.9 jit_solution(4561598137522136020)
XLA Ops:
  0.7 2.5 %collective-permute-start = (bf16[2,256,256]{2,1,0:T(8,128)(2,1)}, bf16[2,256,256]{2,1,0:T(8,128)(2,1)S(1)}, u32[]{:S(2)}, u32[]{:S(2)}) collective-permute-start(bf16[2,256,256]{2,1,0:T(8,128)(2,1)} %param.6), channel_id=1, source_target_pairs={{0,8},{8,16},{16,24},{24,32},{32,40},{40,48},{48,56},{56,64},{64,7... | collective-permute-start | bytes 786440 | tf_op jit(solution)/shard_map/ppermute | solution.py:25
  3.2 6.2 %collective-permute-start.1 = (bf16[2,256,256]{2,1,0:T(8,128)(2,1)}, bf16[2,256,256]{2,1,0:T(8,128)(2,1)S(1)}, u32[]{:S(2)}, u32[]{:S(2)}) collective-permute-start(bf16[2,256,256]{2,1,0:T(8,128)(2,1)} %param.6), channel_id=1, source_target_pairs={{8,0},{16,8},{24,16},{32,24},{40,32},{48,40},{56,48},{64,56},{72,6... | collective-permute-start | bytes 786440 | tf_op jit(solution)/shard_map/ppermute | solution.py:27
  9.4 0.0 collective-permute-start.2
  9.4 2.9 %fusion.19 = (bf16[2,2,256,256]{3,2,1,0:T(8,128)(2,1)}, bf16[2,2,256,256]{3,2,1,0:T(8,128)(2,1)}, bf16[2,2,256,256]{3,2,1,0:T(8,128)(2,1)}, bf16[2,2,256,256]{3,2,1,0:T(8,128)(2,1)}) fusion(bf16[8,2,256,256]{3,2,1,0:T(8,128)(2,1)} %left_ref.7), kind=kLoop, calls=%fused_computation.19 | loop fusion | bytes 4194304 | tf_op jit(solution)/shard_map/slice | solution.py:579
  12.3 0.1 broadcast_in_dim.4
  12.4 0.7 broadcast_in_dim_reshape.3.sh_ref
  13.1 0.7 copy.14.partner_ref
  13.8 1.9 collective-permute-done.2
  15.6 0.1 compare_convert_fusion
  15.7 0.0 collective-permute-done
  15.8 0.0 collective-permute-done.1
  15.8 0.0 copy-start
  15.8 0.9 copy-done
  16.7 5.0 %shard_map.77 = f32[2,256,256]{2,1,0:T(8,128)} custom-call(s32[8,2]{1,0:T(8,128)} %copy.14.partner_ref, bf16[6,256,256]{2,1,0:T(8,128)(2,1)} %copy-done, bf16[8,2,256,256]{3,2,1,0:T(8,128)(2,1)} %left_ref.7, bf16[8,2,256,256]{3,2,1,0:T(8,128)(2,1)} %right_ref.7), custom_call_target="tpu_custom_call" | custom-call | flops 1073741824 | bytes 5505024 | tf_op jit(solution)/shard_map/pallas_call | solution.py:535
  21.7 39.0 %shard_map.78 = (bf16[24,64,256]{2,1,0:T(8,128)(2,1)}, bf16[2,2,256,256]{3,2,1,0:T(8,128)(2,1)}) custom-call(f32[8,64,256]{2,1,0:T(8,128)} %bitcast.31, bf16[24,64,256]{2,1,0:T(8,128)(2,1)} %bitcast.24, f32[8,1,1]{2,1,0:T(1,128)} %broadcast_in_dim_reshape.3.sh_ref, bf16[2,2,256,256]{3,2,1,0:T(8,128)(2,1)} %get-tuple-element.21.piece_ref), custom_call_target="tpu_custom_call" | custom-call | tf_op jit(solution)/shard_map/pallas_call | solution.py:505
  60.7 5.0 %shard_map.79 = f32[2,256,256]{2,1,0:T(8,128)} custom-call(s32[8,2]{1,0:T(8,128)} %copy.14.partner_ref, bf16[6,256,256]{2,1,0:T(8,128)(2,1)} %bitcast.26, bf16[8,2,256,256]{3,2,1,0:T(8,128)(2,1)} %left_ref.7, bf16[8,2,256,256]{3,2,1,0:T(8,128)(2,1)} %right_ref.7), custom_call_target="tpu_custom_call" | custom-call | flops 1073741824 | bytes 5505024 | tf_op jit(solution)/shard_map/pallas_call | solution.py:535
  65.7 37.0 %shard_map.80 = (bf16[24,64,256]{2,1,0:T(8,128)(2,1)}, bf16[2,2,256,256]{3,2,1,0:T(8,128)(2,1)}) custom-call(f32[8,64,256]{2,1,0:T(8,128)} %bitcast.32, bf16[24,64,256]{2,1,0:T(8,128)(2,1)} %get-tuple-element.10.st_ref, f32[8,1,1]{2,1,0:T(1,128)} %broadcast_in_dim_reshape.3.sh_ref, bf16[2,2,256,256]{3,2,1,0:T(8,128)(2,1)} %get-tuple-element.20.piece_ref), custom_call_target="tpu_custom_call" | custom-call | tf_op jit(solution)/shard_map/pallas_call | solution.py:505
  102.7 5.0 %shard_map.81 = f32[2,256,256]{2,1,0:T(8,128)} custom-call(s32[8,2]{1,0:T(8,128)} %copy.14.partner_ref, bf16[6,256,256]{2,1,0:T(8,128)(2,1)} %bitcast.27, bf16[8,2,256,256]{3,2,1,0:T(8,128)(2,1)} %left_ref.7, bf16[8,2,256,256]{3,2,1,0:T(8,128)(2,1)} %right_ref.7), custom_call_target="tpu_custom_call" | custom-call | flops 1073741824 | bytes 5505024 | tf_op jit(solution)/shard_map/pallas_call | solution.py:535
  107.7 35.9 %shard_map.82 = (bf16[24,64,256]{2,1,0:T(8,128)(2,1)}, bf16[2,2,256,256]{3,2,1,0:T(8,128)(2,1)}) custom-call(f32[8,64,256]{2,1,0:T(8,128)} %bitcast.33, bf16[24,64,256]{2,1,0:T(8,128)(2,1)} %get-tuple-element.11.st_ref, f32[8,1,1]{2,1,0:T(1,128)} %broadcast_in_dim_reshape.3.sh_ref, bf16[2,2,256,256]{3,2,1,0:T(8,128)(2,1)} %get-tuple-element.19.piece_ref), custom_call_target="tpu_custom_call" | custom-call | tf_op jit(solution)/shard_map/pallas_call | solution.py:505
  143.6 5.0 %shard_map.83 = f32[2,256,256]{2,1,0:T(8,128)} custom-call(s32[8,2]{1,0:T(8,128)} %copy.14.partner_ref, bf16[6,256,256]{2,1,0:T(8,128)(2,1)} %bitcast.25, bf16[8,2,256,256]{3,2,1,0:T(8,128)(2,1)} %left_ref.7, bf16[8,2,256,256]{3,2,1,0:T(8,128)(2,1)} %right_ref.7), custom_call_target="tpu_custom_call" | custom-call | flops 1073741824 | bytes 5505024 | tf_op jit(solution)/shard_map/pallas_call | solution.py:535
  148.7 40.9 %shard_map.84 = (bf16[16,64,256]{2,1,0:T(8,128)(2,1)}, bf16[2,2,256,256]{3,2,1,0:T(8,128)(2,1)}) custom-call(f32[8,64,256]{2,1,0:T(8,128)} %bitcast.30, bf16[24,64,256]{2,1,0:T(8,128)(2,1)} %get-tuple-element.12.st_ref, f32[8,1,1]{2,1,0:T(1,128)} %broadcast_in_dim_reshape.3.sh_ref, bf16[2,2,256,256]{3,2,1,0:T(8,128)(2,1)} %get-tuple-element.18.piece_ref), custom_call_target="tpu_custom_call" | custom-call | tf_op jit(solution)/shard_map/pallas_call | solution.py:505
  189.6 1.8 fusion.20
  191.5 0.1 copy.16
  191.7 3.2 %multiply_convert_fusion = bf16[8,2,256,256]{3,2,1,0:T(8,128)(2,1)} fusion(bf16[2,2,256,256]{3,2,1,0:T(8,128)(2,1)S(1)} %copy-done.6, bf16[2,2,256,256]{3,2,1,0:T(8,128)(2,1)S(1)} %copy-done.5, bf16[2,2,256,256]{3,2,1,0:T(8,128)(2,1)S(1)} %copy-done.4, bf16[2,2,256,256]{3,2,1,0:T(8,128)(2,1)S(1)} %copy-done.3, bf16[2,256,256]{2,1,0:T(8,128)(2,1)S(1)} %copy.16, ...), kind=kOutput, calls=%fused_computation | convolution fusion | flops 1085276160 | bytes 4718592 | tf_op jit(solution)/shard_map/tbij,tbjk->tbik/dot_general | solution.py:596
  (19 shorter events, 0.1 us)
Async XLA Ops:
  0.6 15.1 %copy-start.1 = (bf16[2,256,256]{2,1,0:T(8,128)(2,1)S(1)}, bf16[2,256,256]{2,1,0:T(8,128)(2,1)}, u32[]{:S(2)}) copy-start(bf16[2,256,256]{2,1,0:T(8,128)(2,1)} %param.6) | copy-start | bytes 786436
  0.6 11.7 %copy-start.7 = (f32[2]{0:T(128)S(1)}, f32[2]{0:T(128)}, u32[]{:S(2)}) copy-start(f32[2]{0:T(128)} %param.9) | copy-start | bytes 28
  0.7 12.4 %copy-start.2 = (s32[8,2]{0,1:T(2,128)S(1)}, s32[8,2]{0,1:T(2,128)}, u32[]{:S(2)}) copy-start(s32[8,2]{0,1:T(2,128)} %param.10) | copy-start | bytes 196
  0.7 15.0 %collective-permute-start = (bf16[2,256,256]{2,1,0:T(8,128)(2,1)}, bf16[2,256,256]{2,1,0:T(8,128)(2,1)S(1)}, u32[]{:S(2)}, u32[]{:S(2)}) collective-permute-start(bf16[2,256,256]{2,1,0:T(8,128)(2,1)} %param.6), channel_id=1, source_target_pairs={{0,8},{8,16},{16,24},{24,32},{32,40},{40,48},{48,56},{56,64},{64,7... | collective-permute-start | bytes 786440 | tf_op jit(solution)/shard_map/ppermute | solution.py:25
  3.2 12.6 %collective-permute-start.1 = (bf16[2,256,256]{2,1,0:T(8,128)(2,1)}, bf16[2,256,256]{2,1,0:T(8,128)(2,1)S(1)}, u32[]{:S(2)}, u32[]{:S(2)}) collective-permute-start(bf16[2,256,256]{2,1,0:T(8,128)(2,1)} %param.6), channel_id=1, source_target_pairs={{8,0},{16,8},{24,16},{32,24},{40,32},{48,40},{56,48},{64,56},{72,6... | collective-permute-start | bytes 786440 | tf_op jit(solution)/shard_map/ppermute | solution.py:27
  9.4 6.2 %collective-permute-start.2 = (s32[2]{0:T(128)}, s32[2]{0:T(128)S(1)}, u32[]{:S(2)}, u32[]{:S(2)}) collective-permute-start(s32[2]{0:T(128)} %param.11), channel_id=1, source_target_pairs={{248,0},{0,8},{8,16},{16,24},{24,32},{32,40},{40,48},{48,56},{56,6... | collective-permute-start | bytes 32 | tf_op jit(solution)/shard_map/ppermute | solution.py:559
  15.8 0.9 copy-start
  148.6 43.0 %copy-start.3 = (bf16[2,2,256,256]{3,2,1,0:T(8,128)(2,1)S(1)}, bf16[2,2,256,256]{3,2,1,0:T(8,128)(2,1)}, u32[]{:S(2)}) copy-start(bf16[2,2,256,256]{3,2,1,0:T(8,128)(2,1)} %get-tuple-element.14) | copy-start | bytes 1572868
  148.6 43.0 %copy-start.4 = (bf16[2,2,256,256]{3,2,1,0:T(8,128)(2,1)S(1)}, bf16[2,2,256,256]{3,2,1,0:T(8,128)(2,1)}, u32[]{:S(2)}) copy-start(bf16[2,2,256,256]{3,2,1,0:T(8,128)(2,1)} %get-tuple-element.15) | copy-start | bytes 1572868
  148.6 43.0 %copy-start.5 = (bf16[2,2,256,256]{3,2,1,0:T(8,128)(2,1)S(1)}, bf16[2,2,256,256]{3,2,1,0:T(8,128)(2,1)}, u32[]{:S(2)}) copy-start(bf16[2,2,256,256]{3,2,1,0:T(8,128)(2,1)} %get-tuple-element.16) | copy-start | bytes 1572868
  189.6 2.1 %copy-start.6 = (bf16[2,2,256,256]{3,2,1,0:T(8,128)(2,1)S(1)}, bf16[2,2,256,256]{3,2,1,0:T(8,128)(2,1)}, u32[]{:S(2)}) copy-start(bf16[2,2,256,256]{3,2,1,0:T(8,128)(2,1)} %get-tuple-element.17) | copy-start | bytes 1572868

commit v13 on v12

--- a/solution.py
+++ b/solution.py
@@ -553,6 +553,48 @@
     )(partner, window, left_ops, right_ops)
 
 
+def halo_kernel(n_sec, st_ref, win_ref, win_buf, send, recv):
+    me_sec = lax.axis_index("sec")
+    me_op = lax.axis_index("op")
+    prev_sec = (me_sec + n_sec - 1) % n_sec
+    next_sec = (me_sec + 1) % n_sec
+    barrier = pltpu.get_barrier_semaphore()
+    for side in (prev_sec, next_sec):
+        pl.semaphore_signal(barrier, 1, device_id=(side, me_op), device_id_type=MESH)
+    pl.semaphore_wait(barrier, 2)
+    copies = [
+        pltpu.make_async_remote_copy(
+            src_ref=st_ref, dst_ref=win_buf.at[slot], send_sem=send.at[k],
+            recv_sem=recv.at[slot], device_id=(side, me_op), device_id_type=MESH)
+        for k, (side, slot) in enumerate(((next_sec, 0), (prev_sec, 2)))
+    ]
+    for c in copies:
+        c.start()
+    win_buf[1] = st_ref[...]
+    for c in copies:
+        c.wait_recv()
+    win_ref[...] = win_buf[...]
+    for c in copies:
+        c.wait_send()
+
+
+def halo(state, n_sec):
+    vmem = pl.BlockSpec(memory_space=pltpu.VMEM)
+    window = pl.pallas_call(
+        functools.partial(halo_kernel, n_sec),
+        out_shape=jax.ShapeDtypeStruct((3,) + state.shape, state.dtype),
+        in_specs=[vmem],
+        out_specs=vmem,
+        scratch_shapes=[
+            pltpu.VMEM((3,) + state.shape, state.dtype),
+            pltpu.SemaphoreType.DMA((2,)),
+            pltpu.SemaphoreType.DMA((3,)),
+        ],
+        compiler_params=pltpu.CompilerParams(collective_id=4, has_side_effects=True),
+    )(state)
+    return window.reshape((3 * state.shape[0],) + state.shape[1:])
+
+
 def shifted(block, axis, distance):
     devices = range(lax.axis_size(axis))
     route = [((i - distance) % len(devices), i) for i in devices]
@@ -567,7 +609,7 @@
     n_op = lax.axis_size("op")
     kept_prev = shifted(kept, "sec", 1)
     state = state_start
-    window = padded(state, (("sec", 0),), sector_local)
+    window = halo(state, n_sec)
     terms = left_ops.shape[0]
     cuts = [terms * k // ITERS for k in range(ITERS + 1)]
     left_pieces = []

time: 195 us -> 202 us (1.036)
  Pallas kernels: 173 us -> 187 us
  starting transfers between devices: 8.77 us -> 2.54 us
    pallas_call x0 -> x1, Pallas kernels: none -> 14.9 us  [halo(): pl.pallas_call(functools.partial(halo_kernel, n_sec), out_shape=jax.Shape...]
    ppermute x2 -> x0, starting transfers between devices: 8.77 us -> none  [the longest x1 6.22 us: padded(): lax.ppermute(head, axis, [((i + 1) % count, i) for i in range(count)])]
    ppermute x1, starting transfers between devices: 0.01 us -> 2.54 us  [shifted(): return lax.ppermute(block, axis, route)]
  transfers between devices with their start and end apart: 3 -> 1, of which waited for: 1 -> 0; matrix products, arithmetic and copies ran while one was open for 2% -> 4% of each run, Pallas kernels for 0% -> 93%
where the time goes in v13:
time: 202 us
  Pallas kernels  187 us (93%)
  local copies, waits for them, and re-layouts  7.64 us (4%)
  matrix products  3.23 us (2%)
  starting transfers between devices  2.54 us (1%)
    pallas_call x4, Pallas kernels, step(): pl.pallas_call(functools.partial(step_kernel, n_sec, n_op, count, final),...  153 us
    pallas_call x4, Pallas kernels, sigma_part(): pl.pallas_call(sigma_part_kernel, out_shape=jax.ShapeDtypeStruct((sectors...  20 us
    pallas_call x1, Pallas kernels, halo(): pl.pallas_call(functools.partial(halo_kernel, n_sec), out_shape=jax.Shape...  14.9 us
  transfers between devices with their start and end apart: 1, of which 0 were waited for; matrix products, arithmetic and copies ran while one was open for 4% of the time, Pallas kernels for 93%

profile of v13, /device:TPU:1, one launch (start us, length us, event | category | flops | bytes accessed | tf_op | source)
XLA Modules:
  0.0 201.7 jit_solution(4555032682118830938)
XLA Ops:
  0.6 2.5 %collective-permute-start = (s32[2]{0:T(128)}, s32[2]{0:T(128)S(1)}, u32[]{:S(2)}, u32[]{:S(2)}) collective-permute-start(s32[2]{0:T(128)} %param.11), channel_id=1, source_target_pairs={{248,0},{0,8},{8,16},{16,24},{24,32},{32,40},{40,48},{48,56},{56,6... | collective-permute-start | bytes 32 | tf_op jit(solution)/shard_map/ppermute | solution.py:601
  3.2 0.7 broadcast_in_dim.4
  3.9 0.7 broadcast_in_dim_reshape.3.sh_ref
  4.6 1.3 copy.14.partner_ref
  5.9 14.9 %shard_map.77 = bf16[3,2,256,256]{3,2,1,0:T(8,128)(2,1)} custom-call(bf16[2,256,256]{2,1,0:T(8,128)(2,1)} %st_ref.1), custom_call_target="tpu_custom_call" | custom-call | tf_op jit(solution)/shard_map/pallas_call | solution.py:583
  20.8 2.9 %fusion.19 = (bf16[2,2,256,256]{3,2,1,0:T(8,128)(2,1)}, bf16[2,2,256,256]{3,2,1,0:T(8,128)(2,1)}, bf16[2,2,256,256]{3,2,1,0:T(8,128)(2,1)}, bf16[2,2,256,256]{3,2,1,0:T(8,128)(2,1)}) fusion(bf16[8,2,256,256]{3,2,1,0:T(8,128)(2,1)} %left_ref.7), kind=kLoop, calls=%fused_computation.16 | loop fusion | bytes 4194304 | tf_op jit(solution)/shard_map/slice | solution.py:621
  23.8 5.0 %shard_map.78 = f32[2,256,256]{2,1,0:T(8,128)} custom-call(s32[8,2]{1,0:T(8,128)} %copy.14.partner_ref, bf16[6,256,256]{2,1,0:T(8,128)(2,1)} %bitcast.25, bf16[8,2,256,256]{3,2,1,0:T(8,128)(2,1)} %left_ref.7, bf16[8,2,256,256]{3,2,1,0:T(8,128)(2,1)} %right_ref.7), custom_call_target="tpu_custom_call" | custom-call | flops 1073741824 | bytes 5505024 | tf_op jit(solution)/shard_map/pallas_call | solution.py:535
  28.8 38.9 %shard_map.79 = (bf16[24,64,256]{2,1,0:T(8,128)(2,1)}, bf16[2,2,256,256]{3,2,1,0:T(8,128)(2,1)}) custom-call(f32[8,64,256]{2,1,0:T(8,128)} %bitcast.33, bf16[24,64,256]{2,1,0:T(8,128)(2,1)} %bitcast.26, f32[8,1,1]{2,1,0:T(1,128)} %broadcast_in_dim_reshape.3.sh_ref, bf16[2,2,256,256]{3,2,1,0:T(8,128)(2,1)} %get-tuple-element.21.piece_ref), custom_call_target="tpu_custom_call" | custom-call | tf_op jit(solution)/shard_map/pallas_call | solution.py:505
  67.6 5.0 %shard_map.80 = f32[2,256,256]{2,1,0:T(8,128)} custom-call(s32[8,2]{1,0:T(8,128)} %copy.14.partner_ref, bf16[6,256,256]{2,1,0:T(8,128)(2,1)} %bitcast.28, bf16[8,2,256,256]{3,2,1,0:T(8,128)(2,1)} %left_ref.7, bf16[8,2,256,256]{3,2,1,0:T(8,128)(2,1)} %right_ref.7), custom_call_target="tpu_custom_call" | custom-call | flops 1073741824 | bytes 5505024 | tf_op jit(solution)/shard_map/pallas_call | solution.py:535
  72.6 36.5 %shard_map.81 = (bf16[24,64,256]{2,1,0:T(8,128)(2,1)}, bf16[2,2,256,256]{3,2,1,0:T(8,128)(2,1)}) custom-call(f32[8,64,256]{2,1,0:T(8,128)} %bitcast.34, bf16[24,64,256]{2,1,0:T(8,128)(2,1)} %get-tuple-element.10.st_ref, f32[8,1,1]{2,1,0:T(1,128)} %broadcast_in_dim_reshape.3.sh_ref, bf16[2,2,256,256]{3,2,1,0:T(8,128)(2,1)} %get-tuple-element.20.piece_ref), custom_call_target="tpu_custom_call" | custom-call | tf_op jit(solution)/shard_map/pallas_call | solution.py:505
  109.1 5.0 %shard_map.82 = f32[2,256,256]{2,1,0:T(8,128)} custom-call(s32[8,2]{1,0:T(8,128)} %copy.14.partner_ref, bf16[6,256,256]{2,1,0:T(8,128)(2,1)} %bitcast.29, bf16[8,2,256,256]{3,2,1,0:T(8,128)(2,1)} %left_ref.7, bf16[8,2,256,256]{3,2,1,0:T(8,128)(2,1)} %right_ref.7), custom_call_target="tpu_custom_call" | custom-call | flops 1073741824 | bytes 5505024 | tf_op jit(solution)/shard_map/pallas_call | solution.py:535
  114.1 36.0 %shard_map.83 = (bf16[24,64,256]{2,1,0:T(8,128)(2,1)}, bf16[2,2,256,256]{3,2,1,0:T(8,128)(2,1)}) custom-call(f32[8,64,256]{2,1,0:T(8,128)} %bitcast.35, bf16[24,64,256]{2,1,0:T(8,128)(2,1)} %get-tuple-element.11.st_ref, f32[8,1,1]{2,1,0:T(1,128)} %broadcast_in_dim_reshape.3.sh_ref, bf16[2,2,256,256]{3,2,1,0:T(8,128)(2,1)} %get-tuple-element.19.piece_ref), custom_call_target="tpu_custom_call" | custom-call | tf_op jit(solution)/shard_map/pallas_call | solution.py:505
  150.1 5.0 %shard_map.84 = f32[2,256,256]{2,1,0:T(8,128)} custom-call(s32[8,2]{1,0:T(8,128)} %copy.14.partner_ref, bf16[6,256,256]{2,1,0:T(8,128)(2,1)} %bitcast.27, bf16[8,2,256,256]{3,2,1,0:T(8,128)(2,1)} %left_ref.7, bf16[8,2,256,256]{3,2,1,0:T(8,128)(2,1)} %right_ref.7), custom_call_target="tpu_custom_call" | custom-call | flops 1073741824 | bytes 5505024 | tf_op jit(solution)/shard_map/pallas_call | solution.py:535
  155.1 41.2 %shard_map.85 = (bf16[16,64,256]{2,1,0:T(8,128)(2,1)}, bf16[2,2,256,256]{3,2,1,0:T(8,128)(2,1)}) custom-call(f32[8,64,256]{2,1,0:T(8,128)} %bitcast.32, bf16[24,64,256]{2,1,0:T(8,128)(2,1)} %get-tuple-element.12.st_ref, f32[8,1,1]{2,1,0:T(1,128)} %broadcast_in_dim_reshape.3.sh_ref, bf16[2,2,256,256]{3,2,1,0:T(8,128)(2,1)} %get-tuple-element.18.piece_ref), custom_call_target="tpu_custom_call" | custom-call | tf_op jit(solution)/shard_map/pallas_call | solution.py:505
  196.3 0.0 copy-start.3
  196.3 1.8 fusion.20
  198.2 0.0 collective-permute-done
  198.2 0.1 compare_convert_fusion
  198.3 0.1 copy.16
  198.4 0.0 copy-done
  198.4 0.0 copy-done.1
  198.4 0.0 copy-done.2
  198.5 0.0 copy-done.3
  198.5 3.2 %multiply_convert_fusion = bf16[8,2,256,256]{3,2,1,0:T(8,128)(2,1)} fusion(bf16[2,2,256,256]{3,2,1,0:T(8,128)(2,1)S(1)} %copy-done.3, bf16[2,2,256,256]{3,2,1,0:T(8,128)(2,1)S(1)} %copy-done.2, bf16[2,2,256,256]{3,2,1,0:T(8,128)(2,1)S(1)} %copy-done.1, bf16[2,2,256,256]{3,2,1,0:T(8,128)(2,1)S(1)} %copy-done, bf16[2,256,256]{2,1,0:T(8,128)(2,1)S(1)} %copy.16, ...), kind=kOutput, calls=%fused_computation | convolution fusion | flops 1085276160 | bytes 4718592 | tf_op jit(solution)/shard_map/tbij,tbjk->tbik/dot_general | solution.py:638
  (5 shorter events, 0.1 us)
Async XLA Ops:
  0.6 197.5 %collective-permute-start = (s32[2]{0:T(128)}, s32[2]{0:T(128)S(1)}, u32[]{:S(2)}, u32[]{:S(2)}) collective-permute-start(s32[2]{0:T(128)} %param.11), channel_id=1, source_target_pairs={{248,0},{0,8},{8,16},{16,24},{24,32},{32,40},{40,48},{48,56},{56,6... | collective-permute-start | bytes 32 | tf_op jit(solution)/shard_map/ppermute | solution.py:601
  155.1 43.3 %copy-start = (bf16[2,2,256,256]{3,2,1,0:T(8,128)(2,1)S(1)}, bf16[2,2,256,256]{3,2,1,0:T(8,128)(2,1)}, u32[]{:S(2)}) copy-start(bf16[2,2,256,256]{3,2,1,0:T(8,128)(2,1)} %get-tuple-element.14) | copy-start | bytes 1572868
  155.1 43.3 %copy-start.1 = (bf16[2,2,256,256]{3,2,1,0:T(8,128)(2,1)S(1)}, bf16[2,2,256,256]{3,2,1,0:T(8,128)(2,1)}, u32[]{:S(2)}) copy-start(bf16[2,2,256,256]{3,2,1,0:T(8,128)(2,1)} %get-tuple-element.15) | copy-start | bytes 1572868
  155.1 43.3 %copy-start.2 = (bf16[2,2,256,256]{3,2,1,0:T(8,128)(2,1)S(1)}, bf16[2,2,256,256]{3,2,1,0:T(8,128)(2,1)}, u32[]{:S(2)}) copy-start(bf16[2,2,256,256]{3,2,1,0:T(8,128)(2,1)} %get-tuple-element.16) | copy-start | bytes 1572868
  196.3 2.1 %copy-start.3 = (bf16[2,2,256,256]{3,2,1,0:T(8,128)(2,1)S(1)}, bf16[2,2,256,256]{3,2,1,0:T(8,128)(2,1)}, u32[]{:S(2)}) copy-start(bf16[2,2,256,256]{3,2,1,0:T(8,128)(2,1)} %get-tuple-element.17) | copy-start | bytes 1572868

commit v14 on v12

--- a/solution.py
+++ b/solution.py
@@ -520,9 +520,16 @@
 
 def sigma_part_kernel(partner_ref, win_ref, left_ref, right_ref, o_ref):
     b = pl.program_id(0)
-    total = jnp.zeros(o_ref.shape[1:], jnp.float32)
-    for t in range(left_ref.shape[0]):
-        source = win_ref[partner_ref[t, b]]
+    h = pl.program_id(1)
+    share = left_ref.shape[0]
+
+    @pl.when(h == 0)
+    def _():
+        o_ref[...] = jnp.zeros_like(o_ref)
+
+    total = o_ref[0]
+    for t in range(share):
+        source = win_ref[partner_ref[h * share + t, b]]
         halfway = jnp.dot(left_ref[t, 0], source, preferred_element_type=jnp.float32)
         total = total + jnp.dot(halfway.astype(jnp.bfloat16), right_ref[t, 0],
                                 preferred_element_type=jnp.float32)
@@ -531,19 +538,20 @@
 
 def sigma_part(window, left_ops, right_ops, partner):
     terms, sectors, m, _ = left_ops.shape
-    op_spec = pl.BlockSpec((terms, 1, m, m), lambda b, p: (0, b, 0, 0))
+    halves = 2 if terms % 2 == 0 else 1
+    op_spec = pl.BlockSpec((terms // halves, 1, m, m), lambda b, h, p: (h, b, 0, 0))
     return pl.pallas_call(
         sigma_part_kernel,
         out_shape=jax.ShapeDtypeStruct((sectors, m, m), jnp.float32),
         grid_spec=pltpu.PrefetchScalarGridSpec(
             num_scalar_prefetch=1,
-            grid=(sectors,),
+            grid=(sectors, halves),
             in_specs=[
-                pl.BlockSpec(window.shape, lambda b, p: (0, 0, 0)),
+                pl.BlockSpec(window.shape, lambda b, h, p: (0, 0, 0)),
                 op_spec,
                 op_spec,
             ],
-            out_specs=pl.BlockSpec((1, m, m), lambda b, p: (b, 0, 0)),
+            out_specs=pl.BlockSpec((1, m, m), lambda b, h, p: (b, 0, 0)),
         ),
         cost_estimate=pl.CostEstimate(
             flops=4 * terms * sectors * m * m * m,

time: 195 us -> 200 us (1.026)
  Pallas kernels: 173 us -> 177 us
    pallas_call x4, Pallas kernels: 20 us -> 24.1 us  [sigma_part(): pl.pallas_call(sigma_part_kernel, out_shape=jax.ShapeDtypeStruct((sectors...]
where the time goes in v14:
time: 200 us; the launch traced here: 199 us
  Pallas kernels  177 us (88%)
  starting transfers between devices  8.77 us (4%)
  local copies, waits for them, and re-layouts  7.25 us (4%)
  matrix products  3.23 us (2%)
    pallas_call x4, Pallas kernels, step(): pl.pallas_call(functools.partial(step_kernel, n_sec, n_op, count, final),...  153 us
    pallas_call x4, Pallas kernels, sigma_part(): pl.pallas_call(sigma_part_kernel, out_shape=jax.ShapeDtypeStruct((sectors...  24.1 us
    ppermute x1, starting transfers between devices, padded(): lax.ppermute(head, axis, [((i + 1) % count, i) for i in range(count)])  6.22 us
  transfers between devices with their start and end apart: 3, of which 1 were waited for; matrix products, arithmetic and copies ran while one was open for 2% of the time, Pallas kernels for 0%

profile of v14, /device:TPU:1, one launch (start us, length us, event | category | flops | bytes accessed | tf_op | source)
XLA Modules:
  0.0 199.0 jit_solution(1641350235784622582)
XLA Ops:
  0.7 2.5 %collective-permute-start = (bf16[2,256,256]{2,1,0:T(8,128)(2,1)}, bf16[2,256,256]{2,1,0:T(8,128)(2,1)S(1)}, u32[]{:S(2)}, u32[]{:S(2)}) collective-permute-start(bf16[2,256,256]{2,1,0:T(8,128)(2,1)} %param.6), channel_id=1, source_target_pairs={{0,8},{8,16},{16,24},{24,32},{32,40},{40,48},{48,56},{56,64},{64,7... | collective-permute-start | bytes 786440 | tf_op jit(solution)/shard_map/ppermute | solution.py:25
  3.2 6.2 %collective-permute-start.1 = (bf16[2,256,256]{2,1,0:T(8,128)(2,1)}, bf16[2,256,256]{2,1,0:T(8,128)(2,1)S(1)}, u32[]{:S(2)}, u32[]{:S(2)}) collective-permute-start(bf16[2,256,256]{2,1,0:T(8,128)(2,1)} %param.6), channel_id=1, source_target_pairs={{8,0},{16,8},{24,16},{32,24},{40,32},{48,40},{56,48},{64,56},{72,6... | collective-permute-start | bytes 786440 | tf_op jit(solution)/shard_map/ppermute | solution.py:27
  9.4 0.0 collective-permute-start.2
  9.4 2.9 %fusion.19 = (bf16[2,2,256,256]{3,2,1,0:T(8,128)(2,1)}, bf16[2,2,256,256]{3,2,1,0:T(8,128)(2,1)}, bf16[2,2,256,256]{3,2,1,0:T(8,128)(2,1)}, bf16[2,2,256,256]{3,2,1,0:T(8,128)(2,1)}) fusion(bf16[8,2,256,256]{3,2,1,0:T(8,128)(2,1)} %left_ref.7), kind=kLoop, calls=%fused_computation.19 | loop fusion | bytes 4194304 | tf_op jit(solution)/shard_map/slice | solution.py:587
  12.3 0.1 broadcast_in_dim.4
  12.4 0.7 broadcast_in_dim_reshape.3.sh_ref
  13.1 0.7 copy.14.partner_ref
  13.8 1.9 collective-permute-done.2
  15.6 0.1 compare_convert_fusion
  15.7 0.0 collective-permute-done
  15.8 0.0 collective-permute-done.1
  15.8 0.0 copy-start
  15.8 0.9 copy-done
  16.7 6.0 %shard_map.77 = f32[2,256,256]{2,1,0:T(8,128)} custom-call(s32[8,2]{1,0:T(8,128)} %copy.14.partner_ref, bf16[6,256,256]{2,1,0:T(8,128)(2,1)} %copy-done, bf16[8,2,256,256]{3,2,1,0:T(8,128)(2,1)} %left_ref.7, bf16[8,2,256,256]{3,2,1,0:T(8,128)(2,1)} %right_ref.7), custom_call_target="tpu_custom_call" | custom-call | flops 1073741824 | bytes 5505024 | tf_op jit(solution)/shard_map/pallas_call | solution.py:543
  22.7 39.0 %shard_map.78 = (bf16[24,64,256]{2,1,0:T(8,128)(2,1)}, bf16[2,2,256,256]{3,2,1,0:T(8,128)(2,1)}) custom-call(f32[8,64,256]{2,1,0:T(8,128)} %bitcast.31, bf16[24,64,256]{2,1,0:T(8,128)(2,1)} %bitcast.24, f32[8,1,1]{2,1,0:T(1,128)} %broadcast_in_dim_reshape.3.sh_ref, bf16[2,2,256,256]{3,2,1,0:T(8,128)(2,1)} %get-tuple-element.21.piece_ref), custom_call_target="tpu_custom_call" | custom-call | tf_op jit(solution)/shard_map/pallas_call | solution.py:505
  61.7 6.0 %shard_map.79 = f32[2,256,256]{2,1,0:T(8,128)} custom-call(s32[8,2]{1,0:T(8,128)} %copy.14.partner_ref, bf16[6,256,256]{2,1,0:T(8,128)(2,1)} %bitcast.26, bf16[8,2,256,256]{3,2,1,0:T(8,128)(2,1)} %left_ref.7, bf16[8,2,256,256]{3,2,1,0:T(8,128)(2,1)} %right_ref.7), custom_call_target="tpu_custom_call" | custom-call | flops 1073741824 | bytes 5505024 | tf_op jit(solution)/shard_map/pallas_call | solution.py:543
  67.8 37.0 %shard_map.80 = (bf16[24,64,256]{2,1,0:T(8,128)(2,1)}, bf16[2,2,256,256]{3,2,1,0:T(8,128)(2,1)}) custom-call(f32[8,64,256]{2,1,0:T(8,128)} %bitcast.32, bf16[24,64,256]{2,1,0:T(8,128)(2,1)} %get-tuple-element.10.st_ref, f32[8,1,1]{2,1,0:T(1,128)} %broadcast_in_dim_reshape.3.sh_ref, bf16[2,2,256,256]{3,2,1,0:T(8,128)(2,1)} %get-tuple-element.20.piece_ref), custom_call_target="tpu_custom_call" | custom-call | tf_op jit(solution)/shard_map/pallas_call | solution.py:505
  104.8 6.0 %shard_map.81 = f32[2,256,256]{2,1,0:T(8,128)} custom-call(s32[8,2]{1,0:T(8,128)} %copy.14.partner_ref, bf16[6,256,256]{2,1,0:T(8,128)(2,1)} %bitcast.27, bf16[8,2,256,256]{3,2,1,0:T(8,128)(2,1)} %left_ref.7, bf16[8,2,256,256]{3,2,1,0:T(8,128)(2,1)} %right_ref.7), custom_call_target="tpu_custom_call" | custom-call | flops 1073741824 | bytes 5505024 | tf_op jit(solution)/shard_map/pallas_call | solution.py:543
  110.8 35.9 %shard_map.82 = (bf16[24,64,256]{2,1,0:T(8,128)(2,1)}, bf16[2,2,256,256]{3,2,1,0:T(8,128)(2,1)}) custom-call(f32[8,64,256]{2,1,0:T(8,128)} %bitcast.33, bf16[24,64,256]{2,1,0:T(8,128)(2,1)} %get-tuple-element.11.st_ref, f32[8,1,1]{2,1,0:T(1,128)} %broadcast_in_dim_reshape.3.sh_ref, bf16[2,2,256,256]{3,2,1,0:T(8,128)(2,1)} %get-tuple-element.19.piece_ref), custom_call_target="tpu_custom_call" | custom-call | tf_op jit(solution)/shard_map/pallas_call | solution.py:505
  146.7 6.0 %shard_map.83 = f32[2,256,256]{2,1,0:T(8,128)} custom-call(s32[8,2]{1,0:T(8,128)} %copy.14.partner_ref, bf16[6,256,256]{2,1,0:T(8,128)(2,1)} %bitcast.25, bf16[8,2,256,256]{3,2,1,0:T(8,128)(2,1)} %left_ref.7, bf16[8,2,256,256]{3,2,1,0:T(8,128)(2,1)} %right_ref.7), custom_call_target="tpu_custom_call" | custom-call | flops 1073741824 | bytes 5505024 | tf_op jit(solution)/shard_map/pallas_call | solution.py:543
  152.7 40.9 %shard_map.84 = (bf16[16,64,256]{2,1,0:T(8,128)(2,1)}, bf16[2,2,256,256]{3,2,1,0:T(8,128)(2,1)}) custom-call(f32[8,64,256]{2,1,0:T(8,128)} %bitcast.30, bf16[24,64,256]{2,1,0:T(8,128)(2,1)} %get-tuple-element.12.st_ref, f32[8,1,1]{2,1,0:T(1,128)} %broadcast_in_dim_reshape.3.sh_ref, bf16[2,2,256,256]{3,2,1,0:T(8,128)(2,1)} %get-tuple-element.18.piece_ref), custom_call_target="tpu_custom_call" | custom-call | tf_op jit(solution)/shard_map/pallas_call | solution.py:505
  193.7 1.8 fusion.20
  195.6 0.1 copy.16
  195.7 3.2 %multiply_convert_fusion = bf16[8,2,256,256]{3,2,1,0:T(8,128)(2,1)} fusion(bf16[2,2,256,256]{3,2,1,0:T(8,128)(2,1)S(1)} %copy-done.6, bf16[2,2,256,256]{3,2,1,0:T(8,128)(2,1)S(1)} %copy-done.5, bf16[2,2,256,256]{3,2,1,0:T(8,128)(2,1)S(1)} %copy-done.4, bf16[2,2,256,256]{3,2,1,0:T(8,128)(2,1)S(1)} %copy-done.3, bf16[2,256,256]{2,1,0:T(8,128)(2,1)S(1)} %copy.16, ...), kind=kOutput, calls=%fused_computation | convolution fusion | flops 1085276160 | bytes 4718592 | tf_op jit(solution)/shard_map/tbij,tbjk->tbik/dot_general | solution.py:604
  (19 shorter events, 0.1 us)
Async XLA Ops:
  0.6 15.1 %copy-start.1 = (bf16[2,256,256]{2,1,0:T(8,128)(2,1)S(1)}, bf16[2,256,256]{2,1,0:T(8,128)(2,1)}, u32[]{:S(2)}) copy-start(bf16[2,256,256]{2,1,0:T(8,128)(2,1)} %param.6) | copy-start | bytes 786436
  0.6 11.7 %copy-start.7 = (f32[2]{0:T(128)S(1)}, f32[2]{0:T(128)}, u32[]{:S(2)}) copy-start(f32[2]{0:T(128)} %param.9) | copy-start | bytes 28
  0.7 12.4 %copy-start.2 = (s32[8,2]{0,1:T(2,128)S(1)}, s32[8,2]{0,1:T(2,128)}, u32[]{:S(2)}) copy-start(s32[8,2]{0,1:T(2,128)} %param.10) | copy-start | bytes 196
  0.7 15.0 %collective-permute-start = (bf16[2,256,256]{2,1,0:T(8,128)(2,1)}, bf16[2,256,256]{2,1,0:T(8,128)(2,1)S(1)}, u32[]{:S(2)}, u32[]{:S(2)}) collective-permute-start(bf16[2,256,256]{2,1,0:T(8,128)(2,1)} %param.6), channel_id=1, source_target_pairs={{0,8},{8,16},{16,24},{24,32},{32,40},{40,48},{48,56},{56,64},{64,7... | collective-permute-start | bytes 786440 | tf_op jit(solution)/shard_map/ppermute | solution.py:25
  3.2 12.6 %collective-permute-start.1 = (bf16[2,256,256]{2,1,0:T(8,128)(2,1)}, bf16[2,256,256]{2,1,0:T(8,128)(2,1)S(1)}, u32[]{:S(2)}, u32[]{:S(2)}) collective-permute-start(bf16[2,256,256]{2,1,0:T(8,128)(2,1)} %param.6), channel_id=1, source_target_pairs={{8,0},{16,8},{24,16},{32,24},{40,32},{48,40},{56,48},{64,56},{72,6... | collective-permute-start | bytes 786440 | tf_op jit(solution)/shard_map/ppermute | solution.py:27
  9.4 6.2 %collective-permute-start.2 = (s32[2]{0:T(128)}, s32[2]{0:T(128)S(1)}, u32[]{:S(2)}, u32[]{:S(2)}) collective-permute-start(s32[2]{0:T(128)} %param.11), channel_id=1, source_target_pairs={{248,0},{0,8},{8,16},{16,24},{24,32},{32,40},{40,48},{48,56},{56,6... | collective-permute-start | bytes 32 | tf_op jit(solution)/shard_map/ppermute | solution.py:567
  15.8 0.9 copy-start
  152.7 43.0 %copy-start.3 = (bf16[2,2,256,256]{3,2,1,0:T(8,128)(2,1)S(1)}, bf16[2,2,256,256]{3,2,1,0:T(8,128)(2,1)}, u32[]{:S(2)}) copy-start(bf16[2,2,256,256]{3,2,1,0:T(8,128)(2,1)} %get-tuple-element.14) | copy-start | bytes 1572868
  152.7 43.0 %copy-start.4 = (bf16[2,2,256,256]{3,2,1,0:T(8,128)(2,1)S(1)}, bf16[2,2,256,256]{3,2,1,0:T(8,128)(2,1)}, u32[]{:S(2)}) copy-start(bf16[2,2,256,256]{3,2,1,0:T(8,128)(2,1)} %get-tuple-element.15) | copy-start | bytes 1572868
  152.7 43.0 %copy-start.5 = (bf16[2,2,256,256]{3,2,1,0:T(8,128)(2,1)S(1)}, bf16[2,2,256,256]{3,2,1,0:T(8,128)(2,1)}, u32[]{:S(2)}) copy-start(bf16[2,2,256,256]{3,2,1,0:T(8,128)(2,1)} %get-tuple-element.16) | copy-start | bytes 1572868
  193.7 2.1 %copy-start.6 = (bf16[2,2,256,256]{3,2,1,0:T(8,128)(2,1)S(1)}, bf16[2,2,256,256]{3,2,1,0:T(8,128)(2,1)}, u32[]{:S(2)}) copy-start(bf16[2,2,256,256]{3,2,1,0:T(8,128)(2,1)} %get-tuple-element.17) | copy-start | bytes 1572868

commit v15 on v12

--- a/solution.py
+++ b/solution.py
@@ -278,7 +278,6 @@
     for peer in greet:
         pl.semaphore_signal(barrier, 1, device_id=peer, device_id_type=MESH)
     greeted = len(greet)
-    pl.semaphore_wait(barrier, greeted)
 
     def op_peer(j):
         return (me_sec, j)
@@ -371,6 +370,7 @@
         j = (me_op + d) % n_op
         return copy_to(x_ref.at[j], rs_buf.at[me_op], send_rs.at[d], recv_rs.at[me_op], op_peer(j))
 
+    pl.semaphore_wait(barrier, greeted)
     for d in range(1, n_op):
         rs_copy(d).start()
     a_args = (n_op, me_op, t_out, op_buf, send_a, recv_a, op_peer)

time: 195 us -> 194 us (level)
  no operation moved by 1% of the time
where the time goes in v15:
time: 194 us
  Pallas kernels  172 us (89%)
  starting transfers between devices  8.77 us (5%)
  local copies, waits for them, and re-layouts  7.25 us (4%)
  matrix products  3.23 us (2%)
    pallas_call x4, Pallas kernels, step(): pl.pallas_call(functools.partial(step_kernel, n_sec, n_op, count, final),...  152 us
    pallas_call x4, Pallas kernels, sigma_part(): pl.pallas_call(sigma_part_kernel, out_shape=jax.ShapeDtypeStruct((sectors...  20 us
    ppermute x1, starting transfers between devices, padded(): lax.ppermute(head, axis, [((i + 1) % count, i) for i in range(count)])  6.22 us
  transfers between devices with their start and end apart: 3, of which 1 were waited for; matrix products, arithmetic and copies ran while one was open for 2% of the time, Pallas kernels for 0%

profile of v15, /device:TPU:1, one launch (start us, length us, event | category | flops | bytes accessed | tf_op | source)
XLA Modules:
  0.0 193.8 jit_solution(3701110031247029217)
XLA Ops:
  0.7 2.5 %collective-permute-start = (bf16[2,256,256]{2,1,0:T(8,128)(2,1)}, bf16[2,256,256]{2,1,0:T(8,128)(2,1)S(1)}, u32[]{:S(2)}, u32[]{:S(2)}) collective-permute-start(bf16[2,256,256]{2,1,0:T(8,128)(2,1)} %param.6), channel_id=1, source_target_pairs={{0,8},{8,16},{16,24},{24,32},{32,40},{40,48},{48,56},{56,64},{64,7... | collective-permute-start | bytes 786440 | tf_op jit(solution)/shard_map/ppermute | solution.py:25
  3.2 6.2 %collective-permute-start.1 = (bf16[2,256,256]{2,1,0:T(8,128)(2,1)}, bf16[2,256,256]{2,1,0:T(8,128)(2,1)S(1)}, u32[]{:S(2)}, u32[]{:S(2)}) collective-permute-start(bf16[2,256,256]{2,1,0:T(8,128)(2,1)} %param.6), channel_id=1, source_target_pairs={{8,0},{16,8},{24,16},{32,24},{40,32},{48,40},{56,48},{64,56},{72,6... | collective-permute-start | bytes 786440 | tf_op jit(solution)/shard_map/ppermute | solution.py:27
  9.4 0.0 collective-permute-start.2
  9.4 2.9 %fusion.19 = (bf16[2,2,256,256]{3,2,1,0:T(8,128)(2,1)}, bf16[2,2,256,256]{3,2,1,0:T(8,128)(2,1)}, bf16[2,2,256,256]{3,2,1,0:T(8,128)(2,1)}, bf16[2,2,256,256]{3,2,1,0:T(8,128)(2,1)}) fusion(bf16[8,2,256,256]{3,2,1,0:T(8,128)(2,1)} %left_ref.7), kind=kLoop, calls=%fused_computation.19 | loop fusion | bytes 4194304 | tf_op jit(solution)/shard_map/slice | solution.py:579
  12.3 0.1 broadcast_in_dim.4
  12.4 0.7 broadcast_in_dim_reshape.3.sh_ref
  13.1 0.7 copy.14.partner_ref
  13.8 1.9 collective-permute-done.2
  15.6 0.1 compare_convert_fusion
  15.7 0.0 collective-permute-done
  15.8 0.0 collective-permute-done.1
  15.8 0.0 copy-start
  15.8 0.9 copy-done
  16.7 5.0 %shard_map.77 = f32[2,256,256]{2,1,0:T(8,128)} custom-call(s32[8,2]{1,0:T(8,128)} %copy.14.partner_ref, bf16[6,256,256]{2,1,0:T(8,128)(2,1)} %copy-done, bf16[8,2,256,256]{3,2,1,0:T(8,128)(2,1)} %left_ref.7, bf16[8,2,256,256]{3,2,1,0:T(8,128)(2,1)} %right_ref.7), custom_call_target="tpu_custom_call" | custom-call | flops 1073741824 | bytes 5505024 | tf_op jit(solution)/shard_map/pallas_call | solution.py:535
  21.7 38.7 %shard_map.78 = (bf16[24,64,256]{2,1,0:T(8,128)(2,1)}, bf16[2,2,256,256]{3,2,1,0:T(8,128)(2,1)}) custom-call(f32[8,64,256]{2,1,0:T(8,128)} %bitcast.31, bf16[24,64,256]{2,1,0:T(8,128)(2,1)} %bitcast.24, f32[8,1,1]{2,1,0:T(1,128)} %broadcast_in_dim_reshape.3.sh_ref, bf16[2,2,256,256]{3,2,1,0:T(8,128)(2,1)} %get-tuple-element.21.piece_ref), custom_call_target="tpu_custom_call" | custom-call | tf_op jit(solution)/shard_map/pallas_call | solution.py:505
  60.4 5.0 %shard_map.79 = f32[2,256,256]{2,1,0:T(8,128)} custom-call(s32[8,2]{1,0:T(8,128)} %copy.14.partner_ref, bf16[6,256,256]{2,1,0:T(8,128)(2,1)} %bitcast.26, bf16[8,2,256,256]{3,2,1,0:T(8,128)(2,1)} %left_ref.7, bf16[8,2,256,256]{3,2,1,0:T(8,128)(2,1)} %right_ref.7), custom_call_target="tpu_custom_call" | custom-call | flops 1073741824 | bytes 5505024 | tf_op jit(solution)/shard_map/pallas_call | solution.py:535
  65.4 36.7 %shard_map.80 = (bf16[24,64,256]{2,1,0:T(8,128)(2,1)}, bf16[2,2,256,256]{3,2,1,0:T(8,128)(2,1)}) custom-call(f32[8,64,256]{2,1,0:T(8,128)} %bitcast.32, bf16[24,64,256]{2,1,0:T(8,128)(2,1)} %get-tuple-element.10.st_ref, f32[8,1,1]{2,1,0:T(1,128)} %broadcast_in_dim_reshape.3.sh_ref, bf16[2,2,256,256]{3,2,1,0:T(8,128)(2,1)} %get-tuple-element.20.piece_ref), custom_call_target="tpu_custom_call" | custom-call | tf_op jit(solution)/shard_map/pallas_call | solution.py:505
  102.2 5.0 %shard_map.81 = f32[2,256,256]{2,1,0:T(8,128)} custom-call(s32[8,2]{1,0:T(8,128)} %copy.14.partner_ref, bf16[6,256,256]{2,1,0:T(8,128)(2,1)} %bitcast.27, bf16[8,2,256,256]{3,2,1,0:T(8,128)(2,1)} %left_ref.7, bf16[8,2,256,256]{3,2,1,0:T(8,128)(2,1)} %right_ref.7), custom_call_target="tpu_custom_call" | custom-call | flops 1073741824 | bytes 5505024 | tf_op jit(solution)/shard_map/pallas_call | solution.py:535
  107.2 35.6 %shard_map.82 = (bf16[24,64,256]{2,1,0:T(8,128)(2,1)}, bf16[2,2,256,256]{3,2,1,0:T(8,128)(2,1)}) custom-call(f32[8,64,256]{2,1,0:T(8,128)} %bitcast.33, bf16[24,64,256]{2,1,0:T(8,128)(2,1)} %get-tuple-element.11.st_ref, f32[8,1,1]{2,1,0:T(1,128)} %broadcast_in_dim_reshape.3.sh_ref, bf16[2,2,256,256]{3,2,1,0:T(8,128)(2,1)} %get-tuple-element.19.piece_ref), custom_call_target="tpu_custom_call" | custom-call | tf_op jit(solution)/shard_map/pallas_call | solution.py:505
  142.8 5.0 %shard_map.83 = f32[2,256,256]{2,1,0:T(8,128)} custom-call(s32[8,2]{1,0:T(8,128)} %copy.14.partner_ref, bf16[6,256,256]{2,1,0:T(8,128)(2,1)} %bitcast.25, bf16[8,2,256,256]{3,2,1,0:T(8,128)(2,1)} %left_ref.7, bf16[8,2,256,256]{3,2,1,0:T(8,128)(2,1)} %right_ref.7), custom_call_target="tpu_custom_call" | custom-call | flops 1073741824 | bytes 5505024 | tf_op jit(solution)/shard_map/pallas_call | solution.py:535
  147.8 40.7 %shard_map.84 = (bf16[16,64,256]{2,1,0:T(8,128)(2,1)}, bf16[2,2,256,256]{3,2,1,0:T(8,128)(2,1)}) custom-call(f32[8,64,256]{2,1,0:T(8,128)} %bitcast.30, bf16[24,64,256]{2,1,0:T(8,128)(2,1)} %get-tuple-element.12.st_ref, f32[8,1,1]{2,1,0:T(1,128)} %broadcast_in_dim_reshape.3.sh_ref, bf16[2,2,256,256]{3,2,1,0:T(8,128)(2,1)} %get-tuple-element.18.piece_ref), custom_call_target="tpu_custom_call" | custom-call | tf_op jit(solution)/shard_map/pallas_call | solution.py:505
  188.5 1.8 fusion.20
  190.4 0.1 copy.16
  190.5 3.2 %multiply_convert_fusion = bf16[8,2,256,256]{3,2,1,0:T(8,128)(2,1)} fusion(bf16[2,2,256,256]{3,2,1,0:T(8,128)(2,1)S(1)} %copy-done.6, bf16[2,2,256,256]{3,2,1,0:T(8,128)(2,1)S(1)} %copy-done.5, bf16[2,2,256,256]{3,2,1,0:T(8,128)(2,1)S(1)} %copy-done.4, bf16[2,2,256,256]{3,2,1,0:T(8,128)(2,1)S(1)} %copy-done.3, bf16[2,256,256]{2,1,0:T(8,128)(2,1)S(1)} %copy.16, ...), kind=kOutput, calls=%fused_computation | convolution fusion | flops 1085276160 | bytes 4718592 | tf_op jit(solution)/shard_map/tbij,tbjk->tbik/dot_general | solution.py:596
  (19 shorter events, 0.1 us)
Async XLA Ops:
  0.6 15.1 %copy-start.1 = (bf16[2,256,256]{2,1,0:T(8,128)(2,1)S(1)}, bf16[2,256,256]{2,1,0:T(8,128)(2,1)}, u32[]{:S(2)}) copy-start(bf16[2,256,256]{2,1,0:T(8,128)(2,1)} %param.6) | copy-start | bytes 786436
  0.6 11.7 %copy-start.7 = (f32[2]{0:T(128)S(1)}, f32[2]{0:T(128)}, u32[]{:S(2)}) copy-start(f32[2]{0:T(128)} %param.9) | copy-start | bytes 28
  0.7 12.4 %copy-start.2 = (s32[8,2]{0,1:T(2,128)S(1)}, s32[8,2]{0,1:T(2,128)}, u32[]{:S(2)}) copy-start(s32[8,2]{0,1:T(2,128)} %param.10) | copy-start | bytes 196
  0.7 15.0 %collective-permute-start = (bf16[2,256,256]{2,1,0:T(8,128)(2,1)}, bf16[2,256,256]{2,1,0:T(8,128)(2,1)S(1)}, u32[]{:S(2)}, u32[]{:S(2)}) collective-permute-start(bf16[2,256,256]{2,1,0:T(8,128)(2,1)} %param.6), channel_id=1, source_target_pairs={{0,8},{8,16},{16,24},{24,32},{32,40},{40,48},{48,56},{56,64},{64,7... | collective-permute-start | bytes 786440 | tf_op jit(solution)/shard_map/ppermute | solution.py:25
  3.2 12.6 %collective-permute-start.1 = (bf16[2,256,256]{2,1,0:T(8,128)(2,1)}, bf16[2,256,256]{2,1,0:T(8,128)(2,1)S(1)}, u32[]{:S(2)}, u32[]{:S(2)}) collective-permute-start(bf16[2,256,256]{2,1,0:T(8,128)(2,1)} %param.6), channel_id=1, source_target_pairs={{8,0},{16,8},{24,16},{32,24},{40,32},{48,40},{56,48},{64,56},{72,6... | collective-permute-start | bytes 786440 | tf_op jit(solution)/shard_map/ppermute | solution.py:27
  9.4 6.2 %collective-permute-start.2 = (s32[2]{0:T(128)}, s32[2]{0:T(128)S(1)}, u32[]{:S(2)}, u32[]{:S(2)}) collective-permute-start(s32[2]{0:T(128)} %param.11), channel_id=1, source_target_pairs={{248,0},{0,8},{8,16},{16,24},{24,32},{32,40},{40,48},{48,56},{56,6... | collective-permute-start | bytes 32 | tf_op jit(solution)/shard_map/ppermute | solution.py:559
  15.8 0.9 copy-start
  147.8 42.7 %copy-start.3 = (bf16[2,2,256,256]{3,2,1,0:T(8,128)(2,1)S(1)}, bf16[2,2,256,256]{3,2,1,0:T(8,128)(2,1)}, u32[]{:S(2)}) copy-start(bf16[2,2,256,256]{3,2,1,0:T(8,128)(2,1)} %get-tuple-element.14) | copy-start | bytes 1572868
  147.8 42.7 %copy-start.4 = (bf16[2,2,256,256]{3,2,1,0:T(8,128)(2,1)S(1)}, bf16[2,2,256,256]{3,2,1,0:T(8,128)(2,1)}, u32[]{:S(2)}) copy-start(bf16[2,2,256,256]{3,2,1,0:T(8,128)(2,1)} %get-tuple-element.15) | copy-start | bytes 1572868
  147.8 42.7 %copy-start.5 = (bf16[2,2,256,256]{3,2,1,0:T(8,128)(2,1)S(1)}, bf16[2,2,256,256]{3,2,1,0:T(8,128)(2,1)}, u32[]{:S(2)}) copy-start(bf16[2,2,256,256]{3,2,1,0:T(8,128)(2,1)} %get-tuple-element.16) | copy-start | bytes 1572868
  188.5 2.1 %copy-start.6 = (bf16[2,2,256,256]{3,2,1,0:T(8,128)(2,1)S(1)}, bf16[2,2,256,256]{3,2,1,0:T(8,128)(2,1)}, u32[]{:S(2)}) copy-start(bf16[2,2,256,256]{3,2,1,0:T(8,128)(2,1)} %get-tuple-element.17) | copy-start | bytes 1572868

commit v16 on v15

--- a/solution.py
+++ b/solution.py
@@ -371,10 +371,10 @@
         return copy_to(x_ref.at[j], rs_buf.at[me_op], send_rs.at[d], recv_rs.at[me_op], op_peer(j))
 
     pl.semaphore_wait(barrier, greeted)
-    for d in range(1, n_op):
-        rs_copy(d).start()
     a_args = (n_op, me_op, t_out, op_buf, send_a, recv_a, op_peer)
     start_gather(*a_args)
+    for d in range(1, n_op):
+        rs_copy(d).start()
     rs_buf[me_op] = x_ref[me_op]
 
     operators = copy_to(piece_ref, got_ref, send_w.at[send_w.shape[0] - 1],

time: 194 us -> 194 us (level)
  no operation moved by 1% of the time
where the time goes in v16:
time: 194 us
  Pallas kernels  172 us (89%)
  starting transfers between devices  8.77 us (5%)
  local copies, waits for them, and re-layouts  7.25 us (4%)
  matrix products  3.23 us (2%)
    pallas_call x4, Pallas kernels, step(): pl.pallas_call(functools.partial(step_kernel, n_sec, n_op, count, final),...  152 us
    pallas_call x4, Pallas kernels, sigma_part(): pl.pallas_call(sigma_part_kernel, out_shape=jax.ShapeDtypeStruct((sectors...  20 us
    ppermute x1, starting transfers between devices, padded(): lax.ppermute(head, axis, [((i + 1) % count, i) for i in range(count)])  6.22 us
  transfers between devices with their start and end apart: 3, of which 1 were waited for; matrix products, arithmetic and copies ran while one was open for 2% of the time, Pallas kernels for 0%

profile of v16, /device:TPU:1, one launch (start us, length us, event | category | flops | bytes accessed | tf_op | source)
XLA Modules:
  0.0 193.8 jit_solution(4122397503309131858)
XLA Ops:
  0.7 2.5 %collective-permute-start = (bf16[2,256,256]{2,1,0:T(8,128)(2,1)}, bf16[2,256,256]{2,1,0:T(8,128)(2,1)S(1)}, u32[]{:S(2)}, u32[]{:S(2)}) collective-permute-start(bf16[2,256,256]{2,1,0:T(8,128)(2,1)} %param.6), channel_id=1, source_target_pairs={{0,8},{8,16},{16,24},{24,32},{32,40},{40,48},{48,56},{56,64},{64,7... | collective-permute-start | bytes 786440 | tf_op jit(solution)/shard_map/ppermute | solution.py:25
  3.2 6.2 %collective-permute-start.1 = (bf16[2,256,256]{2,1,0:T(8,128)(2,1)}, bf16[2,256,256]{2,1,0:T(8,128)(2,1)S(1)}, u32[]{:S(2)}, u32[]{:S(2)}) collective-permute-start(bf16[2,256,256]{2,1,0:T(8,128)(2,1)} %param.6), channel_id=1, source_target_pairs={{8,0},{16,8},{24,16},{32,24},{40,32},{48,40},{56,48},{64,56},{72,6... | collective-permute-start | bytes 786440 | tf_op jit(solution)/shard_map/ppermute | solution.py:27
  9.4 0.0 collective-permute-start.2
  9.4 2.9 %fusion.19 = (bf16[2,2,256,256]{3,2,1,0:T(8,128)(2,1)}, bf16[2,2,256,256]{3,2,1,0:T(8,128)(2,1)}, bf16[2,2,256,256]{3,2,1,0:T(8,128)(2,1)}, bf16[2,2,256,256]{3,2,1,0:T(8,128)(2,1)}) fusion(bf16[8,2,256,256]{3,2,1,0:T(8,128)(2,1)} %left_ref.7), kind=kLoop, calls=%fused_computation.19 | loop fusion | bytes 4194304 | tf_op jit(solution)/shard_map/slice | solution.py:579
  12.3 0.1 broadcast_in_dim.4
  12.4 0.7 broadcast_in_dim_reshape.3.sh_ref
  13.1 0.7 copy.14.partner_ref
  13.8 1.9 collective-permute-done.2
  15.6 0.1 compare_convert_fusion
  15.7 0.0 collective-permute-done
  15.8 0.0 collective-permute-done.1
  15.8 0.0 copy-start
  15.8 0.9 copy-done
  16.7 5.0 %shard_map.77 = f32[2,256,256]{2,1,0:T(8,128)} custom-call(s32[8,2]{1,0:T(8,128)} %copy.14.partner_ref, bf16[6,256,256]{2,1,0:T(8,128)(2,1)} %copy-done, bf16[8,2,256,256]{3,2,1,0:T(8,128)(2,1)} %left_ref.7, bf16[8,2,256,256]{3,2,1,0:T(8,128)(2,1)} %right_ref.7), custom_call_target="tpu_custom_call" | custom-call | flops 1073741824 | bytes 5505024 | tf_op jit(solution)/shard_map/pallas_call | solution.py:535
  21.7 38.7 %shard_map.78 = (bf16[24,64,256]{2,1,0:T(8,128)(2,1)}, bf16[2,2,256,256]{3,2,1,0:T(8,128)(2,1)}) custom-call(f32[8,64,256]{2,1,0:T(8,128)} %bitcast.31, bf16[24,64,256]{2,1,0:T(8,128)(2,1)} %bitcast.24, f32[8,1,1]{2,1,0:T(1,128)} %broadcast_in_dim_reshape.3.sh_ref, bf16[2,2,256,256]{3,2,1,0:T(8,128)(2,1)} %get-tuple-element.21.piece_ref), custom_call_target="tpu_custom_call" | custom-call | tf_op jit(solution)/shard_map/pallas_call | solution.py:505
  60.4 5.0 %shard_map.79 = f32[2,256,256]{2,1,0:T(8,128)} custom-call(s32[8,2]{1,0:T(8,128)} %copy.14.partner_ref, bf16[6,256,256]{2,1,0:T(8,128)(2,1)} %bitcast.26, bf16[8,2,256,256]{3,2,1,0:T(8,128)(2,1)} %left_ref.7, bf16[8,2,256,256]{3,2,1,0:T(8,128)(2,1)} %right_ref.7), custom_call_target="tpu_custom_call" | custom-call | flops 1073741824 | bytes 5505024 | tf_op jit(solution)/shard_map/pallas_call | solution.py:535
  65.4 36.6 %shard_map.80 = (bf16[24,64,256]{2,1,0:T(8,128)(2,1)}, bf16[2,2,256,256]{3,2,1,0:T(8,128)(2,1)}) custom-call(f32[8,64,256]{2,1,0:T(8,128)} %bitcast.32, bf16[24,64,256]{2,1,0:T(8,128)(2,1)} %get-tuple-element.10.st_ref, f32[8,1,1]{2,1,0:T(1,128)} %broadcast_in_dim_reshape.3.sh_ref, bf16[2,2,256,256]{3,2,1,0:T(8,128)(2,1)} %get-tuple-element.20.piece_ref), custom_call_target="tpu_custom_call" | custom-call | tf_op jit(solution)/shard_map/pallas_call | solution.py:505
  102.0 5.0 %shard_map.81 = f32[2,256,256]{2,1,0:T(8,128)} custom-call(s32[8,2]{1,0:T(8,128)} %copy.14.partner_ref, bf16[6,256,256]{2,1,0:T(8,128)(2,1)} %bitcast.27, bf16[8,2,256,256]{3,2,1,0:T(8,128)(2,1)} %left_ref.7, bf16[8,2,256,256]{3,2,1,0:T(8,128)(2,1)} %right_ref.7), custom_call_target="tpu_custom_call" | custom-call | flops 1073741824 | bytes 5505024 | tf_op jit(solution)/shard_map/pallas_call | solution.py:535
  107.0 35.7 %shard_map.82 = (bf16[24,64,256]{2,1,0:T(8,128)(2,1)}, bf16[2,2,256,256]{3,2,1,0:T(8,128)(2,1)}) custom-call(f32[8,64,256]{2,1,0:T(8,128)} %bitcast.33, bf16[24,64,256]{2,1,0:T(8,128)(2,1)} %get-tuple-element.11.st_ref, f32[8,1,1]{2,1,0:T(1,128)} %broadcast_in_dim_reshape.3.sh_ref, bf16[2,2,256,256]{3,2,1,0:T(8,128)(2,1)} %get-tuple-element.19.piece_ref), custom_call_target="tpu_custom_call" | custom-call | tf_op jit(solution)/shard_map/pallas_call | solution.py:505
  142.7 5.0 %shard_map.83 = f32[2,256,256]{2,1,0:T(8,128)} custom-call(s32[8,2]{1,0:T(8,128)} %copy.14.partner_ref, bf16[6,256,256]{2,1,0:T(8,128)(2,1)} %bitcast.25, bf16[8,2,256,256]{3,2,1,0:T(8,128)(2,1)} %left_ref.7, bf16[8,2,256,256]{3,2,1,0:T(8,128)(2,1)} %right_ref.7), custom_call_target="tpu_custom_call" | custom-call | flops 1073741824 | bytes 5505024 | tf_op jit(solution)/shard_map/pallas_call | solution.py:535
  147.7 40.7 %shard_map.84 = (bf16[16,64,256]{2,1,0:T(8,128)(2,1)}, bf16[2,2,256,256]{3,2,1,0:T(8,128)(2,1)}) custom-call(f32[8,64,256]{2,1,0:T(8,128)} %bitcast.30, bf16[24,64,256]{2,1,0:T(8,128)(2,1)} %get-tuple-element.12.st_ref, f32[8,1,1]{2,1,0:T(1,128)} %broadcast_in_dim_reshape.3.sh_ref, bf16[2,2,256,256]{3,2,1,0:T(8,128)(2,1)} %get-tuple-element.18.piece_ref), custom_call_target="tpu_custom_call" | custom-call | tf_op jit(solution)/shard_map/pallas_call | solution.py:505
  188.5 1.8 fusion.20
  190.4 0.1 copy.16
  190.5 3.2 %multiply_convert_fusion = bf16[8,2,256,256]{3,2,1,0:T(8,128)(2,1)} fusion(bf16[2,2,256,256]{3,2,1,0:T(8,128)(2,1)S(1)} %copy-done.6, bf16[2,2,256,256]{3,2,1,0:T(8,128)(2,1)S(1)} %copy-done.5, bf16[2,2,256,256]{3,2,1,0:T(8,128)(2,1)S(1)} %copy-done.4, bf16[2,2,256,256]{3,2,1,0:T(8,128)(2,1)S(1)} %copy-done.3, bf16[2,256,256]{2,1,0:T(8,128)(2,1)S(1)} %copy.16, ...), kind=kOutput, calls=%fused_computation | convolution fusion | flops 1085276160 | bytes 4718592 | tf_op jit(solution)/shard_map/tbij,tbjk->tbik/dot_general | solution.py:596
  (19 shorter events, 0.1 us)
Async XLA Ops:
  0.6 15.1 %copy-start.1 = (bf16[2,256,256]{2,1,0:T(8,128)(2,1)S(1)}, bf16[2,256,256]{2,1,0:T(8,128)(2,1)}, u32[]{:S(2)}) copy-start(bf16[2,256,256]{2,1,0:T(8,128)(2,1)} %param.6) | copy-start | bytes 786436
  0.6 11.7 %copy-start.7 = (f32[2]{0:T(128)S(1)}, f32[2]{0:T(128)}, u32[]{:S(2)}) copy-start(f32[2]{0:T(128)} %param.9) | copy-start | bytes 28
  0.7 12.4 %copy-start.2 = (s32[8,2]{0,1:T(2,128)S(1)}, s32[8,2]{0,1:T(2,128)}, u32[]{:S(2)}) copy-start(s32[8,2]{0,1:T(2,128)} %param.10) | copy-start | bytes 196
  0.7 15.0 %collective-permute-start = (bf16[2,256,256]{2,1,0:T(8,128)(2,1)}, bf16[2,256,256]{2,1,0:T(8,128)(2,1)S(1)}, u32[]{:S(2)}, u32[]{:S(2)}) collective-permute-start(bf16[2,256,256]{2,1,0:T(8,128)(2,1)} %param.6), channel_id=1, source_target_pairs={{0,8},{8,16},{16,24},{24,32},{32,40},{40,48},{48,56},{56,64},{64,7... | collective-permute-start | bytes 786440 | tf_op jit(solution)/shard_map/ppermute | solution.py:25
  3.2 12.6 %collective-permute-start.1 = (bf16[2,256,256]{2,1,0:T(8,128)(2,1)}, bf16[2,256,256]{2,1,0:T(8,128)(2,1)S(1)}, u32[]{:S(2)}, u32[]{:S(2)}) collective-permute-start(bf16[2,256,256]{2,1,0:T(8,128)(2,1)} %param.6), channel_id=1, source_target_pairs={{8,0},{16,8},{24,16},{32,24},{40,32},{48,40},{56,48},{64,56},{72,6... | collective-permute-start | bytes 786440 | tf_op jit(solution)/shard_map/ppermute | solution.py:27
  9.4 6.2 %collective-permute-start.2 = (s32[2]{0:T(128)}, s32[2]{0:T(128)S(1)}, u32[]{:S(2)}, u32[]{:S(2)}) collective-permute-start(s32[2]{0:T(128)} %param.11), channel_id=1, source_target_pairs={{248,0},{0,8},{8,16},{16,24},{24,32},{32,40},{40,48},{48,56},{56,6... | collective-permute-start | bytes 32 | tf_op jit(solution)/shard_map/ppermute | solution.py:559
  15.8 0.9 copy-start
  147.7 42.8 %copy-start.3 = (bf16[2,2,256,256]{3,2,1,0:T(8,128)(2,1)S(1)}, bf16[2,2,256,256]{3,2,1,0:T(8,128)(2,1)}, u32[]{:S(2)}) copy-start(bf16[2,2,256,256]{3,2,1,0:T(8,128)(2,1)} %get-tuple-element.14) | copy-start | bytes 1572868
  147.7 42.8 %copy-start.4 = (bf16[2,2,256,256]{3,2,1,0:T(8,128)(2,1)S(1)}, bf16[2,2,256,256]{3,2,1,0:T(8,128)(2,1)}, u32[]{:S(2)}) copy-start(bf16[2,2,256,256]{3,2,1,0:T(8,128)(2,1)} %get-tuple-element.15) | copy-start | bytes 1572868
  147.7 42.8 %copy-start.5 = (bf16[2,2,256,256]{3,2,1,0:T(8,128)(2,1)S(1)}, bf16[2,2,256,256]{3,2,1,0:T(8,128)(2,1)}, u32[]{:S(2)}) copy-start(bf16[2,2,256,256]{3,2,1,0:T(8,128)(2,1)} %get-tuple-element.16) | copy-start | bytes 1572868
  188.5 2.1 %copy-start.6 = (bf16[2,2,256,256]{3,2,1,0:T(8,128)(2,1)S(1)}, bf16[2,2,256,256]{3,2,1,0:T(8,128)(2,1)}, u32[]{:S(2)}) copy-start(bf16[2,2,256,256]{3,2,1,0:T(8,128)(2,1)} %get-tuple-element.17) | copy-start | bytes 1572868

commit v17 on v16

--- a/solution.py
+++ b/solution.py
@@ -377,14 +377,14 @@
         rs_copy(d).start()
     rs_buf[me_op] = x_ref[me_op]
 
-    operators = copy_to(piece_ref, got_ref, send_w.at[send_w.shape[0] - 1],
-                        recv_w.at[recv_w.shape[0] - 1], (next_sec, me_op))
-    operators.start()
 
     wait_gather(*a_args)
     mid[...] = ordered_sum(op_buf, n_op)
     settle(mid, mid_out, local_sem.at[0])
     start_rows(mid_out, sec_buf, send_b, recv_b)
+    operators = copy_to(piece_ref, got_ref, send_w.at[send_w.shape[0] - 1],
+                        recv_w.at[recv_w.shape[0] - 1], (next_sec, me_op))
+    operators.start()
 
     for d in range(1, n_op):
         slot = (me_op + n_op - d) % n_op

time: 194 us -> 210 us (1.082)
  Pallas kernels: 172 us -> 186 us
    pallas_call x4, Pallas kernels: 152 us -> 166 us  [step(): pl.pallas_call(functools.partial(step_kernel, n_sec, n_op, count, final),...]
where the time goes in v17:
time: 210 us; the launch traced here: 208 us
  Pallas kernels  186 us (89%)
  starting transfers between devices  8.77 us (4%)
  local copies, waits for them, and re-layouts  7.25 us (3%)
  matrix products  3.23 us (2%)
    pallas_call x4, Pallas kernels, step(): pl.pallas_call(functools.partial(step_kernel, n_sec, n_op, count, final),...  166 us
    pallas_call x4, Pallas kernels, sigma_part(): pl.pallas_call(sigma_part_kernel, out_shape=jax.ShapeDtypeStruct((sectors...  20 us
    ppermute x1, starting transfers between devices, padded(): lax.ppermute(head, axis, [((i + 1) % count, i) for i in range(count)])  6.22 us
  transfers between devices with their start and end apart: 3, of which 1 were waited for; matrix products, arithmetic and copies ran while one was open for 2% of the time, Pallas kernels for 0%

profile of v17, /device:TPU:1, one launch (start us, length us, event | category | flops | bytes accessed | tf_op | source)
XLA Modules:
  0.0 208.2 jit_solution(15973352156504312166)
XLA Ops:
  0.7 2.5 %collective-permute-start = (bf16[2,256,256]{2,1,0:T(8,128)(2,1)}, bf16[2,256,256]{2,1,0:T(8,128)(2,1)S(1)}, u32[]{:S(2)}, u32[]{:S(2)}) collective-permute-start(bf16[2,256,256]{2,1,0:T(8,128)(2,1)} %param.6), channel_id=1, source_target_pairs={{0,8},{8,16},{16,24},{24,32},{32,40},{40,48},{48,56},{56,64},{64,7... | collective-permute-start | bytes 786440 | tf_op jit(solution)/shard_map/ppermute | solution.py:25
  3.2 6.2 %collective-permute-start.1 = (bf16[2,256,256]{2,1,0:T(8,128)(2,1)}, bf16[2,256,256]{2,1,0:T(8,128)(2,1)S(1)}, u32[]{:S(2)}, u32[]{:S(2)}) collective-permute-start(bf16[2,256,256]{2,1,0:T(8,128)(2,1)} %param.6), channel_id=1, source_target_pairs={{8,0},{16,8},{24,16},{32,24},{40,32},{48,40},{56,48},{64,56},{72,6... | collective-permute-start | bytes 786440 | tf_op jit(solution)/shard_map/ppermute | solution.py:27
  9.4 0.0 collective-permute-start.2
  9.4 2.9 %fusion.19 = (bf16[2,2,256,256]{3,2,1,0:T(8,128)(2,1)}, bf16[2,2,256,256]{3,2,1,0:T(8,128)(2,1)}, bf16[2,2,256,256]{3,2,1,0:T(8,128)(2,1)}, bf16[2,2,256,256]{3,2,1,0:T(8,128)(2,1)}) fusion(bf16[8,2,256,256]{3,2,1,0:T(8,128)(2,1)} %left_ref.7), kind=kLoop, calls=%fused_computation.19 | loop fusion | bytes 4194304 | tf_op jit(solution)/shard_map/slice | solution.py:579
  12.3 0.1 broadcast_in_dim.4
  12.4 0.7 broadcast_in_dim_reshape.3.sh_ref
  13.1 0.7 copy.14.partner_ref
  13.8 1.9 collective-permute-done.2
  15.6 0.1 compare_convert_fusion
  15.7 0.0 collective-permute-done
  15.8 0.0 collective-permute-done.1
  15.8 0.0 copy-start
  15.8 0.9 copy-done
  16.7 5.0 %shard_map.77 = f32[2,256,256]{2,1,0:T(8,128)} custom-call(s32[8,2]{1,0:T(8,128)} %copy.14.partner_ref, bf16[6,256,256]{2,1,0:T(8,128)(2,1)} %copy-done, bf16[8,2,256,256]{3,2,1,0:T(8,128)(2,1)} %left_ref.7, bf16[8,2,256,256]{3,2,1,0:T(8,128)(2,1)} %right_ref.7), custom_call_target="tpu_custom_call" | custom-call | flops 1073741824 | bytes 5505024 | tf_op jit(solution)/shard_map/pallas_call | solution.py:535
  21.7 41.3 %shard_map.78 = (bf16[24,64,256]{2,1,0:T(8,128)(2,1)}, bf16[2,2,256,256]{3,2,1,0:T(8,128)(2,1)}) custom-call(f32[8,64,256]{2,1,0:T(8,128)} %bitcast.31, bf16[24,64,256]{2,1,0:T(8,128)(2,1)} %bitcast.24, f32[8,1,1]{2,1,0:T(1,128)} %broadcast_in_dim_reshape.3.sh_ref, bf16[2,2,256,256]{3,2,1,0:T(8,128)(2,1)} %get-tuple-element.21.piece_ref), custom_call_target="tpu_custom_call" | custom-call | tf_op jit(solution)/shard_map/pallas_call | solution.py:505
  63.0 5.0 %shard_map.79 = f32[2,256,256]{2,1,0:T(8,128)} custom-call(s32[8,2]{1,0:T(8,128)} %copy.14.partner_ref, bf16[6,256,256]{2,1,0:T(8,128)(2,1)} %bitcast.26, bf16[8,2,256,256]{3,2,1,0:T(8,128)(2,1)} %left_ref.7, bf16[8,2,256,256]{3,2,1,0:T(8,128)(2,1)} %right_ref.7), custom_call_target="tpu_custom_call" | custom-call | flops 1073741824 | bytes 5505024 | tf_op jit(solution)/shard_map/pallas_call | solution.py:535
  68.0 40.1 %shard_map.80 = (bf16[24,64,256]{2,1,0:T(8,128)(2,1)}, bf16[2,2,256,256]{3,2,1,0:T(8,128)(2,1)}) custom-call(f32[8,64,256]{2,1,0:T(8,128)} %bitcast.32, bf16[24,64,256]{2,1,0:T(8,128)(2,1)} %get-tuple-element.10.st_ref, f32[8,1,1]{2,1,0:T(1,128)} %broadcast_in_dim_reshape.3.sh_ref, bf16[2,2,256,256]{3,2,1,0:T(8,128)(2,1)} %get-tuple-element.20.piece_ref), custom_call_target="tpu_custom_call" | custom-call | tf_op jit(solution)/shard_map/pallas_call | solution.py:505
  108.1 5.0 %shard_map.81 = f32[2,256,256]{2,1,0:T(8,128)} custom-call(s32[8,2]{1,0:T(8,128)} %copy.14.partner_ref, bf16[6,256,256]{2,1,0:T(8,128)(2,1)} %bitcast.27, bf16[8,2,256,256]{3,2,1,0:T(8,128)(2,1)} %left_ref.7, bf16[8,2,256,256]{3,2,1,0:T(8,128)(2,1)} %right_ref.7), custom_call_target="tpu_custom_call" | custom-call | flops 1073741824 | bytes 5505024 | tf_op jit(solution)/shard_map/pallas_call | solution.py:535
  113.1 40.2 %shard_map.82 = (bf16[24,64,256]{2,1,0:T(8,128)(2,1)}, bf16[2,2,256,256]{3,2,1,0:T(8,128)(2,1)}) custom-call(f32[8,64,256]{2,1,0:T(8,128)} %bitcast.33, bf16[24,64,256]{2,1,0:T(8,128)(2,1)} %get-tuple-element.11.st_ref, f32[8,1,1]{2,1,0:T(1,128)} %broadcast_in_dim_reshape.3.sh_ref, bf16[2,2,256,256]{3,2,1,0:T(8,128)(2,1)} %get-tuple-element.19.piece_ref), custom_call_target="tpu_custom_call" | custom-call | tf_op jit(solution)/shard_map/pallas_call | solution.py:505
  153.3 5.0 %shard_map.83 = f32[2,256,256]{2,1,0:T(8,128)} custom-call(s32[8,2]{1,0:T(8,128)} %copy.14.partner_ref, bf16[6,256,256]{2,1,0:T(8,128)(2,1)} %bitcast.25, bf16[8,2,256,256]{3,2,1,0:T(8,128)(2,1)} %left_ref.7, bf16[8,2,256,256]{3,2,1,0:T(8,128)(2,1)} %right_ref.7), custom_call_target="tpu_custom_call" | custom-call | flops 1073741824 | bytes 5505024 | tf_op jit(solution)/shard_map/pallas_call | solution.py:535
  158.3 44.6 %shard_map.84 = (bf16[16,64,256]{2,1,0:T(8,128)(2,1)}, bf16[2,2,256,256]{3,2,1,0:T(8,128)(2,1)}) custom-call(f32[8,64,256]{2,1,0:T(8,128)} %bitcast.30, bf16[24,64,256]{2,1,0:T(8,128)(2,1)} %get-tuple-element.12.st_ref, f32[8,1,1]{2,1,0:T(1,128)} %broadcast_in_dim_reshape.3.sh_ref, bf16[2,2,256,256]{3,2,1,0:T(8,128)(2,1)} %get-tuple-element.18.piece_ref), custom_call_target="tpu_custom_call" | custom-call | tf_op jit(solution)/shard_map/pallas_call | solution.py:505
  202.9 1.8 fusion.20
  204.8 0.1 copy.16
  205.0 3.2 %multiply_convert_fusion = bf16[8,2,256,256]{3,2,1,0:T(8,128)(2,1)} fusion(bf16[2,2,256,256]{3,2,1,0:T(8,128)(2,1)S(1)} %copy-done.6, bf16[2,2,256,256]{3,2,1,0:T(8,128)(2,1)S(1)} %copy-done.5, bf16[2,2,256,256]{3,2,1,0:T(8,128)(2,1)S(1)} %copy-done.4, bf16[2,2,256,256]{3,2,1,0:T(8,128)(2,1)S(1)} %copy-done.3, bf16[2,256,256]{2,1,0:T(8,128)(2,1)S(1)} %copy.16, ...), kind=kOutput, calls=%fused_computation | convolution fusion | flops 1085276160 | bytes 4718592 | tf_op jit(solution)/shard_map/tbij,tbjk->tbik/dot_general | solution.py:596
  (19 shorter events, 0.1 us)
Async XLA Ops:
  0.6 15.1 %copy-start.1 = (bf16[2,256,256]{2,1,0:T(8,128)(2,1)S(1)}, bf16[2,256,256]{2,1,0:T(8,128)(2,1)}, u32[]{:S(2)}) copy-start(bf16[2,256,256]{2,1,0:T(8,128)(2,1)} %param.6) | copy-start | bytes 786436
  0.6 11.7 %copy-start.7 = (f32[2]{0:T(128)S(1)}, f32[2]{0:T(128)}, u32[]{:S(2)}) copy-start(f32[2]{0:T(128)} %param.9) | copy-start | bytes 28
  0.7 12.4 %copy-start.2 = (s32[8,2]{0,1:T(2,128)S(1)}, s32[8,2]{0,1:T(2,128)}, u32[]{:S(2)}) copy-start(s32[8,2]{0,1:T(2,128)} %param.10) | copy-start | bytes 196
  0.7 15.0 %collective-permute-start = (bf16[2,256,256]{2,1,0:T(8,128)(2,1)}, bf16[2,256,256]{2,1,0:T(8,128)(2,1)S(1)}, u32[]{:S(2)}, u32[]{:S(2)}) collective-permute-start(bf16[2,256,256]{2,1,0:T(8,128)(2,1)} %param.6), channel_id=1, source_target_pairs={{0,8},{8,16},{16,24},{24,32},{32,40},{40,48},{48,56},{56,64},{64,7... | collective-permute-start | bytes 786440 | tf_op jit(solution)/shard_map/ppermute | solution.py:25
  3.2 12.6 %collective-permute-start.1 = (bf16[2,256,256]{2,1,0:T(8,128)(2,1)}, bf16[2,256,256]{2,1,0:T(8,128)(2,1)S(1)}, u32[]{:S(2)}, u32[]{:S(2)}) collective-permute-start(bf16[2,256,256]{2,1,0:T(8,128)(2,1)} %param.6), channel_id=1, source_target_pairs={{8,0},{16,8},{24,16},{32,24},{40,32},{48,40},{56,48},{64,56},{72,6... | collective-permute-start | bytes 786440 | tf_op jit(solution)/shard_map/ppermute | solution.py:27
  9.4 6.2 %collective-permute-start.2 = (s32[2]{0:T(128)}, s32[2]{0:T(128)S(1)}, u32[]{:S(2)}, u32[]{:S(2)}) collective-permute-start(s32[2]{0:T(128)} %param.11), channel_id=1, source_target_pairs={{248,0},{0,8},{8,16},{16,24},{24,32},{32,40},{40,48},{48,56},{56,6... | collective-permute-start | bytes 32 | tf_op jit(solution)/shard_map/ppermute | solution.py:559
  15.8 0.9 copy-start
  158.3 46.7 %copy-start.3 = (bf16[2,2,256,256]{3,2,1,0:T(8,128)(2,1)S(1)}, bf16[2,2,256,256]{3,2,1,0:T(8,128)(2,1)}, u32[]{:S(2)}) copy-start(bf16[2,2,256,256]{3,2,1,0:T(8,128)(2,1)} %get-tuple-element.14) | copy-start | bytes 1572868
  158.3 46.7 %copy-start.4 = (bf16[2,2,256,256]{3,2,1,0:T(8,128)(2,1)S(1)}, bf16[2,2,256,256]{3,2,1,0:T(8,128)(2,1)}, u32[]{:S(2)}) copy-start(bf16[2,2,256,256]{3,2,1,0:T(8,128)(2,1)} %get-tuple-element.15) | copy-start | bytes 1572868
  158.3 46.7 %copy-start.5 = (bf16[2,2,256,256]{3,2,1,0:T(8,128)(2,1)S(1)}, bf16[2,2,256,256]{3,2,1,0:T(8,128)(2,1)}, u32[]{:S(2)}) copy-start(bf16[2,2,256,256]{3,2,1,0:T(8,128)(2,1)} %get-tuple-element.16) | copy-start | bytes 1572868
  202.9 2.1 copy-start.6

commit v18 on v15

--- a/solution.py
+++ b/solution.py
@@ -404,7 +404,7 @@
     new_buf[...] = (updated * factor).astype(new_buf.dtype)
     settle(new_buf, new_out, local_sem.at[2])
 
-    sides = ((next_sec, 0),) if final else ((next_sec, 0), (prev_sec, 2 * n_op))
+    sides = ((next_sec, 0),) if final else ((prev_sec, 2 * n_op), (next_sec, 0))
     sent = 0
     for side, base in sides:
         for j in range(n_op):

time: 194 us -> 194 us (level)
  no operation moved by 1% of the time
where the time goes in v18:
time: 194 us
  Pallas kernels  172 us (89%)
  starting transfers between devices  8.77 us (5%)
  local copies, waits for them, and re-layouts  7.25 us (4%)
  matrix products  3.23 us (2%)
    pallas_call x4, Pallas kernels, step(): pl.pallas_call(functools.partial(step_kernel, n_sec, n_op, count, final),...  152 us
    pallas_call x4, Pallas kernels, sigma_part(): pl.pallas_call(sigma_part_kernel, out_shape=jax.ShapeDtypeStruct((sectors...  20 us
    ppermute x1, starting transfers between devices, padded(): lax.ppermute(head, axis, [((i + 1) % count, i) for i in range(count)])  6.22 us
  transfers between devices with their start and end apart: 3, of which 1 were waited for; matrix products, arithmetic and copies ran while one was open for 2% of the time, Pallas kernels for 0%

profile of v18, /device:TPU:1, one launch (start us, length us, event | category | flops | bytes accessed | tf_op | source)
XLA Modules:
  0.0 193.8 jit_solution(16215383612037701870)
XLA Ops:
  0.7 2.5 %collective-permute-start = (bf16[2,256,256]{2,1,0:T(8,128)(2,1)}, bf16[2,256,256]{2,1,0:T(8,128)(2,1)S(1)}, u32[]{:S(2)}, u32[]{:S(2)}) collective-permute-start(bf16[2,256,256]{2,1,0:T(8,128)(2,1)} %param.6), channel_id=1, source_target_pairs={{0,8},{8,16},{16,24},{24,32},{32,40},{40,48},{48,56},{56,64},{64,7... | collective-permute-start | bytes 786440 | tf_op jit(solution)/shard_map/ppermute | solution.py:25
  3.2 6.2 %collective-permute-start.1 = (bf16[2,256,256]{2,1,0:T(8,128)(2,1)}, bf16[2,256,256]{2,1,0:T(8,128)(2,1)S(1)}, u32[]{:S(2)}, u32[]{:S(2)}) collective-permute-start(bf16[2,256,256]{2,1,0:T(8,128)(2,1)} %param.6), channel_id=1, source_target_pairs={{8,0},{16,8},{24,16},{32,24},{40,32},{48,40},{56,48},{64,56},{72,6... | collective-permute-start | bytes 786440 | tf_op jit(solution)/shard_map/ppermute | solution.py:27
  9.4 0.0 collective-permute-start.2
  9.4 2.9 %fusion.19 = (bf16[2,2,256,256]{3,2,1,0:T(8,128)(2,1)}, bf16[2,2,256,256]{3,2,1,0:T(8,128)(2,1)}, bf16[2,2,256,256]{3,2,1,0:T(8,128)(2,1)}, bf16[2,2,256,256]{3,2,1,0:T(8,128)(2,1)}) fusion(bf16[8,2,256,256]{3,2,1,0:T(8,128)(2,1)} %left_ref.7), kind=kLoop, calls=%fused_computation.19 | loop fusion | bytes 4194304 | tf_op jit(solution)/shard_map/slice | solution.py:579
  12.3 0.1 broadcast_in_dim.4
  12.4 0.7 broadcast_in_dim_reshape.3.sh_ref
  13.1 0.7 copy.14.partner_ref
  13.8 1.9 collective-permute-done.2
  15.6 0.1 compare_convert_fusion
  15.7 0.0 collective-permute-done
  15.8 0.0 collective-permute-done.1
  15.8 0.0 copy-start
  15.8 0.9 copy-done
  16.7 5.0 %shard_map.77 = f32[2,256,256]{2,1,0:T(8,128)} custom-call(s32[8,2]{1,0:T(8,128)} %copy.14.partner_ref, bf16[6,256,256]{2,1,0:T(8,128)(2,1)} %copy-done, bf16[8,2,256,256]{3,2,1,0:T(8,128)(2,1)} %left_ref.7, bf16[8,2,256,256]{3,2,1,0:T(8,128)(2,1)} %right_ref.7), custom_call_target="tpu_custom_call" | custom-call | flops 1073741824 | bytes 5505024 | tf_op jit(solution)/shard_map/pallas_call | solution.py:535
  21.7 38.7 %shard_map.78 = (bf16[24,64,256]{2,1,0:T(8,128)(2,1)}, bf16[2,2,256,256]{3,2,1,0:T(8,128)(2,1)}) custom-call(f32[8,64,256]{2,1,0:T(8,128)} %bitcast.31, bf16[24,64,256]{2,1,0:T(8,128)(2,1)} %bitcast.24, f32[8,1,1]{2,1,0:T(1,128)} %broadcast_in_dim_reshape.3.sh_ref, bf16[2,2,256,256]{3,2,1,0:T(8,128)(2,1)} %get-tuple-element.21.piece_ref), custom_call_target="tpu_custom_call" | custom-call | tf_op jit(solution)/shard_map/pallas_call | solution.py:505
  60.4 5.0 %shard_map.79 = f32[2,256,256]{2,1,0:T(8,128)} custom-call(s32[8,2]{1,0:T(8,128)} %copy.14.partner_ref, bf16[6,256,256]{2,1,0:T(8,128)(2,1)} %bitcast.26, bf16[8,2,256,256]{3,2,1,0:T(8,128)(2,1)} %left_ref.7, bf16[8,2,256,256]{3,2,1,0:T(8,128)(2,1)} %right_ref.7), custom_call_target="tpu_custom_call" | custom-call | flops 1073741824 | bytes 5505024 | tf_op jit(solution)/shard_map/pallas_call | solution.py:535
  65.4 36.8 %shard_map.80 = (bf16[24,64,256]{2,1,0:T(8,128)(2,1)}, bf16[2,2,256,256]{3,2,1,0:T(8,128)(2,1)}) custom-call(f32[8,64,256]{2,1,0:T(8,128)} %bitcast.32, bf16[24,64,256]{2,1,0:T(8,128)(2,1)} %get-tuple-element.10.st_ref, f32[8,1,1]{2,1,0:T(1,128)} %broadcast_in_dim_reshape.3.sh_ref, bf16[2,2,256,256]{3,2,1,0:T(8,128)(2,1)} %get-tuple-element.20.piece_ref), custom_call_target="tpu_custom_call" | custom-call | tf_op jit(solution)/shard_map/pallas_call | solution.py:505
  102.2 5.0 %shard_map.81 = f32[2,256,256]{2,1,0:T(8,128)} custom-call(s32[8,2]{1,0:T(8,128)} %copy.14.partner_ref, bf16[6,256,256]{2,1,0:T(8,128)(2,1)} %bitcast.27, bf16[8,2,256,256]{3,2,1,0:T(8,128)(2,1)} %left_ref.7, bf16[8,2,256,256]{3,2,1,0:T(8,128)(2,1)} %right_ref.7), custom_call_target="tpu_custom_call" | custom-call | flops 1073741824 | bytes 5505024 | tf_op jit(solution)/shard_map/pallas_call | solution.py:535
  107.2 35.5 %shard_map.82 = (bf16[24,64,256]{2,1,0:T(8,128)(2,1)}, bf16[2,2,256,256]{3,2,1,0:T(8,128)(2,1)}) custom-call(f32[8,64,256]{2,1,0:T(8,128)} %bitcast.33, bf16[24,64,256]{2,1,0:T(8,128)(2,1)} %get-tuple-element.11.st_ref, f32[8,1,1]{2,1,0:T(1,128)} %broadcast_in_dim_reshape.3.sh_ref, bf16[2,2,256,256]{3,2,1,0:T(8,128)(2,1)} %get-tuple-element.19.piece_ref), custom_call_target="tpu_custom_call" | custom-call | tf_op jit(solution)/shard_map/pallas_call | solution.py:505
  142.8 5.0 %shard_map.83 = f32[2,256,256]{2,1,0:T(8,128)} custom-call(s32[8,2]{1,0:T(8,128)} %copy.14.partner_ref, bf16[6,256,256]{2,1,0:T(8,128)(2,1)} %bitcast.25, bf16[8,2,256,256]{3,2,1,0:T(8,128)(2,1)} %left_ref.7, bf16[8,2,256,256]{3,2,1,0:T(8,128)(2,1)} %right_ref.7), custom_call_target="tpu_custom_call" | custom-call | flops 1073741824 | bytes 5505024 | tf_op jit(solution)/shard_map/pallas_call | solution.py:535
  147.8 40.7 %shard_map.84 = (bf16[16,64,256]{2,1,0:T(8,128)(2,1)}, bf16[2,2,256,256]{3,2,1,0:T(8,128)(2,1)}) custom-call(f32[8,64,256]{2,1,0:T(8,128)} %bitcast.30, bf16[24,64,256]{2,1,0:T(8,128)(2,1)} %get-tuple-element.12.st_ref, f32[8,1,1]{2,1,0:T(1,128)} %broadcast_in_dim_reshape.3.sh_ref, bf16[2,2,256,256]{3,2,1,0:T(8,128)(2,1)} %get-tuple-element.18.piece_ref), custom_call_target="tpu_custom_call" | custom-call | tf_op jit(solution)/shard_map/pallas_call | solution.py:505
  188.5 1.8 fusion.20
  190.4 0.1 copy.16
  190.5 3.2 %multiply_convert_fusion = bf16[8,2,256,256]{3,2,1,0:T(8,128)(2,1)} fusion(bf16[2,2,256,256]{3,2,1,0:T(8,128)(2,1)S(1)} %copy-done.6, bf16[2,2,256,256]{3,2,1,0:T(8,128)(2,1)S(1)} %copy-done.5, bf16[2,2,256,256]{3,2,1,0:T(8,128)(2,1)S(1)} %copy-done.4, bf16[2,2,256,256]{3,2,1,0:T(8,128)(2,1)S(1)} %copy-done.3, bf16[2,256,256]{2,1,0:T(8,128)(2,1)S(1)} %copy.16, ...), kind=kOutput, calls=%fused_computation | convolution fusion | flops 1085276160 | bytes 4718592 | tf_op jit(solution)/shard_map/tbij,tbjk->tbik/dot_general | solution.py:596
  (19 shorter events, 0.1 us)
Async XLA Ops:
  0.6 15.1 %copy-start.1 = (bf16[2,256,256]{2,1,0:T(8,128)(2,1)S(1)}, bf16[2,256,256]{2,1,0:T(8,128)(2,1)}, u32[]{:S(2)}) copy-start(bf16[2,256,256]{2,1,0:T(8,128)(2,1)} %param.6) | copy-start | bytes 786436
  0.6 11.7 %copy-start.7 = (f32[2]{0:T(128)S(1)}, f32[2]{0:T(128)}, u32[]{:S(2)}) copy-start(f32[2]{0:T(128)} %param.9) | copy-start | bytes 28
  0.7 12.4 %copy-start.2 = (s32[8,2]{0,1:T(2,128)S(1)}, s32[8,2]{0,1:T(2,128)}, u32[]{:S(2)}) copy-start(s32[8,2]{0,1:T(2,128)} %param.10) | copy-start | bytes 196
  0.7 15.0 %collective-permute-start = (bf16[2,256,256]{2,1,0:T(8,128)(2,1)}, bf16[2,256,256]{2,1,0:T(8,128)(2,1)S(1)}, u32[]{:S(2)}, u32[]{:S(2)}) collective-permute-start(bf16[2,256,256]{2,1,0:T(8,128)(2,1)} %param.6), channel_id=1, source_target_pairs={{0,8},{8,16},{16,24},{24,32},{32,40},{40,48},{48,56},{56,64},{64,7... | collective-permute-start | bytes 786440 | tf_op jit(solution)/shard_map/ppermute | solution.py:25
  3.2 12.6 %collective-permute-start.1 = (bf16[2,256,256]{2,1,0:T(8,128)(2,1)}, bf16[2,256,256]{2,1,0:T(8,128)(2,1)S(1)}, u32[]{:S(2)}, u32[]{:S(2)}) collective-permute-start(bf16[2,256,256]{2,1,0:T(8,128)(2,1)} %param.6), channel_id=1, source_target_pairs={{8,0},{16,8},{24,16},{32,24},{40,32},{48,40},{56,48},{64,56},{72,6... | collective-permute-start | bytes 786440 | tf_op jit(solution)/shard_map/ppermute | solution.py:27
  9.4 6.2 %collective-permute-start.2 = (s32[2]{0:T(128)}, s32[2]{0:T(128)S(1)}, u32[]{:S(2)}, u32[]{:S(2)}) collective-permute-start(s32[2]{0:T(128)} %param.11), channel_id=1, source_target_pairs={{248,0},{0,8},{8,16},{16,24},{24,32},{32,40},{40,48},{48,56},{56,6... | collective-permute-start | bytes 32 | tf_op jit(solution)/shard_map/ppermute | solution.py:559
  15.8 0.9 copy-start
  147.8 42.7 %copy-start.3 = (bf16[2,2,256,256]{3,2,1,0:T(8,128)(2,1)S(1)}, bf16[2,2,256,256]{3,2,1,0:T(8,128)(2,1)}, u32[]{:S(2)}) copy-start(bf16[2,2,256,256]{3,2,1,0:T(8,128)(2,1)} %get-tuple-element.14) | copy-start | bytes 1572868
  147.8 42.7 %copy-start.4 = (bf16[2,2,256,256]{3,2,1,0:T(8,128)(2,1)S(1)}, bf16[2,2,256,256]{3,2,1,0:T(8,128)(2,1)}, u32[]{:S(2)}) copy-start(bf16[2,2,256,256]{3,2,1,0:T(8,128)(2,1)} %get-tuple-element.15) | copy-start | bytes 1572868
  147.8 42.8 %copy-start.5 = (bf16[2,2,256,256]{3,2,1,0:T(8,128)(2,1)S(1)}, bf16[2,2,256,256]{3,2,1,0:T(8,128)(2,1)}, u32[]{:S(2)}) copy-start(bf16[2,2,256,256]{3,2,1,0:T(8,128)(2,1)} %get-tuple-element.16) | copy-start | bytes 1572868
  188.5 2.1 %copy-start.6 = (bf16[2,2,256,256]{3,2,1,0:T(8,128)(2,1)S(1)}, bf16[2,2,256,256]{3,2,1,0:T(8,128)(2,1)}, u32[]{:S(2)}) copy-start(bf16[2,2,256,256]{3,2,1,0:T(8,128)(2,1)} %get-tuple-element.17) | copy-start | bytes 1572868

commit v19 on v15

--- a/solution.py
+++ b/solution.py
@@ -371,15 +371,15 @@
         return copy_to(x_ref.at[j], rs_buf.at[me_op], send_rs.at[d], recv_rs.at[me_op], op_peer(j))
 
     pl.semaphore_wait(barrier, greeted)
+    operators = copy_to(piece_ref, got_ref, send_w.at[send_w.shape[0] - 1],
+                        recv_w.at[recv_w.shape[0] - 1], (next_sec, me_op))
+    operators.start()
     for d in range(1, n_op):
         rs_copy(d).start()
     a_args = (n_op, me_op, t_out, op_buf, send_a, recv_a, op_peer)
     start_gather(*a_args)
     rs_buf[me_op] = x_ref[me_op]
 
-    operators = copy_to(piece_ref, got_ref, send_w.at[send_w.shape[0] - 1],
-                        recv_w.at[recv_w.shape[0] - 1], (next_sec, me_op))
-    operators.start()
 
     wait_gather(*a_args)
     mid[...] = ordered_sum(op_buf, n_op)

time: 194 us -> 194 us (level)
  no operation moved by 1% of the time
where the time goes in v19:
time: 194 us
  Pallas kernels  172 us (89%)
  starting transfers between devices  8.77 us (5%)
  local copies, waits for them, and re-layouts  7.25 us (4%)
  matrix products  3.23 us (2%)
    pallas_call x4, Pallas kernels, step(): pl.pallas_call(functools.partial(step_kernel, n_sec, n_op, count, final),...  152 us
    pallas_call x4, Pallas kernels, sigma_part(): pl.pallas_call(sigma_part_kernel, out_shape=jax.ShapeDtypeStruct((sectors...  20 us
    ppermute x1, starting transfers between devices, padded(): lax.ppermute(head, axis, [((i + 1) % count, i) for i in range(count)])  6.22 us
  transfers between devices with their start and end apart: 3, of which 1 were waited for; matrix products, arithmetic and copies ran while one was open for 2% of the time, Pallas kernels for 0%

profile of v19, /device:TPU:1, one launch (start us, length us, event | category | flops | bytes accessed | tf_op | source)
XLA Modules:
  0.0 193.7 jit_solution(4001601669179892418)
XLA Ops:
  0.7 2.5 %collective-permute-start = (bf16[2,256,256]{2,1,0:T(8,128)(2,1)}, bf16[2,256,256]{2,1,0:T(8,128)(2,1)S(1)}, u32[]{:S(2)}, u32[]{:S(2)}) collective-permute-start(bf16[2,256,256]{2,1,0:T(8,128)(2,1)} %param.6), channel_id=1, source_target_pairs={{0,8},{8,16},{16,24},{24,32},{32,40},{40,48},{48,56},{56,64},{64,7... | collective-permute-start | bytes 786440 | tf_op jit(solution)/shard_map/ppermute | solution.py:25
  3.2 6.2 %collective-permute-start.1 = (bf16[2,256,256]{2,1,0:T(8,128)(2,1)}, bf16[2,256,256]{2,1,0:T(8,128)(2,1)S(1)}, u32[]{:S(2)}, u32[]{:S(2)}) collective-permute-start(bf16[2,256,256]{2,1,0:T(8,128)(2,1)} %param.6), channel_id=1, source_target_pairs={{8,0},{16,8},{24,16},{32,24},{40,32},{48,40},{56,48},{64,56},{72,6... | collective-permute-start | bytes 786440 | tf_op jit(solution)/shard_map/ppermute | solution.py:27
  9.4 0.0 collective-permute-start.2
  9.4 2.9 %fusion.19 = (bf16[2,2,256,256]{3,2,1,0:T(8,128)(2,1)}, bf16[2,2,256,256]{3,2,1,0:T(8,128)(2,1)}, bf16[2,2,256,256]{3,2,1,0:T(8,128)(2,1)}, bf16[2,2,256,256]{3,2,1,0:T(8,128)(2,1)}) fusion(bf16[8,2,256,256]{3,2,1,0:T(8,128)(2,1)} %left_ref.7), kind=kLoop, calls=%fused_computation.19 | loop fusion | bytes 4194304 | tf_op jit(solution)/shard_map/slice | solution.py:579
  12.3 0.1 broadcast_in_dim.4
  12.4 0.7 broadcast_in_dim_reshape.3.sh_ref
  13.1 0.7 copy.14.partner_ref
  13.8 1.9 collective-permute-done.2
  15.6 0.1 compare_convert_fusion
  15.7 0.0 collective-permute-done
  15.8 0.0 collective-permute-done.1
  15.8 0.0 copy-start
  15.8 0.9 copy-done
  16.7 5.0 %shard_map.77 = f32[2,256,256]{2,1,0:T(8,128)} custom-call(s32[8,2]{1,0:T(8,128)} %copy.14.partner_ref, bf16[6,256,256]{2,1,0:T(8,128)(2,1)} %copy-done, bf16[8,2,256,256]{3,2,1,0:T(8,128)(2,1)} %left_ref.7, bf16[8,2,256,256]{3,2,1,0:T(8,128)(2,1)} %right_ref.7), custom_call_target="tpu_custom_call" | custom-call | flops 1073741824 | bytes 5505024 | tf_op jit(solution)/shard_map/pallas_call | solution.py:535
  21.7 38.7 %shard_map.78 = (bf16[24,64,256]{2,1,0:T(8,128)(2,1)}, bf16[2,2,256,256]{3,2,1,0:T(8,128)(2,1)}) custom-call(f32[8,64,256]{2,1,0:T(8,128)} %bitcast.31, bf16[24,64,256]{2,1,0:T(8,128)(2,1)} %bitcast.24, f32[8,1,1]{2,1,0:T(1,128)} %broadcast_in_dim_reshape.3.sh_ref, bf16[2,2,256,256]{3,2,1,0:T(8,128)(2,1)} %get-tuple-element.21.piece_ref), custom_call_target="tpu_custom_call" | custom-call | tf_op jit(solution)/shard_map/pallas_call | solution.py:505
  60.4 5.0 %shard_map.79 = f32[2,256,256]{2,1,0:T(8,128)} custom-call(s32[8,2]{1,0:T(8,128)} %copy.14.partner_ref, bf16[6,256,256]{2,1,0:T(8,128)(2,1)} %bitcast.26, bf16[8,2,256,256]{3,2,1,0:T(8,128)(2,1)} %left_ref.7, bf16[8,2,256,256]{3,2,1,0:T(8,128)(2,1)} %right_ref.7), custom_call_target="tpu_custom_call" | custom-call | flops 1073741824 | bytes 5505024 | tf_op jit(solution)/shard_map/pallas_call | solution.py:535
  65.4 36.7 %shard_map.80 = (bf16[24,64,256]{2,1,0:T(8,128)(2,1)}, bf16[2,2,256,256]{3,2,1,0:T(8,128)(2,1)}) custom-call(f32[8,64,256]{2,1,0:T(8,128)} %bitcast.32, bf16[24,64,256]{2,1,0:T(8,128)(2,1)} %get-tuple-element.10.st_ref, f32[8,1,1]{2,1,0:T(1,128)} %broadcast_in_dim_reshape.3.sh_ref, bf16[2,2,256,256]{3,2,1,0:T(8,128)(2,1)} %get-tuple-element.20.piece_ref), custom_call_target="tpu_custom_call" | custom-call | tf_op jit(solution)/shard_map/pallas_call | solution.py:505
  102.1 5.0 %shard_map.81 = f32[2,256,256]{2,1,0:T(8,128)} custom-call(s32[8,2]{1,0:T(8,128)} %copy.14.partner_ref, bf16[6,256,256]{2,1,0:T(8,128)(2,1)} %bitcast.27, bf16[8,2,256,256]{3,2,1,0:T(8,128)(2,1)} %left_ref.7, bf16[8,2,256,256]{3,2,1,0:T(8,128)(2,1)} %right_ref.7), custom_call_target="tpu_custom_call" | custom-call | flops 1073741824 | bytes 5505024 | tf_op jit(solution)/shard_map/pallas_call | solution.py:535
  107.1 35.6 %shard_map.82 = (bf16[24,64,256]{2,1,0:T(8,128)(2,1)}, bf16[2,2,256,256]{3,2,1,0:T(8,128)(2,1)}) custom-call(f32[8,64,256]{2,1,0:T(8,128)} %bitcast.33, bf16[24,64,256]{2,1,0:T(8,128)(2,1)} %get-tuple-element.11.st_ref, f32[8,1,1]{2,1,0:T(1,128)} %broadcast_in_dim_reshape.3.sh_ref, bf16[2,2,256,256]{3,2,1,0:T(8,128)(2,1)} %get-tuple-element.19.piece_ref), custom_call_target="tpu_custom_call" | custom-call | tf_op jit(solution)/shard_map/pallas_call | solution.py:505
  142.7 5.0 %shard_map.83 = f32[2,256,256]{2,1,0:T(8,128)} custom-call(s32[8,2]{1,0:T(8,128)} %copy.14.partner_ref, bf16[6,256,256]{2,1,0:T(8,128)(2,1)} %bitcast.25, bf16[8,2,256,256]{3,2,1,0:T(8,128)(2,1)} %left_ref.7, bf16[8,2,256,256]{3,2,1,0:T(8,128)(2,1)} %right_ref.7), custom_call_target="tpu_custom_call" | custom-call | flops 1073741824 | bytes 5505024 | tf_op jit(solution)/shard_map/pallas_call | solution.py:535
  147.8 40.6 %shard_map.84 = (bf16[16,64,256]{2,1,0:T(8,128)(2,1)}, bf16[2,2,256,256]{3,2,1,0:T(8,128)(2,1)}) custom-call(f32[8,64,256]{2,1,0:T(8,128)} %bitcast.30, bf16[24,64,256]{2,1,0:T(8,128)(2,1)} %get-tuple-element.12.st_ref, f32[8,1,1]{2,1,0:T(1,128)} %broadcast_in_dim_reshape.3.sh_ref, bf16[2,2,256,256]{3,2,1,0:T(8,128)(2,1)} %get-tuple-element.18.piece_ref), custom_call_target="tpu_custom_call" | custom-call | tf_op jit(solution)/shard_map/pallas_call | solution.py:505
  188.4 1.8 fusion.20
  190.3 0.1 copy.16
  190.5 3.2 %multiply_convert_fusion = bf16[8,2,256,256]{3,2,1,0:T(8,128)(2,1)} fusion(bf16[2,2,256,256]{3,2,1,0:T(8,128)(2,1)S(1)} %copy-done.6, bf16[2,2,256,256]{3,2,1,0:T(8,128)(2,1)S(1)} %copy-done.5, bf16[2,2,256,256]{3,2,1,0:T(8,128)(2,1)S(1)} %copy-done.4, bf16[2,2,256,256]{3,2,1,0:T(8,128)(2,1)S(1)} %copy-done.3, bf16[2,256,256]{2,1,0:T(8,128)(2,1)S(1)} %copy.16, ...), kind=kOutput, calls=%fused_computation | convolution fusion | flops 1085276160 | bytes 4718592 | tf_op jit(solution)/shard_map/tbij,tbjk->tbik/dot_general | solution.py:596
  (19 shorter events, 0.1 us)
Async XLA Ops:
  0.6 15.1 %copy-start.1 = (bf16[2,256,256]{2,1,0:T(8,128)(2,1)S(1)}, bf16[2,256,256]{2,1,0:T(8,128)(2,1)}, u32[]{:S(2)}) copy-start(bf16[2,256,256]{2,1,0:T(8,128)(2,1)} %param.6) | copy-start | bytes 786436
  0.6 11.7 %copy-start.7 = (f32[2]{0:T(128)S(1)}, f32[2]{0:T(128)}, u32[]{:S(2)}) copy-start(f32[2]{0:T(128)} %param.9) | copy-start | bytes 28
  0.7 12.4 %copy-start.2 = (s32[8,2]{0,1:T(2,128)S(1)}, s32[8,2]{0,1:T(2,128)}, u32[]{:S(2)}) copy-start(s32[8,2]{0,1:T(2,128)} %param.10) | copy-start | bytes 196
  0.7 15.0 %collective-permute-start = (bf16[2,256,256]{2,1,0:T(8,128)(2,1)}, bf16[2,256,256]{2,1,0:T(8,128)(2,1)S(1)}, u32[]{:S(2)}, u32[]{:S(2)}) collective-permute-start(bf16[2,256,256]{2,1,0:T(8,128)(2,1)} %param.6), channel_id=1, source_target_pairs={{0,8},{8,16},{16,24},{24,32},{32,40},{40,48},{48,56},{56,64},{64,7... | collective-permute-start | bytes 786440 | tf_op jit(solution)/shard_map/ppermute | solution.py:25
  3.2 12.6 %collective-permute-start.1 = (bf16[2,256,256]{2,1,0:T(8,128)(2,1)}, bf16[2,256,256]{2,1,0:T(8,128)(2,1)S(1)}, u32[]{:S(2)}, u32[]{:S(2)}) collective-permute-start(bf16[2,256,256]{2,1,0:T(8,128)(2,1)} %param.6), channel_id=1, source_target_pairs={{8,0},{16,8},{24,16},{32,24},{40,32},{48,40},{56,48},{64,56},{72,6... | collective-permute-start | bytes 786440 | tf_op jit(solution)/shard_map/ppermute | solution.py:27
  9.4 6.2 %collective-permute-start.2 = (s32[2]{0:T(128)}, s32[2]{0:T(128)S(1)}, u32[]{:S(2)}, u32[]{:S(2)}) collective-permute-start(s32[2]{0:T(128)} %param.11), channel_id=1, source_target_pairs={{248,0},{0,8},{8,16},{16,24},{24,32},{32,40},{40,48},{48,56},{56,6... | collective-permute-start | bytes 32 | tf_op jit(solution)/shard_map/ppermute | solution.py:559
  15.8 0.9 copy-start
  147.7 42.7 %copy-start.3 = (bf16[2,2,256,256]{3,2,1,0:T(8,128)(2,1)S(1)}, bf16[2,2,256,256]{3,2,1,0:T(8,128)(2,1)}, u32[]{:S(2)}) copy-start(bf16[2,2,256,256]{3,2,1,0:T(8,128)(2,1)} %get-tuple-element.14) | copy-start | bytes 1572868
  147.8 42.7 %copy-start.4 = (bf16[2,2,256,256]{3,2,1,0:T(8,128)(2,1)S(1)}, bf16[2,2,256,256]{3,2,1,0:T(8,128)(2,1)}, u32[]{:S(2)}) copy-start(bf16[2,2,256,256]{3,2,1,0:T(8,128)(2,1)} %get-tuple-element.15) | copy-start | bytes 1572868
  147.8 42.7 %copy-start.5 = (bf16[2,2,256,256]{3,2,1,0:T(8,128)(2,1)S(1)}, bf16[2,2,256,256]{3,2,1,0:T(8,128)(2,1)}, u32[]{:S(2)}) copy-start(bf16[2,2,256,256]{3,2,1,0:T(8,128)(2,1)} %get-tuple-element.16) | copy-start | bytes 1572868
  188.4 2.1 %copy-start.6 = (bf16[2,2,256,256]{3,2,1,0:T(8,128)(2,1)S(1)}, bf16[2,2,256,256]{3,2,1,0:T(8,128)(2,1)}, u32[]{:S(2)}) copy-start(bf16[2,2,256,256]{3,2,1,0:T(8,128)(2,1)} %get-tuple-element.17) | copy-start | bytes 1572868
